TPU v7x, 32 devices: a whole 2x2x4 slice. The times are simulated.
32 devices in a mesh: groups: 2 (over x), slab: 16 (over z, y, core).
Axes of the slice: x: 2, y: 2, z: 4, core: 2. Of those that a mesh axis runs over, the one named last changes fastest.
Arguments:
- recorded: float32 [3, 256, 256, 128], P(None, 'slab', 'groups'), parts along dimension 2, may hold values from 0.02 to 14, as said below
- initial: float32 [256, 256, 128], P('slab', 'groups'), parts along dimension 1, may hold values from 0.5 to 2
- kernel_x: float32 [3, 64], replicated, may hold values from 0.01 to 1.05, as said below
- kernel_y: float32 [3, 64], replicated, may hold values from 0.01 to 1.05, as said below
- kernel_z: float32 [3, 32], replicated, may hold values from 0.01 to 1.05, as said below
Outputs:
- deconvolved: float32 [256, 256, 128], P('slab', 'groups'), parts along dimension 1
There are 2 independent parts, one for each index of `groups`. A program takes and returns all parts, laid end to end along the dimension named above; an argument that names none is the same for every part. Nothing has to cross between parts.
Inputs may be any that keep to these rules, and one draw needn't show every extreme that they name: `recorded`: positive intensities. `kernel_x`: positive taps. `kernel_y`: positive taps. `kernel_z`: positive taps.
All inputs are finite; a program needn't handle non-finite values.
Results may differ from a plain program's by a relative error of at most 0.0001.
Values sent between devices are 32-bit elements; how exact they have to be, the bound alone decides.
No kernel may reach another device: no remote copies, remote signals or barrier semaphores. Data moves between devices by JAX's collectives and lax.ppermute only.
A program may use at most 128 MiB of HBM per device.

v0:
```python
import functools

import jax
import jax.numpy as jnp
from jax import lax
from jax.experimental import pallas as pl
from jax.experimental.pallas import tpu as pltpu
from jax.sharding import PartitionSpec as P

ITERS = 2
CHUNKS = 2
GROUP = 8
LANES = 128
F32 = jnp.float32
BF16 = jnp.bfloat16
PRECISE = lax.Precision.HIGHEST


def split(value):
    high = value.astype(BF16)
    low = (value - high.astype(F32)).astype(BF16)
    return high, low


def dot(left, right):
    return jnp.dot(left, right, preferred_element_type=F32)


def normalize(kernel):
    return kernel / jnp.sum(kernel, axis=1, keepdims=True)


def lateral_kernel(taps_x, taps_y, fwd_x, bwd_x, fwd_y, bwd_y, sums_x, sums_y, *, tap_count):
    view_count = taps_x.shape[0]
    size = fwd_x.shape[1]
    rows = lax.broadcasted_iota(jnp.int32, (size, size), 0)
    cols = lax.broadcasted_iota(jnp.int32, (size, size), 1)
    tap_ids = cols - rows + tap_count // 2
    inside = (tap_ids >= 0) & (tap_ids < tap_count)
    for taps, is_x in ((taps_x, True), (taps_y, False)):
        values = taps[...]
        values = values / jnp.sum(values, axis=1, keepdims=True)
        for view in range(view_count):
            line = jnp.broadcast_to(values[view : view + 1, :], (size, size))
            matrix = pltpu.roll(line, size - tap_count // 2, 1, stride=1, stride_axis=0)
            matrix = jnp.where(inside, matrix, 0.0)
            high, low = split(matrix)
            high_t, low_t = split(matrix.T)
            total = jnp.sum(matrix, axis=0, keepdims=True)
            if is_x:
                fwd_x[view] = jnp.concatenate([high, high, low], axis=1)
                bwd_x[view] = jnp.concatenate([high_t, high_t, low_t], axis=1)
                sums_x[view : view + 1, :] = total
            else:
                one = jnp.concatenate([high_t, low_t], axis=1)
                fwd_y[view] = jnp.concatenate([one, one], axis=0)
                one = jnp.concatenate([high, low], axis=1)
                bwd_y[view] = jnp.concatenate([one, one], axis=0)
                sums_y[view : view + 1, :] = total


def lateral_matrices(kernel_x, kernel_y, size_x, size_y):
    view_count, tap_count = kernel_x.shape
    assert size_x == size_y == LANES and tap_count <= size_x
    pads = ((0, 0), (0, size_x - tap_count))
    out = lambda *shape: jax.ShapeDtypeStruct(shape, BF16)
    return pl.pallas_call(
        functools.partial(lateral_kernel, tap_count=tap_count),
        out_shape=(
            out(view_count, size_x, 3 * size_x),
            out(view_count, size_x, 3 * size_x),
            out(view_count, 2 * size_y, 2 * size_y),
            out(view_count, 2 * size_y, 2 * size_y),
            jax.ShapeDtypeStruct((view_count, size_x), F32),
            jax.ShapeDtypeStruct((view_count, size_y), F32),
        ),
        name="lateral_matrices",
    )(jnp.pad(kernel_x, pads), jnp.pad(kernel_y, pads))


def axial_matrices(taps, block_len, odd):
    view_count, tap_count = taps.shape
    reach = tap_count // 2
    base = jnp.arange(block_len)
    near = jnp.where(odd, -block_len, block_len)
    source = jnp.concatenate([base, base + near, base - near])
    tap_ids = source[None, :] - base[:, None] + reach
    pick = (tap_ids[:, :, None] == jnp.arange(tap_count)).astype(F32)
    bands = jnp.einsum("zsk,vk->vzs", pick, taps, precision=PRECISE)
    return bands.reshape(view_count * block_len, -1)


def stacked(matrix):
    high = lax.reduce_precision(matrix, 8, 7)
    low = matrix - high
    return jnp.concatenate([high, high, low], axis=1).astype(BF16)


def totals_kernel(recorded, initial, sums_x, sums_y, weights_z, out, *, block_len):
    view_count = sums_x.shape[0]
    lanes = lax.broadcasted_iota(jnp.int32, out.shape, 1)
    view_of = (lanes % (view_count * block_len)) // block_len
    row_of = lax.broadcasted_iota(jnp.int32, out.shape, 0)
    along_x = sums_x[...]
    weighted = jnp.zeros(sums_y.shape, F32)
    for z in range(block_len):
        part = jnp.dot(along_x, initial[z], precision=PRECISE, preferred_element_type=F32)
        weighted = weighted + part * weights_z[:, z : z + 1]
    weighted = weighted * sums_y[...]
    result = jnp.zeros(out.shape, F32)
    for view in range(view_count):

        def add(z, total):
            return total + jnp.sum(recorded[view * block_len + z].reshape(-1, 8, LANES), axis=0)

        data = lax.fori_loop(0, block_len, add, jnp.zeros((8, LANES), F32), unroll=4)
        blur_total = jnp.sum(weighted[view : view + 1, :])
        data_total = jnp.sum(data)
        value = jnp.where(row_of == 0, data_total, blur_total)
        result = jnp.where(view_of == view, value, result)
    out[...] = result


def totals(recorded, initial, sums_x, sums_y, taps, axis):
    block_len = initial.shape[0]
    view_count, tap_count = taps.shape
    count = lax.axis_size(axis)
    plane = lax.axis_index(axis) * block_len + jnp.arange(block_len)
    target = plane[:, None] + tap_count // 2 - jnp.arange(tap_count)[None, :]
    inside = ((target >= 0) & (target < count * block_len)).astype(F32)
    weights = jnp.sum(taps[:, None, :] * inside[None], axis=2)
    mine = pl.pallas_call(
        functools.partial(totals_kernel, block_len=block_len),
        out_shape=jax.ShapeDtypeStruct((8, 2 * LANES), F32),
        name="totals",
    )(recorded, initial, sums_x, sums_y, weights)
    copies = jnp.broadcast_to(mine[None], (count,) + mine.shape)
    return lax.all_to_all(copies, axis, 0, 0)


def forward_kernel(own, near, far, axial, lateral, out, *, block_len):
    chunk = own.shape[0]
    view_count = lateral.shape[0]
    axial_matrix = axial[...]

    def step(index, carry):
        start = index * GROUP
        window = jnp.concatenate(
            [ref[pl.ds(start, GROUP)] for ref in (own, near, far)], axis=1
        )
        high, low = split(window)
        terms = jnp.concatenate([high, low, high], axis=1)
        blurred = []
        for pair in range(0, GROUP, 2):
            blurred.append(dot(axial_matrix, jnp.concatenate([terms[pair], terms[pair + 1]], axis=1)))
        for view in range(view_count):
            rows = slice(view * block_len, (view + 1) * block_len)
            field = jnp.concatenate(
                [part[rows, side : side + LANES] for part in blurred for side in (0, LANES)], axis=0
            )
            result = dot(jnp.concatenate(split(field), axis=1), lateral[view])
            result = result[:, :LANES] + result[:, LANES:]
            for i in range(GROUP):
                first = view * block_len * chunk + start + i
                out[pl.ds(first, block_len, stride=chunk), :] = result[
                    i * block_len : (i + 1) * block_len
                ]
        return carry

    lax.fori_loop(0, chunk // GROUP, step, 0)


def forward_part(own, near, far, axial, lateral):
    chunk, block_len, size_y = own.shape
    view_count = lateral.shape[0]
    return pl.pallas_call(
        functools.partial(forward_kernel, block_len=block_len),
        out_shape=jax.ShapeDtypeStruct((view_count * block_len * chunk, size_y), F32),
        name="forward_part",
    )(own, near, far, axial, lateral)


def quotient_kernel(*refs, chunks, block_len):
    parts, (recorded, fwd, bwd, out) = refs[:chunks], refs[chunks:]
    view_count = fwd.shape[0]
    chunk = parts[0].shape[0] // (view_count * block_len)
    planes = view_count * block_len
    size_x = chunk * chunks
    for view in range(view_count):

        def step(index, carry):
            plane = view * block_len + 2 * index
            field = jnp.concatenate(
                [
                    jnp.concatenate([ref[pl.ds((plane + side) * chunk, chunk), :] for ref in parts], axis=0)
                    for side in (0, 1)
                ],
                axis=1,
            )
            high, low = split(field)
            blurred = dot(fwd[view], jnp.concatenate([high, low, high], axis=0))
            data = jnp.concatenate([recorded[plane], recorded[plane + 1]], axis=1)
            high, low = split(data / blurred)
            back = dot(bwd[view], jnp.concatenate([high, low, high], axis=0))
            out[pl.ds(plane, size_x, stride=planes), :] = back[:, :LANES]
            out[pl.ds(plane + 1, size_x, stride=planes), :] = back[:, LANES:]
            return carry

        lax.fori_loop(0, block_len // 2, step, 0, unroll=2)


def quotient_part(parts, recorded, fwd, bwd):
    planes, size_x, size_y = recorded.shape
    view_count = fwd.shape[0]
    return pl.pallas_call(
        functools.partial(quotient_kernel, chunks=len(parts), block_len=planes // view_count),
        out_shape=jax.ShapeDtypeStruct((size_x * planes, size_y), F32),
        name="quotient_part",
    )(*parts, recorded, fwd, bwd)


def backward_kernel(field, axial, sums, lateral, own, near, far, *, block_len, offset):
    chunk = own.shape[0]
    view_count = lateral.shape[0]
    planes = view_count * block_len
    total = jnp.sum(sums[...], axis=0)
    gains = (total[1:2, :] / total[0:1, :])[:, : axial.shape[1]]
    scaled = axial[...] * gains
    high, low = split(scaled)
    lanes = lax.broadcasted_iota(jnp.int32, scaled.shape, 1)
    axial_matrix = jnp.where(lanes < 2 * planes, high.astype(F32), low.astype(F32)).astype(BF16)

    def step(index, carry):
        start = index * GROUP
        rows = field[pl.ds((offset + start) * planes, GROUP * planes), :].reshape(GROUP, planes, LANES)
        results = []
        for view in range(view_count):
            part = rows[:, view * block_len : (view + 1) * block_len, :].reshape(GROUP * block_len, LANES)
            result = dot(jnp.concatenate(split(part), axis=1), lateral[view])
            results.append((result[:, :LANES] + result[:, LANES:]).reshape(GROUP, block_len, LANES))
        high, low = split(jnp.concatenate(results, axis=1))
        terms = jnp.concatenate([high, low, high], axis=1)
        for pair in range(0, GROUP, 2):
            sent = dot(axial_matrix, jnp.concatenate([terms[pair], terms[pair + 1]], axis=1))
            for side in (0, 1):
                lanes_of = slice(side * LANES, (side + 1) * LANES)
                for place, ref in enumerate((own, near, far)):
                    ref[start + pair + side] = sent[place * block_len : (place + 1) * block_len, lanes_of]
        return carry

    lax.fori_loop(0, chunk // GROUP, step, 0)


def backward_part(field, axial, sums, lateral, block_len, chunk, offset):
    size_y = field.shape[1]
    shape = jax.ShapeDtypeStruct((chunk, block_len, size_y), F32)
    return pl.pallas_call(
        functools.partial(backward_kernel, block_len=block_len, offset=offset),
        out_shape=(shape, shape, shape),
        name="backward_part",
    )(field, axial, sums, lateral)


def body(recorded, initial, kernel_x, kernel_y, kernel_z):
    view_count, block_len, size_x, size_y = recorded.shape
    assert kernel_z.shape[1] // 2 <= block_len
    count = lax.axis_size("slab")
    chunk = size_x // CHUNKS
    odd = lax.axis_index("slab") % 2 == 1
    near_pairs = [p for i in range(0, count - 1, 2) for p in ((i, i + 1), (i + 1, i))]
    far_pairs = [p for i in range(1, count - 1, 2) for p in ((i, i + 1), (i + 1, i))]

    def exchange(far_value, near_value):
        return lax.ppermute(far_value, "slab", far_pairs), lax.ppermute(near_value, "slab", near_pairs)

    turned = jnp.transpose(initial, (1, 0, 2))
    estimate = [turned[i * chunk : (i + 1) * chunk] for i in range(CHUNKS)]
    planes = recorded.reshape(view_count * block_len, size_x, size_y)
    fwd_x, bwd_x, fwd_y, bwd_y, sums_x, sums_y = lateral_matrices(kernel_x, kernel_y, size_x, size_y)
    taps_z = normalize(kernel_z)
    bands = axial_matrices(taps_z, block_len, odd)
    axial_fwd = stacked(bands)
    axial_bwd = jnp.concatenate([bands.T] * 3, axis=1)
    sums = totals(planes, initial, sums_x, sums_y, taps_z, "slab")
    for _ in range(ITERS):
        halos = [exchange(part, part) for part in estimate]
        parts = [
            forward_part(part, near, far, axial_fwd, fwd_y)
            for part, (far, near) in zip(estimate, halos)
        ]
        field = quotient_part(parts, planes, fwd_x, bwd_x)
        sent = [
            backward_part(field, axial_bwd, sums, bwd_y, block_len, chunk, i * chunk)
            for i in range(CHUNKS)
        ]
        halos = [exchange(far, near) for _, near, far in sent]
        estimate = [
            part * (own + near + far) / view_count
            for part, (own, _, _), (far, near) in zip(estimate, sent, halos)
        ]
    return jnp.transpose(jnp.concatenate(estimate, axis=0), (1, 0, 2))


def solution(mesh):
    in_specs = (P(None, "slab", "groups", None), P("slab", "groups", None), P(), P(), P())
    out_specs = P("slab", "groups", None)
    return jax.shard_map(body, mesh=mesh, in_specs=in_specs, out_specs=out_specs, check_vma=False)
```

profile of v0, /device:TPU:11, one launch (start us, length us, event | category | flops | bytes accessed | tf_op | source)
XLA Modules:
  0.0 169.6 jit_solution(16734111515990484521)
XLA Ops:
  0.0 1.8 %copy.22 = f32[16,128,128]{2,0,1:T(8,128)S(1)} copy(f32[16,128,128]{2,1,0:T(8,128)} %initial.1) | data formatting | bytes 2097152 | tf_op args[1]
  2.0 0.7 collective-permute-start.2
  2.7 3.0 %collective-permute-start.3 = (f32[64,16,128]{2,1,0:T(8,128)S(1)}, f32[64,16,128]{2,1,0:T(8,128)}, u32[]{:S(2)}, u32[]{:S(2)}) collective-permute-start(f32[64,16,128]{2,1,0:T(8,128)S(1)} %get-tuple-element.43.own), channel_id=1, source_target_pairs={{1,2},{2,1},{3,4},{4,3},{5,6},{6,5},{7,8},{8,7},{9,10},{10,9},{11,... | collective-permute-start | bytes 1572872 | tf_op jit(solution)/shard_map/ppermute | solution.py:274
  5.8 0.4 collective-permute-start
  6.2 3.2 %collective-permute-start.1 = (f32[64,16,128]{2,1,0:T(8,128)S(1)}, f32[64,16,128]{2,1,0:T(8,128)}, u32[]{:S(2)}, u32[]{:S(2)}) collective-permute-start(f32[64,16,128]{2,1,0:T(8,128)S(1)} %get-tuple-element.44.own), channel_id=1, source_target_pairs={{1,2},{2,1},{3,4},{4,3},{5,6},{6,5},{7,8},{8,7},{9,10},{10,9},{11,... | collective-permute-start | bytes 1572872 | tf_op jit(solution)/shard_map/ppermute | solution.py:274
  9.6 0.6 pad.7.taps_x
  10.2 0.6 pad.8.taps_y
  10.8 2.1 %lateral_matrices.1 = (bf16[3,128,384]{2,1,0:T(8,128)(2,1)}, bf16[3,128,384]{2,1,0:T(8,128)(2,1)}, bf16[3,256,256]{2,1,0:T(8,128)(2,1)}, bf16[3,256,256]{2,1,0:T...) custom-call(f32[3,128]{1,0:T(4,128)} %pad.7.taps_x, f32[3,128]{1,0:T(4,128)} %pad.8.taps_y), custom_call_target="tpu_custom_call" | custom-call | tf_op jit(solution)/shard_map/lateral_matrices/pallas_call | solution.py:67
  13.0 0.7 multiply_reduce_fusion.weights_z
  13.6 4.4 %totals.1 = f32[8,256]{1,0:T(8,128)} custom-call(f32[48,128,128]{2,1,0:T(8,128)} %bitcast.13, f32[16,128,128]{2,1,0:T(8,128)} %initial.1, f32[3,128]{1,0:T(4,128)} %get-tuple-element.26.sums_x, f32[3,128]{1,0:T(4,128)} %get-tuple-element.27.sums_y, f32[3,16]{1,0:T(4,128)} %multiply_reduce_fusion.weights_z), custom_call_target="tpu_custom_call" | custom-call | tf_op jit(solution)/shard_map/totals/pallas_call | solution.py:132
  18.0 1.4 broadcast_in_dim.2
  19.4 5.3 %all-to-all-start = ((f32[16,8,256]{2,1,0:T(8,128)}), f32[16,8,256]{2,1,0:T(8,128)S(1)}, u32[]{:S(2)}, u32[]{:S(2)}) async-start(f32[16,8,256]{2,1,0:T(8,128)} %broadcast_in_dim.2), calls=%async_computation | async-start | bytes 262144 | tf_op jit(solution)/shard_map/all_to_all | solution.py:138
  24.7 0.2 fusion
  25.0 0.7 pad_maximum_fusion.1.axial
  25.7 0.7 pad_maximum_fusion.axial
  26.5 0.8 copy-done.8
  27.3 5.9 %forward_part.5.refs_1_ = f32[3072,128]{1,0:T(8,128)} custom-call(f32[64,16,128]{2,1,0:T(8,128)} %copy-done.6, f32[64,16,128]{2,1,0:T(8,128)} %copy-done.8, f32[64,16,128]{2,1,0:T(8,128)} %collective-permute-done.3.far, bf16[48,144]{1,0:T(8,128)(2,1)} %pad_maximum_fusion.1.axial, bf16[3,256,256]{2,1,0:T(8,128)(2,1)} %get-tuple-element.23.lateral), custom_call_target="tpu_custom_call" | custom-call | tf_op jit(solution)/shard_map/forward_part/pallas_call | solution.py:176
  33.2 0.8 copy-done.7
  34.0 6.0 %forward_part.4.refs_0_ = f32[3072,128]{1,0:T(8,128)} custom-call(f32[64,16,128]{2,1,0:T(8,128)} %copy-done.5, f32[64,16,128]{2,1,0:T(8,128)} %copy-done.7, f32[64,16,128]{2,1,0:T(8,128)} %collective-permute-done.1.far, bf16[48,144]{1,0:T(8,128)(2,1)} %pad_maximum_fusion.1.axial, bf16[3,256,256]{2,1,0:T(8,128)(2,1)} %get-tuple-element.23.lateral), custom_call_target="tpu_custom_call" | custom-call | tf_op jit(solution)/shard_map/forward_part/pallas_call | solution.py:176
  40.0 10.7 %quotient_part.2.field = f32[6144,128]{1,0:T(8,128)} custom-call(f32[3072,128]{1,0:T(8,128)} %forward_part.4.refs_0_, f32[3072,128]{1,0:T(8,128)} %forward_part.5.refs_1_, f32[48,128,128]{2,1,0:T(8,128)} %bitcast.14, bf16[3,128,384]{2,1,0:T(8,128)(2,1)} %get-tuple-element.24.refs_3_, bf16[3,128,384]{2,1,0:T(8,128)(2,1)} %get-tuple-element.25.refs_4_), custom_call_target="tpu_custom_call" | custom-call | tf_op jit(solution)/shard_map/quotient_part/pallas_call | solution.py:215
  50.7 0.6 copy-done.4
  51.4 6.3 %backward_part.5 = (f32[64,16,128]{2,1,0:T(8,128)}, f32[64,16,128]{2,1,0:T(8,128)}, f32[64,16,128]{2,1,0:T(8,128)}) custom-call(f32[6144,128]{1,0:T(8,128)} %quotient_part.2.field, f32[48,144]{1,0:T(8,128)} %pad_maximum_fusion.axial, f32[16,8,256]{2,1,0:T(8,128)} %copy-done.4, bf16[3,256,256]{2,1,0:T(8,128)(2,1)} %get-tuple-element.28.lateral), custom_call_target="tpu_custom_call" | custom-call | tf_op jit(solution)/shard_map/backward_part/pallas_call | solution.py:257
  57.6 0.4 collective-permute-start.8
  58.0 3.2 %collective-permute-start.9 = (f32[64,16,128]{2,1,0:T(8,128)}, f32[64,16,128]{2,1,0:T(8,128)S(1)}, u32[]{:S(2)}, u32[]{:S(2)}) collective-permute-start(f32[64,16,128]{2,1,0:T(8,128)} %get-tuple-element.34), channel_id=1, source_target_pairs={{1,2},{2,1},{3,4},{4,3},{5,6},{6,5},{7,8},{8,7},{9,10},{10,9},{11,... | collective-permute-start | bytes 1572872 | tf_op jit(solution)/shard_map/ppermute | solution.py:274
  61.3 6.3 %backward_part.4 = (f32[64,16,128]{2,1,0:T(8,128)}, f32[64,16,128]{2,1,0:T(8,128)}, f32[64,16,128]{2,1,0:T(8,128)}) custom-call(f32[6144,128]{1,0:T(8,128)} %quotient_part.2.field, f32[48,144]{1,0:T(8,128)} %pad_maximum_fusion.axial, f32[16,8,256]{2,1,0:T(8,128)} %copy-done.4, bf16[3,256,256]{2,1,0:T(8,128)(2,1)} %get-tuple-element.28.lateral), custom_call_target="tpu_custom_call" | custom-call | tf_op jit(solution)/shard_map/backward_part/pallas_call | solution.py:257
  67.5 0.4 collective-permute-start.4
  67.9 3.1 %collective-permute-start.5 = (f32[64,16,128]{2,1,0:T(8,128)}, f32[64,16,128]{2,1,0:T(8,128)S(1)}, u32[]{:S(2)}, u32[]{:S(2)}) collective-permute-start(f32[64,16,128]{2,1,0:T(8,128)} %get-tuple-element.31), channel_id=1, source_target_pairs={{1,2},{2,1},{3,4},{4,3},{5,6},{6,5},{7,8},{8,7},{9,10},{10,9},{11,... | collective-permute-start | bytes 1572872 | tf_op jit(solution)/shard_map/ppermute | solution.py:274
  71.0 9.1 %collective-permute-done.9 = f32[64,16,128]{2,1,0:T(8,128)S(1)} collective-permute-done((f32[64,16,128]{2,1,0:T(8,128)}, f32[64,16,128]{2,1,0:T(8,128)S(1)}, u32[]{:S(2)}, u32[]{:S(2)}) %collective-permute-start.9) | collective-permute-done | bytes 524320 | tf_op jit(solution)/shard_map/ppermute | solution.py:274
  80.1 5.6 %collective-permute-done.5 = f32[64,16,128]{2,1,0:T(8,128)S(1)} collective-permute-done((f32[64,16,128]{2,1,0:T(8,128)}, f32[64,16,128]{2,1,0:T(8,128)S(1)}, u32[]{:S(2)}, u32[]{:S(2)}) %collective-permute-start.5) | collective-permute-done | bytes 524320 | tf_op jit(solution)/shard_map/ppermute | solution.py:274
  85.7 1.5 multiply_multiply_fusion.3
  87.4 3.1 %collective-permute-start.11 = (f32[64,16,128]{2,1,0:T(8,128)S(1)}, f32[64,16,128]{2,1,0:T(8,128)S(1)}, u32[]{:S(2)}, u32[]{:S(2)}) collective-permute-start(f32[64,16,128]{2,1,0:T(8,128)S(1)} %get-tuple-element.42.own), channel_id=1, source_target_pairs={{1,2},{2,1},{3,4},{4,3},{5,6},{6,5},{7,8},{8,7},{9,10},{10,9},{11,... | collective-permute-start | bytes 1572872 | tf_op jit(solution)/shard_map/ppermute | solution.py:274
  90.5 0.5 collective-permute-start.6
  91.0 3.4 %collective-permute-start.7 = (f32[64,16,128]{2,1,0:T(8,128)S(1)}, f32[64,16,128]{2,1,0:T(8,128)S(1)}, u32[]{:S(2)}, u32[]{:S(2)}) collective-permute-start(f32[64,16,128]{2,1,0:T(8,128)S(1)} %get-tuple-element.41.own), channel_id=1, source_target_pairs={{1,2},{2,1},{3,4},{4,3},{5,6},{6,5},{7,8},{8,7},{9,10},{10,9},{11,... | collective-permute-start | bytes 1572872 | tf_op jit(solution)/shard_map/ppermute | solution.py:274
  94.4 14.7 %collective-permute-done.11.far = f32[64,16,128]{2,1,0:T(8,128)S(1)} collective-permute-done((f32[64,16,128]{2,1,0:T(8,128)S(1)}, f32[64,16,128]{2,1,0:T(8,128)S(1)}, u32[]{:S(2)}, u32[]{:S(2)}) %collective-permute-start.11) | collective-permute-done | bytes 524320 | tf_op jit(solution)/shard_map/ppermute | solution.py:274
  109.1 0.8 copy-done.16
  109.9 5.9 %forward_part.7.refs_1_ = f32[3072,128]{1,0:T(8,128)} custom-call(f32[64,16,128]{2,1,0:T(8,128)} %copy-done, f32[64,16,128]{2,1,0:T(8,128)} %copy-done.14, f32[64,16,128]{2,1,0:T(8,128)} %copy-done.16, bf16[48,144]{1,0:T(8,128)(2,1)} %pad_maximum_fusion.1.axial, bf16[3,256,256]{2,1,0:T(8,128)(2,1)} %get-tuple-element.23.lateral), custom_call_target="tpu_custom_call" | custom-call | tf_op jit(solution)/shard_map/forward_part/pallas_call | solution.py:176
  115.8 0.8 copy-done.13
  116.6 0.8 copy-done.15
  117.4 6.0 %forward_part.6.refs_0_ = f32[3072,128]{1,0:T(8,128)} custom-call(f32[64,16,128]{2,1,0:T(8,128)} %copy-done.2, f32[64,16,128]{2,1,0:T(8,128)} %copy-done.13, f32[64,16,128]{2,1,0:T(8,128)} %copy-done.15, bf16[48,144]{1,0:T(8,128)(2,1)} %pad_maximum_fusion.1.axial, bf16[3,256,256]{2,1,0:T(8,128)(2,1)} %get-tuple-element.23.lateral), custom_call_target="tpu_custom_call" | custom-call | tf_op jit(solution)/shard_map/forward_part/pallas_call | solution.py:176
  123.4 10.7 %quotient_part.3.field = f32[6144,128]{1,0:T(8,128)} custom-call(f32[3072,128]{1,0:T(8,128)} %forward_part.6.refs_0_, f32[3072,128]{1,0:T(8,128)} %forward_part.7.refs_1_, f32[48,128,128]{2,1,0:T(8,128)} %bitcast.15, bf16[3,128,384]{2,1,0:T(8,128)(2,1)} %get-tuple-element.24.refs_3_, bf16[3,128,384]{2,1,0:T(8,128)(2,1)} %get-tuple-element.25.refs_4_), custom_call_target="tpu_custom_call" | custom-call | tf_op jit(solution)/shard_map/quotient_part/pallas_call | solution.py:215
  134.1 6.3 %backward_part.6 = (f32[64,16,128]{2,1,0:T(8,128)}, f32[64,16,128]{2,1,0:T(8,128)}, f32[64,16,128]{2,1,0:T(8,128)}) custom-call(f32[6144,128]{1,0:T(8,128)} %quotient_part.3.field, f32[48,144]{1,0:T(8,128)} %pad_maximum_fusion.axial, f32[16,8,256]{2,1,0:T(8,128)} %copy-done.4, bf16[3,256,256]{2,1,0:T(8,128)(2,1)} %get-tuple-element.28.lateral), custom_call_target="tpu_custom_call" | custom-call | tf_op jit(solution)/shard_map/backward_part/pallas_call | solution.py:257
  140.4 3.2 %collective-permute-start.13 = (f32[64,16,128]{2,1,0:T(8,128)}, f32[64,16,128]{2,1,0:T(8,128)S(1)}, u32[]{:S(2)}, u32[]{:S(2)}) collective-permute-start(f32[64,16,128]{2,1,0:T(8,128)} %get-tuple-element.37), channel_id=1, source_target_pairs={{1,2},{2,1},{3,4},{4,3},{5,6},{6,5},{7,8},{8,7},{9,10},{10,9},{11,... | collective-permute-start | bytes 1572872 | tf_op jit(solution)/shard_map/ppermute | solution.py:274
  143.7 6.2 %backward_part.7 = (f32[64,16,128]{2,1,0:T(8,128)}, f32[64,16,128]{2,1,0:T(8,128)}, f32[64,16,128]{2,1,0:T(8,128)}) custom-call(f32[6144,128]{1,0:T(8,128)} %quotient_part.3.field, f32[48,144]{1,0:T(8,128)} %pad_maximum_fusion.axial, f32[16,8,256]{2,1,0:T(8,128)} %copy-done.4, bf16[3,256,256]{2,1,0:T(8,128)(2,1)} %get-tuple-element.28.lateral), custom_call_target="tpu_custom_call" | custom-call | tf_op jit(solution)/shard_map/backward_part/pallas_call | solution.py:257
  149.9 0.5 collective-permute-start.14
  150.4 3.4 %collective-permute-start.15 = (f32[64,16,128]{2,1,0:T(8,128)}, f32[64,16,128]{2,1,0:T(8,128)S(1)}, u32[]{:S(2)}, u32[]{:S(2)}) collective-permute-start(f32[64,16,128]{2,1,0:T(8,128)} %get-tuple-element.40), channel_id=1, source_target_pairs={{1,2},{2,1},{3,4},{4,3},{5,6},{6,5},{7,8},{8,7},{9,10},{10,9},{11,... | collective-permute-start | bytes 1572872 | tf_op jit(solution)/shard_map/ppermute | solution.py:274
  153.8 8.7 %collective-permute-done.13 = f32[64,16,128]{2,1,0:T(8,128)S(1)} collective-permute-done((f32[64,16,128]{2,1,0:T(8,128)}, f32[64,16,128]{2,1,0:T(8,128)S(1)}, u32[]{:S(2)}, u32[]{:S(2)}) %collective-permute-start.13) | collective-permute-done | bytes 524320 | tf_op jit(solution)/shard_map/ppermute | solution.py:274
  162.7 5.5 %collective-permute-done.15 = f32[64,16,128]{2,1,0:T(8,128)S(1)} collective-permute-done((f32[64,16,128]{2,1,0:T(8,128)}, f32[64,16,128]{2,1,0:T(8,128)S(1)}, u32[]{:S(2)}, u32[]{:S(2)}) %collective-permute-start.15) | collective-permute-done | bytes 524320 | tf_op jit(solution)/shard_map/ppermute | solution.py:274
  168.4 1.3 copy.20
  (63 shorter events, 1.0 us)
Async XLA Ops:
  1.8 7.5 %copy-start.17 = (f32[3,32]{1,0:T(4,128)S(1)}, f32[3,32]{1,0:T(4,128)}, u32[]{:S(2)}) copy-start(f32[3,32]{1,0:T(4,128)} %param.9) | copy-start | bytes 1156
  1.9 7.7 %copy-start.18 = (f32[3,64]{1,0:T(4,128)S(1)}, f32[3,64]{1,0:T(4,128)}, u32[]{:S(2)}) copy-start(f32[3,64]{1,0:T(4,128)} %param.7) | copy-start | bytes 2308
  1.9 8.3 %copy-start.19 = (f32[3,64]{1,0:T(4,128)S(1)}, f32[3,64]{1,0:T(4,128)}, u32[]{:S(2)}) copy-start(f32[3,64]{1,0:T(4,128)} %param.8) | copy-start | bytes 2308
  2.0 16.1 %copy-start.5 = (f32[64,16,128]{2,1,0:T(8,128)}, f32[64,16,128]{2,1,0:T(8,128)S(1)}, u32[]{:S(2)}) copy-start(f32[64,16,128]{2,1,0:T(8,128)S(1)} %get-tuple-element.44.own) | copy-start | bytes 1572868
  2.0 16.1 %copy-start.6 = (f32[64,16,128]{2,1,0:T(8,128)}, f32[64,16,128]{2,1,0:T(8,128)S(1)}, u32[]{:S(2)}) copy-start(f32[64,16,128]{2,1,0:T(8,128)S(1)} %get-tuple-element.43.own) | copy-start | bytes 1572868
  2.0 24.5 %collective-permute-start.2 = (f32[64,16,128]{2,1,0:T(8,128)S(1)}, f32[64,16,128]{2,1,0:T(8,128)S(1)}, u32[]{:S(2)}, u32[]{:S(2)}) collective-permute-start(f32[64,16,128]{2,1,0:T(8,128)S(1)} %get-tuple-element.43.own), channel_id=1, source_target_pairs={{0,1},{1,0},{2,3},{3,2},{4,5},{5,4},{6,7},{7,6},{8,9},{9,8},{10,11... | collective-permute-start | bytes 1572872 | tf_op jit(solution)/shard_map/ppermute | solution.py:274
  2.7 23.8 %collective-permute-start.3 = (f32[64,16,128]{2,1,0:T(8,128)S(1)}, f32[64,16,128]{2,1,0:T(8,128)}, u32[]{:S(2)}, u32[]{:S(2)}) collective-permute-start(f32[64,16,128]{2,1,0:T(8,128)S(1)} %get-tuple-element.43.own), channel_id=1, source_target_pairs={{1,2},{2,1},{3,4},{4,3},{5,6},{6,5},{7,8},{8,7},{9,10},{10,9},{11,... | collective-permute-start | bytes 1572872 | tf_op jit(solution)/shard_map/ppermute | solution.py:274
  5.8 27.4 %collective-permute-start = (f32[64,16,128]{2,1,0:T(8,128)S(1)}, f32[64,16,128]{2,1,0:T(8,128)S(1)}, u32[]{:S(2)}, u32[]{:S(2)}) collective-permute-start(f32[64,16,128]{2,1,0:T(8,128)S(1)} %get-tuple-element.44.own), channel_id=1, source_target_pairs={{0,1},{1,0},{2,3},{3,2},{4,5},{5,4},{6,7},{7,6},{8,9},{9,8},{10,11... | collective-permute-start | bytes 1572872 | tf_op jit(solution)/shard_map/ppermute | solution.py:274
  6.2 27.0 %collective-permute-start.1 = (f32[64,16,128]{2,1,0:T(8,128)S(1)}, f32[64,16,128]{2,1,0:T(8,128)}, u32[]{:S(2)}, u32[]{:S(2)}) collective-permute-start(f32[64,16,128]{2,1,0:T(8,128)S(1)} %get-tuple-element.44.own), channel_id=1, source_target_pairs={{1,2},{2,1},{3,4},{4,3},{5,6},{6,5},{7,8},{8,7},{9,10},{10,9},{11,... | collective-permute-start | bytes 1572872 | tf_op jit(solution)/shard_map/ppermute | solution.py:274
  19.4 31.3 %all-to-all-start = ((f32[16,8,256]{2,1,0:T(8,128)}), f32[16,8,256]{2,1,0:T(8,128)S(1)}, u32[]{:S(2)}, u32[]{:S(2)}) async-start(f32[16,8,256]{2,1,0:T(8,128)} %broadcast_in_dim.2), calls=%async_computation | async-start | bytes 262144 | tf_op jit(solution)/shard_map/all_to_all | solution.py:138
  26.5 0.8 copy-start.8
  33.2 0.8 copy-start.7
  50.7 0.6 copy-start.4
  57.6 13.4 %collective-permute-start.8 = (f32[64,16,128]{2,1,0:T(8,128)}, f32[64,16,128]{2,1,0:T(8,128)S(1)}, u32[]{:S(2)}, u32[]{:S(2)}) collective-permute-start(f32[64,16,128]{2,1,0:T(8,128)} %get-tuple-element.33), channel_id=1, source_target_pairs={{0,1},{1,0},{2,3},{3,2},{4,5},{5,4},{6,7},{7,6},{8,9},{9,8},{10,11... | collective-permute-start | bytes 1572872 | tf_op jit(solution)/shard_map/ppermute | solution.py:274
  58.0 27.7 %copy-start.9 = (f32[64,16,128]{2,1,0:T(8,128)S(1)}, f32[64,16,128]{2,1,0:T(8,128)}, u32[]{:S(2)}) copy-start(f32[64,16,128]{2,1,0:T(8,128)} %get-tuple-element.32) | copy-start | bytes 1572868
  58.0 22.1 %collective-permute-start.9 = (f32[64,16,128]{2,1,0:T(8,128)}, f32[64,16,128]{2,1,0:T(8,128)S(1)}, u32[]{:S(2)}, u32[]{:S(2)}) collective-permute-start(f32[64,16,128]{2,1,0:T(8,128)} %get-tuple-element.34), channel_id=1, source_target_pairs={{1,2},{2,1},{3,4},{4,3},{5,6},{6,5},{7,8},{8,7},{9,10},{10,9},{11,... | collective-permute-start | bytes 1572872 | tf_op jit(solution)/shard_map/ppermute | solution.py:274
  67.5 12.6 %collective-permute-start.4 = (f32[64,16,128]{2,1,0:T(8,128)}, f32[64,16,128]{2,1,0:T(8,128)S(1)}, u32[]{:S(2)}, u32[]{:S(2)}) collective-permute-start(f32[64,16,128]{2,1,0:T(8,128)} %get-tuple-element.30), channel_id=1, source_target_pairs={{0,1},{1,0},{2,3},{3,2},{4,5},{5,4},{6,7},{7,6},{8,9},{9,8},{10,11... | collective-permute-start | bytes 1572872 | tf_op jit(solution)/shard_map/ppermute | solution.py:274
  67.9 17.8 %collective-permute-start.5 = (f32[64,16,128]{2,1,0:T(8,128)}, f32[64,16,128]{2,1,0:T(8,128)S(1)}, u32[]{:S(2)}, u32[]{:S(2)}) collective-permute-start(f32[64,16,128]{2,1,0:T(8,128)} %get-tuple-element.31), channel_id=1, source_target_pairs={{1,2},{2,1},{3,4},{4,3},{5,6},{6,5},{7,8},{8,7},{9,10},{10,9},{11,... | collective-permute-start | bytes 1572872 | tf_op jit(solution)/shard_map/ppermute | solution.py:274
  80.1 5.6 %copy-start.10 = (f32[64,16,128]{2,1,0:T(8,128)}, f32[64,16,128]{2,1,0:T(8,128)S(1)}, u32[]{:S(2)}) copy-start(f32[64,16,128]{2,1,0:T(8,128)S(1)} %collective-permute-done.9) | copy-start | bytes 1572868
  87.3 21.8 %copy-start = (f32[64,16,128]{2,1,0:T(8,128)}, f32[64,16,128]{2,1,0:T(8,128)S(1)}, u32[]{:S(2)}) copy-start(f32[64,16,128]{2,1,0:T(8,128)S(1)} %get-tuple-element.42.own) | copy-start | bytes 1572868
  87.3 28.5 %copy-start.2 = (f32[64,16,128]{2,1,0:T(8,128)}, f32[64,16,128]{2,1,0:T(8,128)S(1)}, u32[]{:S(2)}) copy-start(f32[64,16,128]{2,1,0:T(8,128)S(1)} %get-tuple-element.41.own) | copy-start | bytes 1572868
  87.3 7.1 %collective-permute-start.10 = (f32[64,16,128]{2,1,0:T(8,128)S(1)}, f32[64,16,128]{2,1,0:T(8,128)S(1)}, u32[]{:S(2)}, u32[]{:S(2)}) collective-permute-start(f32[64,16,128]{2,1,0:T(8,128)S(1)} %get-tuple-element.42.own), channel_id=1, source_target_pairs={{0,1},{1,0},{2,3},{3,2},{4,5},{5,4},{6,7},{7,6},{8,9},{9,8},{10,11... | collective-permute-start | bytes 1572872 | tf_op jit(solution)/shard_map/ppermute | solution.py:274
  87.4 21.7 %collective-permute-start.11 = (f32[64,16,128]{2,1,0:T(8,128)S(1)}, f32[64,16,128]{2,1,0:T(8,128)S(1)}, u32[]{:S(2)}, u32[]{:S(2)}) collective-permute-start(f32[64,16,128]{2,1,0:T(8,128)S(1)} %get-tuple-element.42.own), channel_id=1, source_target_pairs={{1,2},{2,1},{3,4},{4,3},{5,6},{6,5},{7,8},{8,7},{9,10},{10,9},{11,... | collective-permute-start | bytes 1572872 | tf_op jit(solution)/shard_map/ppermute | solution.py:274
  90.5 25.3 %collective-permute-start.6 = (f32[64,16,128]{2,1,0:T(8,128)S(1)}, f32[64,16,128]{2,1,0:T(8,128)S(1)}, u32[]{:S(2)}, u32[]{:S(2)}) collective-permute-start(f32[64,16,128]{2,1,0:T(8,128)S(1)} %get-tuple-element.41.own), channel_id=1, source_target_pairs={{0,1},{1,0},{2,3},{3,2},{4,5},{5,4},{6,7},{7,6},{8,9},{9,8},{10,11... | collective-permute-start | bytes 1572872 | tf_op jit(solution)/shard_map/ppermute | solution.py:274
  91.0 24.8 %collective-permute-start.7 = (f32[64,16,128]{2,1,0:T(8,128)S(1)}, f32[64,16,128]{2,1,0:T(8,128)S(1)}, u32[]{:S(2)}, u32[]{:S(2)}) collective-permute-start(f32[64,16,128]{2,1,0:T(8,128)S(1)} %get-tuple-element.41.own), channel_id=1, source_target_pairs={{1,2},{2,1},{3,4},{4,3},{5,6},{6,5},{7,8},{8,7},{9,10},{10,9},{11,... | collective-permute-start | bytes 1572872 | tf_op jit(solution)/shard_map/ppermute | solution.py:274
  94.4 14.7 %copy-start.14 = (f32[64,16,128]{2,1,0:T(8,128)}, f32[64,16,128]{2,1,0:T(8,128)S(1)}, u32[]{:S(2)}) copy-start(f32[64,16,128]{2,1,0:T(8,128)S(1)} %collective-permute-done.10.near) | copy-start | bytes 1572868
  109.1 0.8 copy-start.16
  115.8 0.8 copy-start.13
  116.6 0.8 copy-start.15
  140.4 13.4 %collective-permute-start.12 = (f32[64,16,128]{2,1,0:T(8,128)}, f32[64,16,128]{2,1,0:T(8,128)S(1)}, u32[]{:S(2)}, u32[]{:S(2)}) collective-permute-start(f32[64,16,128]{2,1,0:T(8,128)} %get-tuple-element.36), channel_id=1, source_target_pairs={{0,1},{1,0},{2,3},{3,2},{4,5},{5,4},{6,7},{7,6},{8,9},{9,8},{10,11... | collective-permute-start | bytes 1572872 | tf_op jit(solution)/shard_map/ppermute | solution.py:274
  140.4 22.1 %copy-start.3 = (f32[64,16,128]{2,1,0:T(8,128)S(1)}, f32[64,16,128]{2,1,0:T(8,128)}, u32[]{:S(2)}) copy-start(f32[64,16,128]{2,1,0:T(8,128)} %copy-done.2) | copy-start | bytes 1572868
  140.4 22.1 %copy-start.12 = (f32[64,16,128]{2,1,0:T(8,128)S(1)}, f32[64,16,128]{2,1,0:T(8,128)}, u32[]{:S(2)}) copy-start(f32[64,16,128]{2,1,0:T(8,128)} %get-tuple-element.35) | copy-start | bytes 1572868
  140.4 22.1 %collective-permute-start.13 = (f32[64,16,128]{2,1,0:T(8,128)}, f32[64,16,128]{2,1,0:T(8,128)S(1)}, u32[]{:S(2)}, u32[]{:S(2)}) collective-permute-start(f32[64,16,128]{2,1,0:T(8,128)} %get-tuple-element.37), channel_id=1, source_target_pairs={{1,2},{2,1},{3,4},{4,3},{5,6},{6,5},{7,8},{8,7},{9,10},{10,9},{11,... | collective-permute-start | bytes 1572872 | tf_op jit(solution)/shard_map/ppermute | solution.py:274
  149.9 18.2 %copy-start.1 = (f32[64,16,128]{2,1,0:T(8,128)S(1)}, f32[64,16,128]{2,1,0:T(8,128)}, u32[]{:S(2)}) copy-start(f32[64,16,128]{2,1,0:T(8,128)} %copy-done) | copy-start | bytes 1572868
  149.9 18.2 %copy-start.11 = (f32[64,16,128]{2,1,0:T(8,128)S(1)}, f32[64,16,128]{2,1,0:T(8,128)}, u32[]{:S(2)}) copy-start(f32[64,16,128]{2,1,0:T(8,128)} %get-tuple-element.38) | copy-start | bytes 1572868
  149.9 12.7 %collective-permute-start.14 = (f32[64,16,128]{2,1,0:T(8,128)}, f32[64,16,128]{2,1,0:T(8,128)S(1)}, u32[]{:S(2)}, u32[]{:S(2)}) collective-permute-start(f32[64,16,128]{2,1,0:T(8,128)} %get-tuple-element.39), channel_id=1, source_target_pairs={{0,1},{1,0},{2,3},{3,2},{4,5},{5,4},{6,7},{7,6},{8,9},{9,8},{10,11... | collective-permute-start | bytes 1572872 | tf_op jit(solution)/shard_map/ppermute | solution.py:274
  150.4 17.7 %collective-permute-start.15 = (f32[64,16,128]{2,1,0:T(8,128)}, f32[64,16,128]{2,1,0:T(8,128)S(1)}, u32[]{:S(2)}, u32[]{:S(2)}) collective-permute-start(f32[64,16,128]{2,1,0:T(8,128)} %get-tuple-element.40), channel_id=1, source_target_pairs={{1,2},{2,1},{3,4},{4,3},{5,6},{6,5},{7,8},{8,7},{9,10},{10,9},{11,... | collective-permute-start | bytes 1572872 | tf_op jit(solution)/shard_map/ppermute | solution.py:274
where the time goes:
time: 170 us
  Pallas kernels  76.8 us (45%)
  waiting for transfers between devices  43.6 us (26%)
  starting transfers between devices  33.9 us (20%)
  local copies, waits for them, and re-layouts  10.5 us (6%)
  other arithmetic  4.34 us (3%)
    ppermute x8, waiting for transfers between devices, exchange(): lax.ppermute(far_value, 'slab', far_pairs)  43.6 us
    ppermute x8, starting transfers between devices, exchange(): lax.ppermute(far_value, 'slab', far_pairs)  25.6 us
    pallas_call x4, Pallas kernels, backward_part(): pl.pallas_call(functools.partial(backward_kernel, block_len=block_len, of...  25.1 us
    pallas_call x4, Pallas kernels, forward_part(): pl.pallas_call(functools.partial(forward_kernel, block_len=block_len), ou...  23.8 us
    pallas_call x2, Pallas kernels, quotient_part(): pl.pallas_call(functools.partial(quotient_kernel, chunks=len(parts), bloc...  21.4 us
    unnamed x41, local copies, waits for them, and re-layouts  6.54 us
    all_to_all x1, starting transfers between devices, totals(): return lax.all_to_all(copies, axis, 0, 0)  5.26 us
    pallas_call x1, Pallas kernels, totals(): pl.pallas_call(functools.partial(totals_kernel, block_len=block_len), out...  4.38 us
  transfers between devices with their start and end apart: 17, of which 5 were waited for; matrix products, arithmetic and copies ran while one was open for 3% of the time, Pallas kernels for 28%

commit v1 on v0

--- a/solution.py
+++ b/solution.py
@@ -10,6 +10,11 @@
 ITERS = 2
 CHUNKS = 2
 GROUP = 8
+VMEM_LIMIT = 16 << 20
+ROWS = 16
+FORWARD_Z = 2
+BACKWARD_Z = 2
+QUOTIENT = 2
 LANES = 128
 F32 = jnp.float32
 BF16 = jnp.bfloat16
@@ -138,36 +143,47 @@
     return lax.all_to_all(copies, axis, 0, 0)
 
 
-def forward_kernel(own, near, far, axial, lateral, out, *, block_len):
+def in_vmem(*values):
+    return [pltpu.with_memory_space_constraint(value, pltpu.VMEM) for value in values]
+
+
+def forward_kernel(own, near, far, axial, lateral, out, fields, *, block_len):
     chunk = own.shape[0]
     view_count = lateral.shape[0]
     axial_matrix = axial[...]
-
-    def step(index, carry):
+    spread = chunk + 1
+
+    def along_z(index, carry):
         start = index * GROUP
-        window = jnp.concatenate(
-            [ref[pl.ds(start, GROUP)] for ref in (own, near, far)], axis=1
-        )
+        window = jnp.concatenate([ref[pl.ds(start, GROUP)] for ref in (own, near, far)], axis=1)
         high, low = split(window)
         terms = jnp.concatenate([high, low, high], axis=1)
-        blurred = []
         for pair in range(0, GROUP, 2):
-            blurred.append(dot(axial_matrix, jnp.concatenate([terms[pair], terms[pair + 1]], axis=1)))
+            result = dot(axial_matrix, jnp.concatenate([terms[pair], terms[pair + 1]], axis=1))
+            for side in (0, 1):
+                row = (start + pair + side) * block_len
+                high, low = split(result[:, side * LANES : (side + 1) * LANES])
+                for view in range(view_count):
+                    part = slice(view * block_len, (view + 1) * block_len)
+                    fields[view, pl.ds(row, block_len), :LANES] = high[part]
+                    fields[view, pl.ds(row, block_len), LANES:] = low[part]
+        return carry
+
+    lax.fori_loop(0, chunk // GROUP, along_z, 0, unroll=FORWARD_Z)
+
+    def along_y(index, carry):
+        start = index * ROWS
         for view in range(view_count):
-            rows = slice(view * block_len, (view + 1) * block_len)
-            field = jnp.concatenate(
-                [part[rows, side : side + LANES] for part in blurred for side in (0, LANES)], axis=0
-            )
-            result = dot(jnp.concatenate(split(field), axis=1), lateral[view])
+            result = dot(fields[view, pl.ds(start * block_len, ROWS * block_len), :], lateral[view])
             result = result[:, :LANES] + result[:, LANES:]
-            for i in range(GROUP):
-                first = view * block_len * chunk + start + i
-                out[pl.ds(first, block_len, stride=chunk), :] = result[
+            for i in range(ROWS):
+                first = view * block_len * spread + start + i
+                out[pl.ds(first, block_len, stride=spread), :] = result[
                     i * block_len : (i + 1) * block_len
                 ]
         return carry
 
-    lax.fori_loop(0, chunk // GROUP, step, 0)
+    lax.fori_loop(0, chunk // ROWS, along_y, 0)
 
 
 def forward_part(own, near, far, axial, lateral):
@@ -175,24 +191,30 @@
     view_count = lateral.shape[0]
     return pl.pallas_call(
         functools.partial(forward_kernel, block_len=block_len),
-        out_shape=jax.ShapeDtypeStruct((view_count * block_len * chunk, size_y), F32),
+        out_shape=pltpu.VMEM((view_count * block_len * (chunk + 1), size_y), F32),
+        scratch_shapes=[pltpu.VMEM((view_count, chunk * block_len, 2 * size_y), BF16)],
+        compiler_params=pltpu.CompilerParams(vmem_limit_bytes=VMEM_LIMIT),
         name="forward_part",
-    )(own, near, far, axial, lateral)
+    )(*in_vmem(own, near, far, axial, lateral))
 
 
 def quotient_kernel(*refs, chunks, block_len):
     parts, (recorded, fwd, bwd, out) = refs[:chunks], refs[chunks:]
     view_count = fwd.shape[0]
-    chunk = parts[0].shape[0] // (view_count * block_len)
     planes = view_count * block_len
-    size_x = chunk * chunks
+    size_x = fwd.shape[1]
+    chunk = size_x // chunks
+    spread = planes + 1
+
     for view in range(view_count):
 
         def step(index, carry):
             plane = view * block_len + 2 * index
             field = jnp.concatenate(
                 [
-                    jnp.concatenate([ref[pl.ds((plane + side) * chunk, chunk), :] for ref in parts], axis=0)
+                    jnp.concatenate(
+                        [ref[pl.ds((plane + side) * (chunk + 1), chunk), :] for ref in parts], axis=0
+                    )
                     for side in (0, 1)
                 ],
                 axis=1,
@@ -202,11 +224,11 @@
             data = jnp.concatenate([recorded[plane], recorded[plane + 1]], axis=1)
             high, low = split(data / blurred)
             back = dot(bwd[view], jnp.concatenate([high, low, high], axis=0))
-            out[pl.ds(plane, size_x, stride=planes), :] = back[:, :LANES]
-            out[pl.ds(plane + 1, size_x, stride=planes), :] = back[:, LANES:]
+            out[pl.ds(plane, size_x, stride=spread), :] = back[:, :LANES]
+            out[pl.ds(plane + 1, size_x, stride=spread), :] = back[:, LANES:]
             return carry
 
-        lax.fori_loop(0, block_len // 2, step, 0, unroll=2)
+        lax.fori_loop(0, block_len // 2, step, 0, unroll=QUOTIENT)
 
 
 def quotient_part(parts, recorded, fwd, bwd):
@@ -214,15 +236,17 @@
     view_count = fwd.shape[0]
     return pl.pallas_call(
         functools.partial(quotient_kernel, chunks=len(parts), block_len=planes // view_count),
-        out_shape=jax.ShapeDtypeStruct((size_x * planes, size_y), F32),
+        out_shape=pltpu.VMEM((size_x * (planes + 1), size_y), F32),
+        compiler_params=pltpu.CompilerParams(vmem_limit_bytes=VMEM_LIMIT),
         name="quotient_part",
-    )(*parts, recorded, fwd, bwd)
-
-
-def backward_kernel(field, axial, sums, lateral, own, near, far, *, block_len, offset):
+    )(*in_vmem(*parts, recorded, fwd, bwd))
+
+
+def backward_kernel(field, axial, sums, lateral, own, near, far, terms, *, block_len, offset):
     chunk = own.shape[0]
     view_count = lateral.shape[0]
     planes = view_count * block_len
+    spread = planes + 1
     total = jnp.sum(sums[...], axis=0)
     gains = (total[1:2, :] / total[0:1, :])[:, : axial.shape[1]]
     scaled = axial[...] * gains
@@ -230,35 +254,52 @@
     lanes = lax.broadcasted_iota(jnp.int32, scaled.shape, 1)
     axial_matrix = jnp.where(lanes < 2 * planes, high.astype(F32), low.astype(F32)).astype(BF16)
 
-    def step(index, carry):
+    def along_y(index, carry):
+        start = index * ROWS
+        for view in range(view_count):
+            rows = jnp.concatenate(
+                [
+                    field[pl.ds((offset + start + i) * spread + view * block_len, block_len), :]
+                    for i in range(ROWS)
+                ],
+                axis=0,
+            )
+            result = dot(jnp.concatenate(split(rows), axis=1), lateral[view])
+            result = result[:, :LANES] + result[:, LANES:]
+            high, low = split(result.reshape(ROWS, block_len, LANES))
+            for place, part in enumerate((high, low, high)):
+                row = place * planes + view * block_len
+                terms[pl.ds(start, ROWS), row : row + block_len, :] = part
+        return carry
+
+    lax.fori_loop(0, chunk // ROWS, along_y, 0)
+
+    def along_z(index, carry):
         start = index * GROUP
-        rows = field[pl.ds((offset + start) * planes, GROUP * planes), :].reshape(GROUP, planes, LANES)
-        results = []
-        for view in range(view_count):
-            part = rows[:, view * block_len : (view + 1) * block_len, :].reshape(GROUP * block_len, LANES)
-            result = dot(jnp.concatenate(split(part), axis=1), lateral[view])
-            results.append((result[:, :LANES] + result[:, LANES:]).reshape(GROUP, block_len, LANES))
-        high, low = split(jnp.concatenate(results, axis=1))
-        terms = jnp.concatenate([high, low, high], axis=1)
         for pair in range(0, GROUP, 2):
-            sent = dot(axial_matrix, jnp.concatenate([terms[pair], terms[pair + 1]], axis=1))
+            sent = dot(
+                axial_matrix, jnp.concatenate([terms[start + pair], terms[start + pair + 1]], axis=1)
+            )
             for side in (0, 1):
                 lanes_of = slice(side * LANES, (side + 1) * LANES)
                 for place, ref in enumerate((own, near, far)):
                     ref[start + pair + side] = sent[place * block_len : (place + 1) * block_len, lanes_of]
         return carry
 
-    lax.fori_loop(0, chunk // GROUP, step, 0)
+    lax.fori_loop(0, chunk // GROUP, along_z, 0, unroll=BACKWARD_Z)
 
 
 def backward_part(field, axial, sums, lateral, block_len, chunk, offset):
     size_y = field.shape[1]
-    shape = jax.ShapeDtypeStruct((chunk, block_len, size_y), F32)
+    planes = lateral.shape[0] * block_len
+    shape = pltpu.VMEM((chunk, block_len, size_y), F32)
     return pl.pallas_call(
         functools.partial(backward_kernel, block_len=block_len, offset=offset),
         out_shape=(shape, shape, shape),
+        scratch_shapes=[pltpu.VMEM((chunk, 3 * planes, size_y), BF16)],
+        compiler_params=pltpu.CompilerParams(vmem_limit_bytes=VMEM_LIMIT),
         name="backward_part",
-    )(field, axial, sums, lateral)
+    )(*in_vmem(field, axial, sums, lateral))
 
 
 def body(recorded, initial, kernel_x, kernel_y, kernel_z):

time: 170 us -> 137 us (0.81)
  Pallas kernels: 76.8 us -> 35.8 us
  waiting for transfers between devices: 43.6 us -> 57.3 us
  local copies, waits for them, and re-layouts: 10.5 us -> 6.88 us
  other arithmetic: 4.34 us -> 1.85 us
    pallas_call x4, Pallas kernels: 25.1 us -> 8.16 us  [backward_part(): pl.pallas_call(functools.partial(backward_kernel, block_len=block_len, of...]
    pallas_call x4, Pallas kernels: 23.8 us -> 9.16 us  [forward_part(): pl.pallas_call(functools.partial(forward_kernel, block_len=block_len), ou...]
    ppermute x8, waiting for transfers between devices: 43.6 us -> 57.2 us  [exchange(): lax.ppermute(far_value, 'slab', far_pairs)]
    pallas_call x2, Pallas kernels: 21.4 us -> 11.9 us  [quotient_part(): pl.pallas_call(functools.partial(quotient_kernel, chunks=len(parts), bloc...]
    unnamed x41 -> x31, local copies, waits for them, and re-layouts: 6.54 us -> 2.93 us
  transfers between devices with their start and end apart: 17 -> 17, of which waited for: 5 -> 7; matrix products, arithmetic and copies ran while one was open for 3% -> 3% of each run, Pallas kernels for 28% -> 17%
where the time goes in v1:
time: 137 us
  waiting for transfers between devices  57.3 us (42%)
  Pallas kernels  35.8 us (26%)
  starting transfers between devices  34.3 us (25%)
  local copies, waits for them, and re-layouts  6.88 us (5%)
  other arithmetic  1.85 us (1%)
    ppermute x8, waiting for transfers between devices, exchange(): lax.ppermute(far_value, 'slab', far_pairs)  57.2 us
    ppermute x8, starting transfers between devices, exchange(): lax.ppermute(far_value, 'slab', far_pairs)  26.4 us
    pallas_call x2, Pallas kernels, quotient_part(): pl.pallas_call(functools.partial(quotient_kernel, chunks=len(parts), bloc...  11.9 us
    pallas_call x4, Pallas kernels, forward_part(): pl.pallas_call(functools.partial(forward_kernel, block_len=block_len), ou...  9.16 us
    pallas_call x4, Pallas kernels, backward_part(): pl.pallas_call(functools.partial(backward_kernel, block_len=block_len, of...  8.16 us
    all_to_all x1, starting transfers between devices, totals(): return lax.all_to_all(copies, axis, 0, 0)  5.26 us
    pallas_call x1, Pallas kernels, totals(): pl.pallas_call(functools.partial(totals_kernel, block_len=block_len), out...  4.42 us
    unnamed x31, local copies, waits for them, and re-layouts  2.93 us
  transfers between devices with their start and end apart: 17, of which 7 were waited for; matrix products, arithmetic and copies ran while one was open for 3% of the time, Pallas kernels for 17%

profile of v1, /device:TPU:11, one launch (start us, length us, event | category | flops | bytes accessed | tf_op | source)
XLA Modules:
  0.0 136.7 jit_solution(11300020832611369624)
XLA Ops:
  0.0 1.9 %copy.22 = f32[16,128,128]{2,0,1:T(8,128)S(1)} copy(f32[16,128,128]{2,1,0:T(8,128)} %initial.1) | data formatting | bytes 2097152 | tf_op args[1]
  2.0 0.7 collective-permute-start.2
  2.7 3.0 %collective-permute-start.3 = (f32[64,16,128]{2,1,0:T(8,128)S(1)}, f32[64,16,128]{2,1,0:T(8,128)}, u32[]{:S(2)}, u32[]{:S(2)}) collective-permute-start(f32[64,16,128]{2,1,0:T(8,128)S(1)} %get-tuple-element.43.own), channel_id=1, source_target_pairs={{1,2},{2,1},{3,4},{4,3},{5,6},{6,5},{7,8},{8,7},{9,10},{10,9},{11,... | collective-permute-start | bytes 1572872 | tf_op jit(solution)/shard_map/ppermute | solution.py:315
  5.8 0.4 collective-permute-start
  6.2 3.2 %collective-permute-start.1 = (f32[64,16,128]{2,1,0:T(8,128)S(1)}, f32[64,16,128]{2,1,0:T(8,128)S(1)}, u32[]{:S(2)}, u32[]{:S(2)}) collective-permute-start(f32[64,16,128]{2,1,0:T(8,128)S(1)} %get-tuple-element.44.own), channel_id=1, source_target_pairs={{1,2},{2,1},{3,4},{4,3},{5,6},{6,5},{7,8},{8,7},{9,10},{10,9},{11,... | collective-permute-start | bytes 1572872 | tf_op jit(solution)/shard_map/ppermute | solution.py:315
  9.4 0.1 reduce_sum.18
  9.6 0.6 pad.7.taps_x
  10.2 0.6 pad.8.taps_y
  10.8 2.1 %lateral_matrices.1 = (bf16[3,128,384]{2,1,0:T(8,128)(2,1)}, bf16[3,128,384]{2,1,0:T(8,128)(2,1)}, bf16[3,256,256]{2,1,0:T(8,128)(2,1)}, bf16[3,256,256]{2,1,0:T...) custom-call(f32[3,128]{1,0:T(4,128)} %pad.7.taps_x, f32[3,128]{1,0:T(4,128)} %pad.8.taps_y), custom_call_target="tpu_custom_call" | custom-call | tf_op jit(solution)/shard_map/lateral_matrices/pallas_call | solution.py:72
  12.9 0.6 multiply_reduce_fusion.weights_z
  13.5 4.4 %totals.1 = f32[8,256]{1,0:T(8,128)} custom-call(f32[48,128,128]{2,1,0:T(8,128)} %bitcast.13, f32[16,128,128]{2,1,0:T(8,128)} %initial.1, f32[3,128]{1,0:T(4,128)} %get-tuple-element.26.sums_x, f32[3,128]{1,0:T(4,128)} %get-tuple-element.27.sums_y, f32[3,16]{1,0:T(4,128)} %multiply_reduce_fusion.weights_z), custom_call_target="tpu_custom_call" | custom-call | tf_op jit(solution)/shard_map/totals/pallas_call | solution.py:137
  18.0 1.4 %broadcast_in_dim.2 = f32[16,8,256]{2,1,0:T(8,128)} broadcast(f32[8,256]{1,0:T(8,128)} %totals.1), dimensions={1,2} | broadcast | bytes 139264 | tf_op jit(solution)/shard_map/broadcast_in_dim | solution.py:142
  19.3 5.3 %all-to-all-start = ((f32[16,8,256]{2,1,0:T(8,128)}), f32[16,8,256]{2,1,0:T(8,128)S(1)}, u32[]{:S(2)}, u32[]{:S(2)}) async-start(f32[16,8,256]{2,1,0:T(8,128)} %broadcast_in_dim.2), calls=%async_computation | async-start | bytes 262144 | tf_op jit(solution)/shard_map/all_to_all | solution.py:143
  24.6 0.1 pad_add_fusion
  24.7 0.2 fusion
  25.0 0.1 pad_maximum_fusion.1.axial
  25.1 0.1 pad_maximum_fusion.axial
  25.2 3.1 %forward_part.5.refs_1_ = f32[3120,128]{1,0:T(8,128)S(1)} custom-call(f32[64,16,128]{2,1,0:T(8,128)S(1)} %get-tuple-element.43.own, f32[64,16,128]{2,1,0:T(8,128)S(1)} %collective-permute-done.2.near, f32[64,16,128]{2,1,0:T(8,128)} %collective-permute-done.3.far, bf16[48,144]{1,0:T(8,128)(2,1)S(1)} %pad_maximum_fusion.1.axial, bf16[3,256,256]{2,1,0:T(8,128)(2,1)S(1)} %copy-done.2), custom_call_target="tpu_custom_call" | custom-call | tf_op jit(solution)/shard_map/forward_part/pallas_call | solution.py:192
  28.4 2.9 %collective-permute-done.1.far = f32[64,16,128]{2,1,0:T(8,128)S(1)} collective-permute-done((f32[64,16,128]{2,1,0:T(8,128)S(1)}, f32[64,16,128]{2,1,0:T(8,128)S(1)}, u32[]{:S(2)}, u32[]{:S(2)}) %collective-permute-start.1) | collective-permute-done | bytes 524320 | tf_op jit(solution)/shard_map/ppermute | solution.py:315
  31.3 2.0 %forward_part.4.refs_0_ = f32[3120,128]{1,0:T(8,128)S(1)} custom-call(f32[64,16,128]{2,1,0:T(8,128)S(1)} %get-tuple-element.44.own, f32[64,16,128]{2,1,0:T(8,128)S(1)} %collective-permute-done.near, f32[64,16,128]{2,1,0:T(8,128)S(1)} %collective-permute-done.1.far, bf16[48,144]{1,0:T(8,128)(2,1)S(1)} %pad_maximum_fusion.1.axial, ...), custom_call_target="tpu_custom_call" | custom-call | tf_op jit(solution)/shard_map/forward_part/pallas_call | solution.py:192
  33.3 6.0 %quotient_part.2.field = f32[6272,128]{1,0:T(8,128)S(1)} custom-call(f32[3120,128]{1,0:T(8,128)S(1)} %forward_part.4.refs_0_, f32[3120,128]{1,0:T(8,128)S(1)} %forward_part.5.refs_1_, f32[48,128,128]{2,1,0:T(8,128)S(1)} %bitcast.14, bf16[3,128,384]{2,1,0:T(8,128)(2,1)S(1)} %copy-done.6, bf16[3,128,384]{2,1,0:T(8,128)(2,1)S(1)} %copy-done.8), custom_call_target="tpu_custom_call" | custom-call | tf_op jit(solution)/shard_map/quotient_part/pallas_call | solution.py:237
  39.3 1.0 copy-done.4
  40.3 2.0 %backward_part.5 = (f32[64,16,128]{2,1,0:T(8,128)S(1)}, f32[64,16,128]{2,1,0:T(8,128)S(1)}, f32[64,16,128]{2,1,0:T(8,128)S(1)}) custom-call(f32[6272,128]{1,0:T(8,128)S(1)} %quotient_part.2.field, f32[48,144]{1,0:T(8,128)S(1)} %pad_maximum_fusion.axial, f32[16,8,256]{2,1,0:T(8,128)S(1)} %all-to-all-done.sums, bf16[3,256,256]{2,1,0:T(8,128)(2,1)S(1)} %copy-done.4), custom_call_target="tpu_custom_call" | custom-call | tf_op jit(solution)/shard_map/backward_part/pallas_call | solution.py:296
  42.5 3.2 %collective-permute-start.9 = (f32[64,16,128]{2,1,0:T(8,128)S(1)}, f32[64,16,128]{2,1,0:T(8,128)S(1)}, u32[]{:S(2)}, u32[]{:S(2)}) collective-permute-start(f32[64,16,128]{2,1,0:T(8,128)S(1)} %get-tuple-element.34), channel_id=1, source_target_pairs={{1,2},{2,1},{3,4},{4,3},{5,6},{6,5},{7,8},{8,7},{9,10},{10,9},{11,... | collective-permute-start | bytes 1572872 | tf_op jit(solution)/shard_map/ppermute | solution.py:315
  45.7 2.0 %backward_part.4 = (f32[64,16,128]{2,1,0:T(8,128)S(1)}, f32[64,16,128]{2,1,0:T(8,128)S(1)}, f32[64,16,128]{2,1,0:T(8,128)S(1)}) custom-call(f32[6272,128]{1,0:T(8,128)S(1)} %quotient_part.2.field, f32[48,144]{1,0:T(8,128)S(1)} %pad_maximum_fusion.axial, f32[16,8,256]{2,1,0:T(8,128)S(1)} %all-to-all-done.sums, bf16[3,256,256]{2,1,0:T(8,128)(2,1)S(1)} %copy-done.4), custom_call_target="tpu_custom_call" | custom-call | tf_op jit(solution)/shard_map/backward_part/pallas_call | solution.py:296
  47.7 0.4 collective-permute-start.4
  48.1 3.6 %collective-permute-start.5 = (f32[64,16,128]{2,1,0:T(8,128)S(1)}, f32[64,16,128]{2,1,0:T(8,128)S(1)}, u32[]{:S(2)}, u32[]{:S(2)}) collective-permute-start(f32[64,16,128]{2,1,0:T(8,128)S(1)} %get-tuple-element.31), channel_id=1, source_target_pairs={{1,2},{2,1},{3,4},{4,3},{5,6},{6,5},{7,8},{8,7},{9,10},{10,9},{11,... | collective-permute-start | bytes 1572872 | tf_op jit(solution)/shard_map/ppermute | solution.py:315
  51.8 12.6 %collective-permute-done.9 = f32[64,16,128]{2,1,0:T(8,128)S(1)} collective-permute-done((f32[64,16,128]{2,1,0:T(8,128)S(1)}, f32[64,16,128]{2,1,0:T(8,128)S(1)}, u32[]{:S(2)}, u32[]{:S(2)}) %collective-permute-start.9) | collective-permute-done | bytes 524320 | tf_op jit(solution)/shard_map/ppermute | solution.py:315
  64.3 5.6 %collective-permute-done.5 = f32[64,16,128]{2,1,0:T(8,128)S(1)} collective-permute-done((f32[64,16,128]{2,1,0:T(8,128)S(1)}, f32[64,16,128]{2,1,0:T(8,128)S(1)}, u32[]{:S(2)}, u32[]{:S(2)}) %collective-permute-start.5) | collective-permute-done | bytes 524320 | tf_op jit(solution)/shard_map/ppermute | solution.py:315
  69.9 0.3 multiply_multiply_fusion.3
  70.4 3.1 %collective-permute-start.11 = (f32[64,16,128]{2,1,0:T(8,128)S(1)}, f32[64,16,128]{2,1,0:T(8,128)S(1)}, u32[]{:S(2)}, u32[]{:S(2)}) collective-permute-start(f32[64,16,128]{2,1,0:T(8,128)S(1)} %get-tuple-element.42.own), channel_id=1, source_target_pairs={{1,2},{2,1},{3,4},{4,3},{5,6},{6,5},{7,8},{8,7},{9,10},{10,9},{11,... | collective-permute-start | bytes 1572872 | tf_op jit(solution)/shard_map/ppermute | solution.py:315
  73.4 0.4 collective-permute-start.6
  73.9 3.6 %collective-permute-start.7 = (f32[64,16,128]{2,1,0:T(8,128)S(1)}, f32[64,16,128]{2,1,0:T(8,128)S(1)}, u32[]{:S(2)}, u32[]{:S(2)}) collective-permute-start(f32[64,16,128]{2,1,0:T(8,128)S(1)} %get-tuple-element.41.own), channel_id=1, source_target_pairs={{1,2},{2,1},{3,4},{4,3},{5,6},{6,5},{7,8},{8,7},{9,10},{10,9},{11,... | collective-permute-start | bytes 1572872 | tf_op jit(solution)/shard_map/ppermute | solution.py:315
  77.5 14.6 %collective-permute-done.11.far = f32[64,16,128]{2,1,0:T(8,128)S(1)} collective-permute-done((f32[64,16,128]{2,1,0:T(8,128)S(1)}, f32[64,16,128]{2,1,0:T(8,128)S(1)}, u32[]{:S(2)}, u32[]{:S(2)}) %collective-permute-start.11) | collective-permute-done | bytes 524320 | tf_op jit(solution)/shard_map/ppermute | solution.py:315
  92.1 2.0 %forward_part.7.refs_1_ = f32[3120,128]{1,0:T(8,128)S(1)} custom-call(f32[64,16,128]{2,1,0:T(8,128)S(1)} %get-tuple-element.42.own, f32[64,16,128]{2,1,0:T(8,128)S(1)} %collective-permute-done.10.near, f32[64,16,128]{2,1,0:T(8,128)S(1)} %collective-permute-done.11.far, bf16[48,144]{1,0:T(8,128)(2,1)S(1)} %pad_maximum_fusion.1.axial, ...), custom_call_target="tpu_custom_call" | custom-call | tf_op jit(solution)/shard_map/forward_part/pallas_call | solution.py:192
  94.2 3.5 %collective-permute-done.7.far = f32[64,16,128]{2,1,0:T(8,128)S(1)} collective-permute-done((f32[64,16,128]{2,1,0:T(8,128)S(1)}, f32[64,16,128]{2,1,0:T(8,128)S(1)}, u32[]{:S(2)}, u32[]{:S(2)}) %collective-permute-start.7) | collective-permute-done | bytes 524320 | tf_op jit(solution)/shard_map/ppermute | solution.py:315
  97.7 2.0 %forward_part.6.refs_0_ = f32[3120,128]{1,0:T(8,128)S(1)} custom-call(f32[64,16,128]{2,1,0:T(8,128)S(1)} %get-tuple-element.41.own, f32[64,16,128]{2,1,0:T(8,128)S(1)} %collective-permute-done.6.near, f32[64,16,128]{2,1,0:T(8,128)S(1)} %collective-permute-done.7.far, bf16[48,144]{1,0:T(8,128)(2,1)S(1)} %pad_maximum_fusion.1.axial, ...), custom_call_target="tpu_custom_call" | custom-call | tf_op jit(solution)/shard_map/forward_part/pallas_call | solution.py:192
  99.8 6.0 %quotient_part.3.field = f32[6272,128]{1,0:T(8,128)S(1)} custom-call(f32[3120,128]{1,0:T(8,128)S(1)} %forward_part.6.refs_0_, f32[3120,128]{1,0:T(8,128)S(1)} %forward_part.7.refs_1_, f32[48,128,128]{2,1,0:T(8,128)S(1)} %bitcast.15, bf16[3,128,384]{2,1,0:T(8,128)(2,1)S(1)} %copy-done.7, bf16[3,128,384]{2,1,0:T(8,128)(2,1)S(1)} %copy-done.9), custom_call_target="tpu_custom_call" | custom-call | tf_op jit(solution)/shard_map/quotient_part/pallas_call | solution.py:237
  105.8 2.0 %backward_part.6 = (f32[64,16,128]{2,1,0:T(8,128)S(1)}, f32[64,16,128]{2,1,0:T(8,128)S(1)}, f32[64,16,128]{2,1,0:T(8,128)S(1)}) custom-call(f32[6272,128]{1,0:T(8,128)S(1)} %quotient_part.3.field, f32[48,144]{1,0:T(8,128)S(1)} %pad_maximum_fusion.axial, f32[16,8,256]{2,1,0:T(8,128)S(1)} %all-to-all-done.sums, bf16[3,256,256]{2,1,0:T(8,128)(2,1)S(1)} %copy-done.5), custom_call_target="tpu_custom_call" | custom-call | tf_op jit(solution)/shard_map/backward_part/pallas_call | solution.py:296
  107.9 3.1 %collective-permute-start.13 = (f32[64,16,128]{2,1,0:T(8,128)S(1)}, f32[64,16,128]{2,1,0:T(8,128)S(1)}, u32[]{:S(2)}, u32[]{:S(2)}) collective-permute-start(f32[64,16,128]{2,1,0:T(8,128)S(1)} %get-tuple-element.37), channel_id=1, source_target_pairs={{1,2},{2,1},{3,4},{4,3},{5,6},{6,5},{7,8},{8,7},{9,10},{10,9},{11,... | collective-permute-start | bytes 1572872 | tf_op jit(solution)/shard_map/ppermute | solution.py:315
  111.0 2.0 %backward_part.7 = (f32[64,16,128]{2,1,0:T(8,128)S(1)}, f32[64,16,128]{2,1,0:T(8,128)S(1)}, f32[64,16,128]{2,1,0:T(8,128)S(1)}) custom-call(f32[6272,128]{1,0:T(8,128)S(1)} %quotient_part.3.field, f32[48,144]{1,0:T(8,128)S(1)} %pad_maximum_fusion.axial, f32[16,8,256]{2,1,0:T(8,128)S(1)} %all-to-all-done.sums, bf16[3,256,256]{2,1,0:T(8,128)(2,1)S(1)} %copy-done.5), custom_call_target="tpu_custom_call" | custom-call | tf_op jit(solution)/shard_map/backward_part/pallas_call | solution.py:296
  113.0 0.4 collective-permute-start.14
  113.4 3.6 %collective-permute-start.15 = (f32[64,16,128]{2,1,0:T(8,128)S(1)}, f32[64,16,128]{2,1,0:T(8,128)S(1)}, u32[]{:S(2)}, u32[]{:S(2)}) collective-permute-start(f32[64,16,128]{2,1,0:T(8,128)S(1)} %get-tuple-element.40), channel_id=1, source_target_pairs={{1,2},{2,1},{3,4},{4,3},{5,6},{6,5},{7,8},{8,7},{9,10},{10,9},{11,... | collective-permute-start | bytes 1572872 | tf_op jit(solution)/shard_map/ppermute | solution.py:315
  117.1 12.5 %collective-permute-done.13 = f32[64,16,128]{2,1,0:T(8,128)S(1)} collective-permute-done((f32[64,16,128]{2,1,0:T(8,128)S(1)}, f32[64,16,128]{2,1,0:T(8,128)S(1)}, u32[]{:S(2)}, u32[]{:S(2)}) %collective-permute-start.13) | collective-permute-done | bytes 524320 | tf_op jit(solution)/shard_map/ppermute | solution.py:315
  129.6 0.1 multiply_multiply_fusion.1
  129.8 5.5 %collective-permute-done.15 = f32[64,16,128]{2,1,0:T(8,128)S(1)} collective-permute-done((f32[64,16,128]{2,1,0:T(8,128)S(1)}, f32[64,16,128]{2,1,0:T(8,128)S(1)}, u32[]{:S(2)}, u32[]{:S(2)}) %collective-permute-start.15) | collective-permute-done | bytes 524320 | tf_op jit(solution)/shard_map/ppermute | solution.py:315
  135.2 0.1 multiply_multiply_fusion
  135.5 1.3 copy.20
  (53 shorter events, 0.7 us)
Async XLA Ops:
  0.0 9.4 %copy-start.12 = (f32[3,32]{1,0:T(4,128)S(1)}, f32[3,32]{1,0:T(4,128)}, u32[]{:S(2)}) copy-start(f32[3,32]{1,0:T(4,128)} %param.9) | copy-start | bytes 1156
  0.0 9.6 %copy-start.13 = (f32[3,64]{1,0:T(4,128)S(1)}, f32[3,64]{1,0:T(4,128)}, u32[]{:S(2)}) copy-start(f32[3,64]{1,0:T(4,128)} %param.7) | copy-start | bytes 2308
  0.0 10.1 %copy-start.14 = (f32[3,64]{1,0:T(4,128)S(1)}, f32[3,64]{1,0:T(4,128)}, u32[]{:S(2)}) copy-start(f32[3,64]{1,0:T(4,128)} %param.8) | copy-start | bytes 2308
  1.9 3.9 %copy-start.10 = (f32[16,128,128]{2,0,1:T(8,128)}, f32[16,128,128]{2,0,1:T(8,128)S(1)}, u32[]{:S(2)}) copy-start(f32[16,128,128]{2,0,1:T(8,128)S(1)} %copy.22) | copy-start | bytes 3145732
  2.0 23.2 %collective-permute-start.2 = (f32[64,16,128]{2,1,0:T(8,128)S(1)}, f32[64,16,128]{2,1,0:T(8,128)S(1)}, u32[]{:S(2)}, u32[]{:S(2)}) collective-permute-start(f32[64,16,128]{2,1,0:T(8,128)S(1)} %get-tuple-element.43.own), channel_id=1, source_target_pairs={{0,1},{1,0},{2,3},{3,2},{4,5},{5,4},{6,7},{7,6},{8,9},{9,8},{10,11... | collective-permute-start | bytes 1572872 | tf_op jit(solution)/shard_map/ppermute | solution.py:315
  2.7 22.5 %collective-permute-start.3 = (f32[64,16,128]{2,1,0:T(8,128)S(1)}, f32[64,16,128]{2,1,0:T(8,128)}, u32[]{:S(2)}, u32[]{:S(2)}) collective-permute-start(f32[64,16,128]{2,1,0:T(8,128)S(1)} %get-tuple-element.43.own), channel_id=1, source_target_pairs={{1,2},{2,1},{3,4},{4,3},{5,6},{6,5},{7,8},{8,7},{9,10},{10,9},{11,... | collective-permute-start | bytes 1572872 | tf_op jit(solution)/shard_map/ppermute | solution.py:315
  5.8 22.6 %collective-permute-start = (f32[64,16,128]{2,1,0:T(8,128)S(1)}, f32[64,16,128]{2,1,0:T(8,128)S(1)}, u32[]{:S(2)}, u32[]{:S(2)}) collective-permute-start(f32[64,16,128]{2,1,0:T(8,128)S(1)} %get-tuple-element.44.own), channel_id=1, source_target_pairs={{0,1},{1,0},{2,3},{3,2},{4,5},{5,4},{6,7},{7,6},{8,9},{9,8},{10,11... | collective-permute-start | bytes 1572872 | tf_op jit(solution)/shard_map/ppermute | solution.py:315
  6.2 25.1 %collective-permute-start.1 = (f32[64,16,128]{2,1,0:T(8,128)S(1)}, f32[64,16,128]{2,1,0:T(8,128)S(1)}, u32[]{:S(2)}, u32[]{:S(2)}) collective-permute-start(f32[64,16,128]{2,1,0:T(8,128)S(1)} %get-tuple-element.44.own), channel_id=1, source_target_pairs={{1,2},{2,1},{3,4},{4,3},{5,6},{6,5},{7,8},{8,7},{9,10},{10,9},{11,... | collective-permute-start | bytes 1572872 | tf_op jit(solution)/shard_map/ppermute | solution.py:315
  13.5 11.7 %copy-start.2 = (bf16[3,256,256]{2,1,0:T(8,128)(2,1)S(1)}, bf16[3,256,256]{2,1,0:T(8,128)(2,1)}, u32[]{:S(2)}) copy-start(bf16[3,256,256]{2,1,0:T(8,128)(2,1)} %get-tuple-element.23.lateral) | copy-start | bytes 1179652
  19.3 20.0 %all-to-all-start = ((f32[16,8,256]{2,1,0:T(8,128)}), f32[16,8,256]{2,1,0:T(8,128)S(1)}, u32[]{:S(2)}, u32[]{:S(2)}) async-start(f32[16,8,256]{2,1,0:T(8,128)} %broadcast_in_dim.2), calls=%async_computation | async-start | bytes 262144 | tf_op jit(solution)/shard_map/all_to_all | solution.py:143
  25.2 8.1 %copy-start.8 = (bf16[3,128,384]{2,1,0:T(8,128)(2,1)S(1)}, bf16[3,128,384]{2,1,0:T(8,128)(2,1)}, u32[]{:S(2)}) copy-start(bf16[3,128,384]{2,1,0:T(8,128)(2,1)} %get-tuple-element.25.refs_4_) | copy-start | bytes 884740
  28.3 5.0 %copy-start = (f32[3,16,128,128]{3,2,1,0:T(8,128)S(1)}, f32[3,16,128,128]{3,2,1,0:T(8,128)}, u32[]{:S(2)}) copy-start(f32[3,16,128,128]{3,2,1,0:T(8,128)} %param.5) | copy-start | bytes 9437188
  28.3 5.0 %copy-start.6 = (bf16[3,128,384]{2,1,0:T(8,128)(2,1)S(1)}, bf16[3,128,384]{2,1,0:T(8,128)(2,1)}, u32[]{:S(2)}) copy-start(bf16[3,128,384]{2,1,0:T(8,128)(2,1)} %get-tuple-element.24.refs_3_) | copy-start | bytes 884740
  39.3 1.0 copy-start.4
  42.4 9.4 %collective-permute-start.8 = (f32[64,16,128]{2,1,0:T(8,128)S(1)}, f32[64,16,128]{2,1,0:T(8,128)S(1)}, u32[]{:S(2)}, u32[]{:S(2)}) collective-permute-start(f32[64,16,128]{2,1,0:T(8,128)S(1)} %get-tuple-element.33), channel_id=1, source_target_pairs={{0,1},{1,0},{2,3},{3,2},{4,5},{5,4},{6,7},{7,6},{8,9},{9,8},{10,11... | collective-permute-start | bytes 1572872 | tf_op jit(solution)/shard_map/ppermute | solution.py:315
  42.4 27.5 %copy-start.11 = (f32[16,128,128]{2,0,1:T(8,128)S(1)}, f32[16,128,128]{2,0,1:T(8,128)}, u32[]{:S(2)}) copy-start(f32[16,128,128]{2,0,1:T(8,128)} %copy-done.10) | copy-start | bytes 3145732
  42.5 21.9 %collective-permute-start.9 = (f32[64,16,128]{2,1,0:T(8,128)S(1)}, f32[64,16,128]{2,1,0:T(8,128)S(1)}, u32[]{:S(2)}, u32[]{:S(2)}) collective-permute-start(f32[64,16,128]{2,1,0:T(8,128)S(1)} %get-tuple-element.34), channel_id=1, source_target_pairs={{1,2},{2,1},{3,4},{4,3},{5,6},{6,5},{7,8},{8,7},{9,10},{10,9},{11,... | collective-permute-start | bytes 1572872 | tf_op jit(solution)/shard_map/ppermute | solution.py:315
  47.7 16.6 %collective-permute-start.4 = (f32[64,16,128]{2,1,0:T(8,128)S(1)}, f32[64,16,128]{2,1,0:T(8,128)S(1)}, u32[]{:S(2)}, u32[]{:S(2)}) collective-permute-start(f32[64,16,128]{2,1,0:T(8,128)S(1)} %get-tuple-element.30), channel_id=1, source_target_pairs={{0,1},{1,0},{2,3},{3,2},{4,5},{5,4},{6,7},{7,6},{8,9},{9,8},{10,11... | collective-permute-start | bytes 1572872 | tf_op jit(solution)/shard_map/ppermute | solution.py:315
  48.1 21.8 %collective-permute-start.5 = (f32[64,16,128]{2,1,0:T(8,128)S(1)}, f32[64,16,128]{2,1,0:T(8,128)S(1)}, u32[]{:S(2)}, u32[]{:S(2)}) collective-permute-start(f32[64,16,128]{2,1,0:T(8,128)S(1)} %get-tuple-element.31), channel_id=1, source_target_pairs={{1,2},{2,1},{3,4},{4,3},{5,6},{6,5},{7,8},{8,7},{9,10},{10,9},{11,... | collective-permute-start | bytes 1572872 | tf_op jit(solution)/shard_map/ppermute | solution.py:315
  69.9 22.1 %copy-start.3 = (bf16[3,256,256]{2,1,0:T(8,128)(2,1)S(1)}, bf16[3,256,256]{2,1,0:T(8,128)(2,1)}, u32[]{:S(2)}) copy-start(bf16[3,256,256]{2,1,0:T(8,128)(2,1)} %get-tuple-element.23.lateral) | copy-start | bytes 1179652
  70.3 7.2 %collective-permute-start.10 = (f32[64,16,128]{2,1,0:T(8,128)S(1)}, f32[64,16,128]{2,1,0:T(8,128)S(1)}, u32[]{:S(2)}, u32[]{:S(2)}) collective-permute-start(f32[64,16,128]{2,1,0:T(8,128)S(1)} %get-tuple-element.42.own), channel_id=1, source_target_pairs={{0,1},{1,0},{2,3},{3,2},{4,5},{5,4},{6,7},{7,6},{8,9},{9,8},{10,11... | collective-permute-start | bytes 1572872 | tf_op jit(solution)/shard_map/ppermute | solution.py:315
  70.4 21.7 %collective-permute-start.11 = (f32[64,16,128]{2,1,0:T(8,128)S(1)}, f32[64,16,128]{2,1,0:T(8,128)S(1)}, u32[]{:S(2)}, u32[]{:S(2)}) collective-permute-start(f32[64,16,128]{2,1,0:T(8,128)S(1)} %get-tuple-element.42.own), channel_id=1, source_target_pairs={{1,2},{2,1},{3,4},{4,3},{5,6},{6,5},{7,8},{8,7},{9,10},{10,9},{11,... | collective-permute-start | bytes 1572872 | tf_op jit(solution)/shard_map/ppermute | solution.py:315
  73.4 20.7 %collective-permute-start.6 = (f32[64,16,128]{2,1,0:T(8,128)S(1)}, f32[64,16,128]{2,1,0:T(8,128)S(1)}, u32[]{:S(2)}, u32[]{:S(2)}) collective-permute-start(f32[64,16,128]{2,1,0:T(8,128)S(1)} %get-tuple-element.41.own), channel_id=1, source_target_pairs={{0,1},{1,0},{2,3},{3,2},{4,5},{5,4},{6,7},{7,6},{8,9},{9,8},{10,11... | collective-permute-start | bytes 1572872 | tf_op jit(solution)/shard_map/ppermute | solution.py:315
  73.9 23.9 %collective-permute-start.7 = (f32[64,16,128]{2,1,0:T(8,128)S(1)}, f32[64,16,128]{2,1,0:T(8,128)S(1)}, u32[]{:S(2)}, u32[]{:S(2)}) collective-permute-start(f32[64,16,128]{2,1,0:T(8,128)S(1)} %get-tuple-element.41.own), channel_id=1, source_target_pairs={{1,2},{2,1},{3,4},{4,3},{5,6},{6,5},{7,8},{8,7},{9,10},{10,9},{11,... | collective-permute-start | bytes 1572872 | tf_op jit(solution)/shard_map/ppermute | solution.py:315
  92.1 7.7 %copy-start.9 = (bf16[3,128,384]{2,1,0:T(8,128)(2,1)S(1)}, bf16[3,128,384]{2,1,0:T(8,128)(2,1)}, u32[]{:S(2)}) copy-start(bf16[3,128,384]{2,1,0:T(8,128)(2,1)} %get-tuple-element.25.refs_4_) | copy-start | bytes 884740
  94.1 5.6 %copy-start.1 = (f32[3,16,128,128]{3,2,1,0:T(8,128)S(1)}, f32[3,16,128,128]{3,2,1,0:T(8,128)}, u32[]{:S(2)}) copy-start(f32[3,16,128,128]{3,2,1,0:T(8,128)} %param.5) | copy-start | bytes 9437188
  94.2 5.6 %copy-start.7 = (bf16[3,128,384]{2,1,0:T(8,128)(2,1)S(1)}, bf16[3,128,384]{2,1,0:T(8,128)(2,1)}, u32[]{:S(2)}) copy-start(bf16[3,128,384]{2,1,0:T(8,128)(2,1)} %get-tuple-element.24.refs_3_) | copy-start | bytes 884740
  99.8 6.0 %copy-start.5 = (bf16[3,256,256]{2,1,0:T(8,128)(2,1)S(1)}, bf16[3,256,256]{2,1,0:T(8,128)(2,1)}, u32[]{:S(2)}) copy-start(bf16[3,256,256]{2,1,0:T(8,128)(2,1)} %get-tuple-element.28.lateral) | copy-start | bytes 1179652
  107.8 9.3 %collective-permute-start.12 = (f32[64,16,128]{2,1,0:T(8,128)S(1)}, f32[64,16,128]{2,1,0:T(8,128)S(1)}, u32[]{:S(2)}, u32[]{:S(2)}) collective-permute-start(f32[64,16,128]{2,1,0:T(8,128)S(1)} %get-tuple-element.36), channel_id=1, source_target_pairs={{0,1},{1,0},{2,3},{3,2},{4,5},{5,4},{6,7},{7,6},{8,9},{9,8},{10,11... | collective-permute-start | bytes 1572872 | tf_op jit(solution)/shard_map/ppermute | solution.py:315
  107.9 21.7 %collective-permute-start.13 = (f32[64,16,128]{2,1,0:T(8,128)S(1)}, f32[64,16,128]{2,1,0:T(8,128)S(1)}, u32[]{:S(2)}, u32[]{:S(2)}) collective-permute-start(f32[64,16,128]{2,1,0:T(8,128)S(1)} %get-tuple-element.37), channel_id=1, source_target_pairs={{1,2},{2,1},{3,4},{4,3},{5,6},{6,5},{7,8},{8,7},{9,10},{10,9},{11,... | collective-permute-start | bytes 1572872 | tf_op jit(solution)/shard_map/ppermute | solution.py:315
  113.0 16.8 %collective-permute-start.14 = (f32[64,16,128]{2,1,0:T(8,128)S(1)}, f32[64,16,128]{2,1,0:T(8,128)S(1)}, u32[]{:S(2)}, u32[]{:S(2)}) collective-permute-start(f32[64,16,128]{2,1,0:T(8,128)S(1)} %get-tuple-element.39), channel_id=1, source_target_pairs={{0,1},{1,0},{2,3},{3,2},{4,5},{5,4},{6,7},{7,6},{8,9},{9,8},{10,11... | collective-permute-start | bytes 1572872 | tf_op jit(solution)/shard_map/ppermute | solution.py:315
  113.4 21.8 %collective-permute-start.15 = (f32[64,16,128]{2,1,0:T(8,128)S(1)}, f32[64,16,128]{2,1,0:T(8,128)S(1)}, u32[]{:S(2)}, u32[]{:S(2)}) collective-permute-start(f32[64,16,128]{2,1,0:T(8,128)S(1)} %get-tuple-element.40), channel_id=1, source_target_pairs={{1,2},{2,1},{3,4},{4,3},{5,6},{6,5},{7,8},{8,7},{9,10},{10,9},{11,... | collective-permute-start | bytes 1572872 | tf_op jit(solution)/shard_map/ppermute | solution.py:315

commit v2 on v1

v2 whole, which is shorter than its diff:
```python
import functools

import jax
import jax.numpy as jnp
from jax import lax
from jax.experimental import pallas as pl
from jax.experimental.pallas import tpu as pltpu
from jax.sharding import PartitionSpec as P


ITERS = 2
GROUP = 8
VMEM_LIMIT = 16 << 20
ROWS = 64
ALONG_Y = 1
FORWARD_Z = 8
BACKWARD_Z = 8
DIVIDE = 8
BACK = 8
LANES = 128
F32 = jnp.float32
BF16 = jnp.bfloat16
PRECISE = lax.Precision.HIGHEST


def split(value):
    high = value.astype(BF16)
    low = (value - high.astype(F32)).astype(BF16)
    return high, low


def dot(left, right):
    return jnp.dot(left, right, preferred_element_type=F32)


def normalized_lines(taps, width):
    view_count, tap_count = taps.shape
    values = jnp.concatenate([taps[...], jnp.zeros((view_count, width - tap_count), F32)], axis=1)
    return values / jnp.sum(values, axis=1, keepdims=True)


def matrices_kernel(
    position, taps_x, taps_y, taps_z, fwd_x, bwd_x, fwd_y, bwd_y, fwd_z, bwd_z, sums_x, sums_y, sums_z, *, count
):
    view_count, tap_count = taps_x.shape
    size = fwd_x.shape[1]
    rows = lax.broadcasted_iota(jnp.int32, (size, size), 0)
    cols = lax.broadcasted_iota(jnp.int32, (size, size), 1)
    tap_ids = cols - rows + tap_count // 2
    inside = (tap_ids >= 0) & (tap_ids < tap_count)
    for taps, is_x in ((taps_x, True), (taps_y, False)):
        values = normalized_lines(taps, size)
        for view in range(view_count):
            line = jnp.broadcast_to(values[view : view + 1, :], (size, size))
            matrix = pltpu.roll(line, size - tap_count // 2, 1, stride=1, stride_axis=0)
            matrix = jnp.where(inside, matrix, 0.0)
            high, low = split(matrix)
            high_t, low_t = split(matrix.T)
            total = jnp.sum(matrix, axis=0, keepdims=True)
            if is_x:
                fwd_x[view] = jnp.concatenate([high, high, low], axis=1)
                bwd_x[view] = jnp.concatenate([high_t, high_t, low_t], axis=1)
                sums_x[view : view + 1, :] = total
            else:
                one = jnp.concatenate([high_t, low_t], axis=1)
                fwd_y[view] = jnp.concatenate([one, one], axis=0)
                one = jnp.concatenate([high, low], axis=1)
                bwd_y[view] = jnp.concatenate([one, one], axis=0)
                sums_y[view : view + 1, :] = total

    block_len = sums_z.shape[1]
    planes = view_count * block_len
    reach = taps_z.shape[1] // 2
    place = position[0]
    odd = (place & 1) == 1
    rows = lax.broadcasted_iota(jnp.int32, (block_len, size), 0)
    cols = lax.broadcasted_iota(jnp.int32, (block_len, size), 1)
    target = place * block_len + rows + reach - cols
    kept = (target >= 0) & (target < count * block_len)
    values = normalized_lines(taps_z, size)
    bands = []
    for view in range(view_count):
        line = jnp.broadcast_to(values[view : view + 1, :], (block_len, size))
        total = jnp.sum(jnp.where(kept, line, 0.0), axis=1, keepdims=True)
        sums_z[view] = jnp.broadcast_to(total, (block_len, size))

        def moved(ahead):
            return pltpu.roll(line, (-ahead) % size, 1, stride=1, stride_axis=0)

        near = jnp.where(odd, moved(reach - 2 * block_len), moved(reach))
        far = jnp.where(odd, moved(reach - block_len), moved(reach - 3 * block_len))
        band = jnp.where(cols < block_len, moved(reach), jnp.where(cols < 2 * block_len, near, far))
        bands.append(jnp.where(cols < 3 * block_len, band, 0.0))
    matrix = jnp.concatenate(bands, axis=0)
    square = jnp.concatenate([matrix, jnp.zeros((size - planes, size), F32)], axis=0)
    blank = jnp.zeros((planes, size), F32)

    def spread(one, two, three):
        wide = [jnp.concatenate([value, blank], axis=1) for value in (one, two, three)]
        return wide[0] + pltpu.roll(wide[1], planes, 1) + pltpu.roll(wide[2], 2 * planes, 1)

    high, low = split(matrix)
    high = high.astype(F32)
    fwd_z[...] = spread(high, high, low.astype(F32)).astype(BF16)
    matrix = square.T[:planes]
    bwd_z[...] = spread(matrix, matrix, matrix)


def matrices(kernel_x, kernel_y, kernel_z, size, block_len, axis):
    view_count, tap_count = kernel_x.shape
    planes = view_count * block_len
    assert size == LANES and tap_count <= size and kernel_y.shape == kernel_x.shape
    assert view_count == 3 and 3 * block_len + kernel_z.shape[1] <= size
    vmem = pl.BlockSpec(memory_space=pltpu.VMEM)
    out = jax.ShapeDtypeStruct
    return pl.pallas_call(
        functools.partial(matrices_kernel, count=lax.axis_size(axis)),
        in_specs=[pl.BlockSpec(memory_space=pltpu.SMEM), vmem, vmem, vmem],
        out_shape=(
            out((view_count, size, 3 * size), BF16),
            out((view_count, size, 3 * size), BF16),
            out((view_count, 2 * size, 2 * size), BF16),
            out((view_count, 2 * size, 2 * size), BF16),
            out((planes, 2 * size), BF16),
            out((planes, 2 * size), F32),
            out((view_count, size), F32),
            out((view_count, size), F32),
            out((view_count, block_len, size), F32),
        ),
        compiler_params=pltpu.CompilerParams(vmem_limit_bytes=VMEM_LIMIT),
        name="matrices",
    )(lax.axis_index(axis).astype(jnp.int32).reshape(1), kernel_x, kernel_y, kernel_z)


def totals_kernel(recorded, initial, sums_x, sums_y, sums_z, out, *, block_len):
    view_count = sums_x.shape[0]
    shape = out.shape
    lanes = lax.broadcasted_iota(jnp.int32, shape, 1)
    view_of = (lanes % (view_count * block_len)) // block_len
    row_of = lax.broadcasted_iota(jnp.int32, shape, 0)
    size_x = initial.shape[1]
    flats = [jnp.zeros((size_x, LANES), F32) for _ in range(view_count)]
    for z in range(block_len):
        plane = initial[z]
        flats = [flat + plane * sums_z[view, z : z + 1, :] for view, flat in enumerate(flats)]
    weighted = jnp.concatenate(
        [
            jnp.dot(sums_x[...], flat, precision=PRECISE, preferred_element_type=F32)[view : view + 1]
            for view, flat in enumerate(flats)
        ],
        axis=0,
    )
    weighted = weighted * sums_y[...]
    result = jnp.zeros(shape, F32)
    for view in range(view_count):

        def add(z, total):
            return total + jnp.sum(recorded[view * block_len + z].reshape(-1, 8, LANES), axis=0)

        data = lax.fori_loop(0, block_len, add, jnp.zeros((8, LANES), F32), unroll=4)
        blur_total = jnp.sum(weighted[view : view + 1, :])
        data_total = jnp.sum(data)
        value = jnp.where(row_of == 0, data_total, blur_total)
        result = jnp.where(view_of == view, value, result)
    out[...] = result


def totals(recorded, initial, sums_x, sums_y, sums_z):
    return pl.pallas_call(
        functools.partial(totals_kernel, block_len=initial.shape[0]),
        out_shape=jax.ShapeDtypeStruct((8, 2 * LANES), F32),
        compiler_params=pltpu.CompilerParams(vmem_limit_bytes=VMEM_LIMIT),
        name="totals",
    )(*in_vmem(recorded), initial, sums_x, sums_y, sums_z)


def summed(value, axis):
    count = lax.axis_size(axis)
    if count & (count - 1):
        return lax.psum(value, axis)
    steps = [1 << bit for bit in range(count.bit_length() - 1)]
    for step in steps[1:2] + steps[:1] + steps[2:]:
        value = value + lax.ppermute(value, axis, [(i, i ^ step) for i in range(count)])
    return value


def in_vmem(*values):
    return [pltpu.with_memory_space_constraint(value, pltpu.VMEM) for value in values]


def forward_kernel(own, near, *refs, block_len):
    *fars, axial, lateral, out, fields = refs
    chunk = own.shape[0]
    view_count = lateral.shape[0]
    axial_matrix = axial[:, : 3 * view_count * block_len]
    spread = chunk + 1

    def along_z(index, carry):
        start = index * GROUP
        far = sum(ref[pl.ds(start, GROUP)] for ref in fars)
        window = jnp.concatenate([own[pl.ds(start, GROUP)], near[pl.ds(start, GROUP)], far], axis=1)
        high, low = split(window)
        terms = jnp.concatenate([high, low, high], axis=1)
        for pair in range(0, GROUP, 2):
            result = dot(axial_matrix, jnp.concatenate([terms[pair], terms[pair + 1]], axis=1))
            for side in (0, 1):
                row = (start + pair + side) * block_len
                high, low = split(result[:, side * LANES : (side + 1) * LANES])
                for view in range(view_count):
                    part = slice(view * block_len, (view + 1) * block_len)
                    fields[view, pl.ds(row, block_len), :LANES] = high[part]
                    fields[view, pl.ds(row, block_len), LANES:] = low[part]
        return carry

    lax.fori_loop(0, chunk // GROUP, along_z, 0, unroll=FORWARD_Z)

    def along_y(index, carry):
        start = index * ROWS
        for view in range(view_count):
            result = dot(fields[view, pl.ds(start * block_len, ROWS * block_len), :], lateral[view])
            result = result[:, :LANES] + result[:, LANES:]
            for i in range(ROWS):
                first = view * block_len * spread + start + i
                out[pl.ds(first, block_len, stride=spread), :] = result[
                    i * block_len : (i + 1) * block_len
                ]
        return carry

    lax.fori_loop(0, chunk // ROWS, along_y, 0, unroll=ALONG_Y)


def forward_part(own, near, fars, axial, lateral):
    chunk, block_len, size_y = own.shape
    view_count = lateral.shape[0]
    return pl.pallas_call(
        functools.partial(forward_kernel, block_len=block_len),
        out_shape=pltpu.VMEM((view_count * block_len * (chunk + 1), size_y), F32),
        scratch_shapes=[pltpu.VMEM((view_count, chunk * block_len, 2 * size_y), BF16)],
        compiler_params=pltpu.CompilerParams(vmem_limit_bytes=VMEM_LIMIT),
        name="forward_part",
    )(*in_vmem(own, near, *fars), axial, *in_vmem(lateral))


def quotient_kernel(*refs, chunks, block_len):
    parts, (recorded, fwd, bwd, out, terms) = refs[:chunks], refs[chunks:]
    view_count = fwd.shape[0]
    planes = view_count * block_len
    size_x = fwd.shape[1]
    chunk = size_x // chunks
    spread = planes + 1

    for view in range(view_count):

        def divide(index, carry):
            plane = view * block_len + 2 * index
            field = jnp.concatenate(
                [
                    jnp.concatenate(
                        [ref[pl.ds((plane + side) * (chunk + 1), chunk), :] for ref in parts], axis=0
                    )
                    for side in (0, 1)
                ],
                axis=1,
            )
            high, low = split(field)
            blurred = dot(fwd[view], jnp.concatenate([high, low, high], axis=0))
            data = jnp.concatenate([recorded[plane], recorded[plane + 1]], axis=1)
            high, low = split(data / blurred)
            terms[index, :size_x] = high
            terms[index, size_x:] = low
            return carry

        lax.fori_loop(0, block_len // 2, divide, 0, unroll=DIVIDE)

        def back(index, carry):
            plane = view * block_len + 2 * index
            both = terms[index]
            result = dot(bwd[view], jnp.concatenate([both, both[:size_x]], axis=0))
            out[pl.ds(plane, size_x, stride=spread), :] = result[:, :LANES]
            out[pl.ds(plane + 1, size_x, stride=spread), :] = result[:, LANES:]
            return carry

        lax.fori_loop(0, block_len // 2, back, 0, unroll=BACK)


def quotient_part(parts, recorded, fwd, bwd):
    planes, size_x, size_y = recorded.shape
    view_count = fwd.shape[0]
    return pl.pallas_call(
        functools.partial(quotient_kernel, chunks=len(parts), block_len=planes // view_count),
        out_shape=pltpu.VMEM((size_x * (planes + 1), size_y), F32),
        scratch_shapes=[pltpu.VMEM((planes // view_count // 2, 2 * size_x, 2 * size_y), BF16)],
        compiler_params=pltpu.CompilerParams(vmem_limit_bytes=VMEM_LIMIT),
        name="quotient_part",
    )(*in_vmem(*parts, recorded, fwd, bwd))


def backward_kernel(field, axial, sums, lateral, own, near, far, terms, *, block_len, offset):
    chunk = own.shape[0]
    view_count = lateral.shape[0]
    planes = view_count * block_len
    spread = planes + 1
    scaled = (axial[...] * (sums[1:2, :] / sums[0:1, :]))[:, : 3 * planes]
    high, low = split(scaled)
    lanes = lax.broadcasted_iota(jnp.int32, scaled.shape, 1)
    axial_matrix = jnp.where(lanes < 2 * planes, high.astype(F32), low.astype(F32)).astype(BF16)

    def along_y(index, carry):
        start = index * ROWS
        for view in range(view_count):
            rows = jnp.concatenate(
                [
                    field[pl.ds((offset + start + i) * spread + view * block_len, block_len), :]
                    for i in range(ROWS)
                ],
                axis=0,
            )
            result = dot(jnp.concatenate(split(rows), axis=1), lateral[view])
            result = result[:, :LANES] + result[:, LANES:]
            high, low = split(result.reshape(ROWS, block_len, LANES))
            for place, part in enumerate((high, low, high)):
                row = place * planes + view * block_len
                terms[pl.ds(start, ROWS), row : row + block_len, :] = part
        return carry

    lax.fori_loop(0, chunk // ROWS, along_y, 0, unroll=ALONG_Y)

    def along_z(index, carry):
        start = index * GROUP
        for pair in range(0, GROUP, 2):
            sent = dot(
                axial_matrix, jnp.concatenate([terms[start + pair], terms[start + pair + 1]], axis=1)
            )
            for side in (0, 1):
                lanes_of = slice(side * LANES, (side + 1) * LANES)
                for place, ref in enumerate((own, near, far)):
                    ref[start + pair + side] = sent[place * block_len : (place + 1) * block_len, lanes_of]
        return carry

    lax.fori_loop(0, chunk // GROUP, along_z, 0, unroll=BACKWARD_Z)


def backward_part(field, axial, sums, lateral, block_len, chunk, offset):
    size_y = field.shape[1]
    planes = lateral.shape[0] * block_len
    shape = pltpu.VMEM((chunk, block_len, size_y), F32)
    return pl.pallas_call(
        functools.partial(backward_kernel, block_len=block_len, offset=offset),
        out_shape=(shape, shape, shape),
        scratch_shapes=[pltpu.VMEM((chunk, 3 * planes, size_y), BF16)],
        compiler_params=pltpu.CompilerParams(vmem_limit_bytes=VMEM_LIMIT),
        name="backward_part",
    )(*in_vmem(field), axial, sums, *in_vmem(lateral))


def body(recorded, initial, kernel_x, kernel_y, kernel_z):
    view_count, block_len, size_x, size_y = recorded.shape
    assert kernel_z.shape[1] // 2 <= block_len
    count = lax.axis_size("slab")
    near_pairs = [p for i in range(0, count - 1, 2) for p in ((i, i + 1), (i + 1, i))]
    first_pairs = [p for i in range(3, count - 1, 4) for p in ((i, i + 1), (i + 1, i))]
    second_pairs = [p for i in range(1, count - 1, 4) for p in ((i, i + 1), (i + 1, i))]

    def swap(value, pairs):
        return lax.ppermute(value, "slab", pairs)

    estimate = jnp.transpose(initial, (1, 0, 2))
    planes = recorded.reshape(view_count * block_len, size_x, size_y)
    fars = [swap(estimate, first_pairs)]
    near = swap(estimate, near_pairs)
    fwd_x, bwd_x, fwd_y, bwd_y, fwd_z, bwd_z, sums_x, sums_y, sums_z = matrices(
        kernel_x, kernel_y, kernel_z, size_x, block_len, "slab"
    )
    sums = totals(planes, initial, sums_x, sums_y, sums_z)
    delayed, sums = lax.optimization_barrier((estimate, sums))
    sums = summed(sums, "slab")
    fars.append(swap(delayed, second_pairs))
    for iteration in range(ITERS):
        if iteration:
            fars = [swap(estimate, first_pairs + second_pairs)]
            near = swap(estimate, near_pairs)
        part = forward_part(estimate, near, fars, fwd_z, fwd_y)
        field = quotient_part([part], planes, fwd_x, bwd_x)
        own, near, far = backward_part(field, bwd_z, sums, bwd_y, block_len, size_x, 0)
        far = swap(far, first_pairs + second_pairs)
        near = swap(near, near_pairs)
        estimate = estimate * (own + near + far) / view_count
    return jnp.transpose(estimate, (1, 0, 2))


def solution(mesh):
    in_specs = (P(None, "slab", "groups", None), P("slab", "groups", None), P(), P(), P())
    out_specs = P("slab", "groups", None)
    return jax.shard_map(body, mesh=mesh, in_specs=in_specs, out_specs=out_specs, check_vma=False)
```

time: 137 us -> 138 us (level)
  waiting for transfers between devices: 57.3 us -> 91.3 us
  Pallas kernels: 35.8 us -> 14.9 us
  starting transfers between devices: 34.3 us -> 22.2 us
  local copies, waits for them, and re-layouts: 6.88 us -> 8.29 us
    ppermute x16 -> x13, waiting for transfers between devices: 57.3 us -> 91.3 us  [the longest x9 73.7 us: swap(): return lax.ppermute(value, 'slab', pairs)]
    pallas_call x2, Pallas kernels: 11.9 us -> 3.97 us  [quotient_part(): pl.pallas_call(functools.partial(quotient_kernel, chunks=len(parts), bloc...]
    ppermute x16 -> x13, starting transfers between devices: 29.1 us -> 22.2 us  [the longest x9 18.4 us: swap(): return lax.ppermute(value, 'slab', pairs)]
    all_to_all x1 -> x0, starting transfers between devices: 5.26 us -> none  [totals(): return lax.all_to_all(copies, axis, 0, 0)]
    pallas_call x2, Pallas kernels: 6.49 us -> 1.91 us  [the longest x1 1.1 us: totals(): pl.pallas_call(functools.partial(totals_kernel, block_len=initial.shape[0...]
    pallas_call x4 -> x2, Pallas kernels: 9.16 us -> 4.83 us  [forward_part(): pl.pallas_call(functools.partial(forward_kernel, block_len=block_len), ou...]
    unnamed x31 -> x15, local copies, waits for them, and re-layouts: 2.93 us -> 7 us
    pallas_call x4 -> x2, Pallas kernels: 8.16 us -> 4.2 us  [backward_part(): pl.pallas_call(functools.partial(backward_kernel, block_len=block_len, of...]
  transfers between devices with their start and end apart: 17 -> 13, of which waited for: 7 -> 7; matrix products, arithmetic and copies ran while one was open for 3% -> 0% of each run, Pallas kernels for 17% -> 1%
where the time goes in v2:
time: 138 us
  waiting for transfers between devices  91.3 us (66%)
  starting transfers between devices  22.2 us (16%)
  Pallas kernels  14.9 us (11%)
  local copies, waits for them, and re-layouts  8.29 us (6%)
    ppermute x9, waiting for transfers between devices, swap(): return lax.ppermute(value, 'slab', pairs)  73.7 us
    ppermute x9, starting transfers between devices, swap(): return lax.ppermute(value, 'slab', pairs)  18.4 us
    ppermute x4, waiting for transfers between devices, summed(): lax.ppermute(value, axis, [(i, i ^ step) for i in range(count)])  17.7 us
    unnamed x15, local copies, waits for them, and re-layouts  7 us
    pallas_call x2, Pallas kernels, forward_part(): pl.pallas_call(functools.partial(forward_kernel, block_len=block_len), ou...  4.83 us
    pallas_call x2, Pallas kernels, backward_part(): pl.pallas_call(functools.partial(backward_kernel, block_len=block_len, of...  4.2 us
    pallas_call x2, Pallas kernels, quotient_part(): pl.pallas_call(functools.partial(quotient_kernel, chunks=len(parts), bloc...  3.97 us
    ppermute x4, starting transfers between devices, summed(): lax.ppermute(value, axis, [(i, i ^ step) for i in range(count)])  3.72 us
  transfers between devices with their start and end apart: 13, of which 7 were waited for; matrix products, arithmetic and copies ran while one was open for 0% of the time, Pallas kernels for 1%

profile of v2, /device:TPU:11, one launch (start us, length us, event | category | flops | bytes accessed | tf_op | source)
XLA Modules:
  0.0 137.9 jit_solution(12154628062161621396)
XLA Ops:
  0.0 1.8 %copy.11 = f32[16,128,128]{2,0,1:T(8,128)S(1)} copy(f32[16,128,128]{2,1,0:T(8,128)} %initial.1) | data formatting | bytes 2097152 | tf_op args[1]
  1.8 0.7 collective-permute-start.1
  2.6 2.8 %collective-permute-start = (f32[128,16,128]{2,1,0:T(8,128)S(1)}, f32[128,16,128]{2,1,0:T(8,128)S(1)}, u32[]{:S(2)}, u32[]{:S(2)}) collective-permute-start(f32[128,16,128]{2,1,0:T(8,128)S(1)} %bitcast.13), channel_id=1, source_target_pairs={{0,1},{1,0},{2,3},{3,2},{4,5},{5,4},{6,7},{7,6},{8,9},{9,8},{10,11... | collective-permute-start | bytes 3145736 | tf_op jit(solution)/shard_map/ppermute | solution.py:365
  5.3 0.7 copy-done.4
  6.0 0.7 copy-done.5
  6.7 0.7 copy-done.6
  7.4 0.8 matrices.1
  8.2 0.0 copy-start
  8.2 1.9 %copy-done = f32[3,16,128,128]{3,2,1,0:T(8,128)S(1)} copy-done((f32[3,16,128,128]{3,2,1,0:T(8,128)S(1)}, f32[3,16,128,128]{3,2,1,0:T(8,128)}, u32[]{:S(2)}) %copy-start) | copy-done | bytes 3145752
  10.1 1.2 copy-done.2
  11.3 1.1 totals.1
  12.4 3.8 %collective-permute-start.2 = (f32[128,16,128]{2,1,0:T(8,128)S(1)}, f32[128,16,128]{2,1,0:T(8,128)S(1)}, u32[]{:S(2)}, u32[]{:S(2)}) collective-permute-start(f32[128,16,128]{2,1,0:T(8,128)S(1)} %bitcast.14), channel_id=1, source_target_pairs={{1,2},{2,1},{5,6},{6,5},{9,10},{10,9},{13,14},{14,13},{17,18},{18,... | collective-permute-start | bytes 3145736 | tf_op jit(solution)/shard_map/ppermute | solution.py:365
  16.3 0.1 collective-permute-start.3
  16.3 13.3 %collective-permute-done.3 = f32[8,256]{1,0:T(8,128)S(1)} collective-permute-done((f32[8,256]{1,0:T(8,128)S(1)}, f32[8,256]{1,0:T(8,128)S(1)}, u32[]{:S(2)}, u32[]{:S(2)}) %collective-permute-start.3) | collective-permute-done | bytes 8224 | tf_op jit(solution)/shard_map/ppermute | solution.py:183
  29.6 1.3 collective-permute-start.4
  30.9 0.8 collective-permute-done.4
  31.8 0.0 collective-permute-start.5
  31.8 2.5 %collective-permute-done.5 = f32[8,256]{1,0:T(8,128)S(1)} collective-permute-done((f32[8,256]{1,0:T(8,128)S(1)}, f32[8,256]{1,0:T(8,128)S(1)}, u32[]{:S(2)}, u32[]{:S(2)}) %collective-permute-start.5) | collective-permute-done | bytes 8224 | tf_op jit(solution)/shard_map/ppermute | solution.py:183
  34.3 2.3 %collective-permute-start.6 = (f32[8,256]{1,0:T(8,128)S(1)}, f32[8,256]{1,0:T(8,128)S(1)}, u32[]{:S(2)}, u32[]{:S(2)}) collective-permute-start(f32[8,256]{1,0:T(8,128)S(1)} %add.26), channel_id=1, source_target_pairs={{0,8},{1,9},{2,10},{3,11},{4,12},{5,13},{6,14},{7,15},{8,0},{9,1},... | collective-permute-start | bytes 24584 | tf_op jit(solution)/shard_map/ppermute | solution.py:183
  36.6 1.1 collective-permute-done.6
  37.7 0.0 collective-permute-done.1.refs_0_
  37.7 0.0 collective-permute-done.near
  37.7 0.0 collective-permute-done.2.refs_1_
  37.7 0.0 copy-start.1
  37.7 2.4 %forward_part.2.refs_0_ = f32[6192,128]{1,0:T(8,128)S(1)} custom-call(f32[128,16,128]{2,1,0:T(8,128)S(1)} %bitcast.15, f32[128,16,128]{2,1,0:T(8,128)S(1)} %collective-permute-done.near, f32[128,16,128]{2,1,0:T(8,128)S(1)} %collective-permute-done.1.refs_0_, f32[128,16,128]{2,1,0:T(8,128)S(1)} %collective-permute-done.2.refs_1_, ...), custom_call_target="tpu_custom_call" | custom-call | tf_op jit(solution)/shard_map/forward_part/pallas_call | solution.py:235
  40.2 0.0 copy-done.1
  40.2 2.0 %quotient_part.2.field = f32[6272,128]{1,0:T(8,128)S(1)} custom-call(f32[6192,128]{1,0:T(8,128)S(1)} %forward_part.2.refs_0_, f32[48,128,128]{2,1,0:T(8,128)S(1)} %bitcast.10, bf16[3,128,384]{2,1,0:T(8,128)(2,1)S(1)} %get-tuple-element.28.refs_2_, bf16[3,128,384]{2,1,0:T(8,128)(2,1)S(1)} %get-tuple-element.29.refs_3_), custom_call_target="tpu_custom_call" | custom-call | tf_op jit(solution)/shard_map/quotient_part/pallas_call | solution.py:289
  42.2 0.0 copy-start.3
  42.2 2.1 %backward_part.2 = (f32[128,16,128]{2,1,0:T(8,128)S(1)}, f32[128,16,128]{2,1,0:T(8,128)S(1)}, f32[128,16,128]{2,1,0:T(8,128)S(1)}) custom-call(f32[6272,128]{1,0:T(8,128)S(1)} %quotient_part.2.field, f32[48,256]{1,0:T(8,128)S(1)} %get-tuple-element.30.axial, f32[8,256]{1,0:T(8,128)S(1)} %add.27.sums, bf16[3,256,256]{2,1,0:T(8,128)(2,1)S(1)} %get-tuple-element.32.lateral), custom_call_target="tpu_custom_call" | custom-call | tf_op jit(solution)/shard_map/backward_part/pallas_call | solution.py:347
  44.3 2.7 %collective-permute-start.7 = (f32[128,16,128]{2,1,0:T(8,128)S(1)}, f32[128,16,128]{2,1,0:T(8,128)S(1)}, u32[]{:S(2)}, u32[]{:S(2)}) collective-permute-start(f32[128,16,128]{2,1,0:T(8,128)S(1)} %get-tuple-element.34), channel_id=1, source_target_pairs={{0,1},{1,0},{2,3},{3,2},{4,5},{5,4},{6,7},{7,6},{8,9},{9,8},{10,11... | collective-permute-start | bytes 3145736 | tf_op jit(solution)/shard_map/ppermute | solution.py:365
  47.0 2.8 %collective-permute-start.8 = (f32[128,16,128]{2,1,0:T(8,128)S(1)}, f32[128,16,128]{2,1,0:T(8,128)S(1)}, u32[]{:S(2)}, u32[]{:S(2)}) collective-permute-start(f32[128,16,128]{2,1,0:T(8,128)S(1)} %get-tuple-element.35), channel_id=1, source_target_pairs={{3,4},{4,3},{7,8},{8,7},{11,12},{12,11},{1,2},{2,1},{5,6},{6,5},{9... | collective-permute-start | bytes 3145736 | tf_op jit(solution)/shard_map/ppermute | solution.py:365
  49.7 0.0 collective-permute-done.7
  49.8 35.8 %collective-permute-done.8 = f32[128,16,128]{2,1,0:T(8,128)S(1)} collective-permute-done((f32[128,16,128]{2,1,0:T(8,128)S(1)}, f32[128,16,128]{2,1,0:T(8,128)S(1)}, u32[]{:S(2)}, u32[]{:S(2)}) %collective-permute-start.8) | collective-permute-done | bytes 1048608 | tf_op jit(solution)/shard_map/ppermute | solution.py:365
  85.6 0.0 copy-done.3
  85.6 0.7 multiply_multiply_fusion.own
  86.3 2.8 %collective-permute-start.10 = (f32[128,16,128]{2,1,0:T(8,128)S(1)}, f32[128,16,128]{2,1,0:T(8,128)S(1)}, u32[]{:S(2)}, u32[]{:S(2)}) collective-permute-start(f32[128,16,128]{2,1,0:T(8,128)S(1)} %multiply_multiply_fusion.own), channel_id=1, source_target_pairs={{3,4},{4,3},{7,8},{8,7},{11,12},{12,11},{1,2},{2,1},{5,6},{6,5},{9... | collective-permute-start | bytes 3145736 | tf_op jit(solution)/shard_map/ppermute | solution.py:365
  89.1 0.1 collective-permute-start.9
  89.1 13.3 %collective-permute-done.10.refs_0_ = f32[128,16,128]{2,1,0:T(8,128)S(1)} collective-permute-done((f32[128,16,128]{2,1,0:T(8,128)S(1)}, f32[128,16,128]{2,1,0:T(8,128)S(1)}, u32[]{:S(2)}, u32[]{:S(2)}) %collective-permute-start.10) | collective-permute-done | bytes 1048608 | tf_op jit(solution)/shard_map/ppermute | solution.py:365
  102.4 0.0 collective-permute-done.9.near
  102.4 2.4 %forward_part.3.refs_0_ = f32[6192,128]{1,0:T(8,128)S(1)} custom-call(f32[128,16,128]{2,1,0:T(8,128)S(1)} %multiply_multiply_fusion.own, f32[128,16,128]{2,1,0:T(8,128)S(1)} %collective-permute-done.9.near, f32[128,16,128]{2,1,0:T(8,128)S(1)} %collective-permute-done.10.refs_0_, bf16[48,256]{1,0:T(8,128)(2,1)S(1)} %get-tuple-element.26.refs_2_.refs_1_, ...), custom_call_target="tpu_custom_call" | custom-call | tf_op jit(solution)/shard_map/forward_part/pallas_call | solution.py:235
  104.8 2.0 %quotient_part.3.field = f32[6272,128]{1,0:T(8,128)S(1)} custom-call(f32[6192,128]{1,0:T(8,128)S(1)} %forward_part.3.refs_0_, f32[48,128,128]{2,1,0:T(8,128)S(1)} %bitcast.11, bf16[3,128,384]{2,1,0:T(8,128)(2,1)S(1)} %get-tuple-element.28.refs_2_, bf16[3,128,384]{2,1,0:T(8,128)(2,1)S(1)} %get-tuple-element.29.refs_3_), custom_call_target="tpu_custom_call" | custom-call | tf_op jit(solution)/shard_map/quotient_part/pallas_call | solution.py:289
  106.8 2.1 %backward_part.3 = (f32[128,16,128]{2,1,0:T(8,128)S(1)}, f32[128,16,128]{2,1,0:T(8,128)S(1)}, f32[128,16,128]{2,1,0:T(8,128)S(1)}) custom-call(f32[6272,128]{1,0:T(8,128)S(1)} %quotient_part.3.field, f32[48,256]{1,0:T(8,128)S(1)} %get-tuple-element.30.axial, f32[8,256]{1,0:T(8,128)S(1)} %add.27.sums, bf16[3,256,256]{2,1,0:T(8,128)(2,1)S(1)} %get-tuple-element.32.lateral), custom_call_target="tpu_custom_call" | custom-call | tf_op jit(solution)/shard_map/backward_part/pallas_call | solution.py:347
  108.9 0.1 collective-permute-start.11
  109.0 2.8 %collective-permute-start.12 = (f32[128,16,128]{2,1,0:T(8,128)S(1)}, f32[128,16,128]{2,1,0:T(8,128)S(1)}, u32[]{:S(2)}, u32[]{:S(2)}) collective-permute-start(f32[128,16,128]{2,1,0:T(8,128)S(1)} %get-tuple-element.38), channel_id=1, source_target_pairs={{3,4},{4,3},{7,8},{8,7},{11,12},{12,11},{1,2},{2,1},{5,6},{6,5},{9... | collective-permute-start | bytes 3145736 | tf_op jit(solution)/shard_map/ppermute | solution.py:365
  111.8 0.0 collective-permute-done.11
  111.8 24.6 %collective-permute-done.12 = f32[128,16,128]{2,1,0:T(8,128)S(1)} collective-permute-done((f32[128,16,128]{2,1,0:T(8,128)S(1)}, f32[128,16,128]{2,1,0:T(8,128)S(1)}, u32[]{:S(2)}, u32[]{:S(2)}) %collective-permute-start.12) | collective-permute-done | bytes 1048608 | tf_op jit(solution)/shard_map/ppermute | solution.py:365
  136.3 0.3 multiply_bitcast_fusion
  136.6 1.3 copy.7
  (8 shorter events, 0.0 us)
Async XLA Ops:
  1.8 35.9 %collective-permute-start.1 = (f32[128,16,128]{2,1,0:T(8,128)S(1)}, f32[128,16,128]{2,1,0:T(8,128)S(1)}, u32[]{:S(2)}, u32[]{:S(2)}) collective-permute-start(f32[128,16,128]{2,1,0:T(8,128)S(1)} %bitcast.12), channel_id=1, source_target_pairs={{3,4},{4,3},{7,8},{8,7},{11,12},{12,11},{19,20},{20,19},{23,24},{2... | collective-permute-start | bytes 3145736 | tf_op jit(solution)/shard_map/ppermute | solution.py:365
  2.6 35.1 %collective-permute-start = (f32[128,16,128]{2,1,0:T(8,128)S(1)}, f32[128,16,128]{2,1,0:T(8,128)S(1)}, u32[]{:S(2)}, u32[]{:S(2)}) collective-permute-start(f32[128,16,128]{2,1,0:T(8,128)S(1)} %bitcast.13), channel_id=1, source_target_pairs={{0,1},{1,0},{2,3},{3,2},{4,5},{5,4},{6,7},{7,6},{8,9},{9,8},{10,11... | collective-permute-start | bytes 3145736 | tf_op jit(solution)/shard_map/ppermute | solution.py:365
  5.3 0.7 copy-start.4
  6.0 0.7 copy-start.5
  6.7 0.7 copy-start.6
  8.2 1.9 %copy-start = (f32[3,16,128,128]{3,2,1,0:T(8,128)S(1)}, f32[3,16,128,128]{3,2,1,0:T(8,128)}, u32[]{:S(2)}) copy-start(f32[3,16,128,128]{3,2,1,0:T(8,128)} %param.5) | copy-start | bytes 9437188
  10.1 1.2 copy-start.2
  12.4 25.3 %collective-permute-start.2 = (f32[128,16,128]{2,1,0:T(8,128)S(1)}, f32[128,16,128]{2,1,0:T(8,128)S(1)}, u32[]{:S(2)}, u32[]{:S(2)}) collective-permute-start(f32[128,16,128]{2,1,0:T(8,128)S(1)} %bitcast.14), channel_id=1, source_target_pairs={{1,2},{2,1},{5,6},{6,5},{9,10},{10,9},{13,14},{14,13},{17,18},{18,... | collective-permute-start | bytes 3145736 | tf_op jit(solution)/shard_map/ppermute | solution.py:365
  16.3 13.3 %collective-permute-start.3 = (f32[8,256]{1,0:T(8,128)S(1)}, f32[8,256]{1,0:T(8,128)S(1)}, u32[]{:S(2)}, u32[]{:S(2)}) collective-permute-start(f32[8,256]{1,0:T(8,128)S(1)} %totals.1), channel_id=1, source_target_pairs={{0,2},{1,3},{2,0},{3,1},{4,6},{5,7},{6,4},{7,5},{8,10},{9,11},{10,... | collective-permute-start | bytes 24584 | tf_op jit(solution)/shard_map/ppermute | solution.py:183
  29.6 2.2 %collective-permute-start.4 = (f32[8,256]{1,0:T(8,128)S(1)}, f32[8,256]{1,0:T(8,128)S(1)}, u32[]{:S(2)}, u32[]{:S(2)}) collective-permute-start(f32[8,256]{1,0:T(8,128)S(1)} %add.24), channel_id=1, source_target_pairs={{0,1},{1,0},{2,3},{3,2},{4,5},{5,4},{6,7},{7,6},{8,9},{9,8},{10,11... | collective-permute-start | bytes 24584 | tf_op jit(solution)/shard_map/ppermute | solution.py:183
  31.8 2.5 %collective-permute-start.5 = (f32[8,256]{1,0:T(8,128)S(1)}, f32[8,256]{1,0:T(8,128)S(1)}, u32[]{:S(2)}, u32[]{:S(2)}) collective-permute-start(f32[8,256]{1,0:T(8,128)S(1)} %add.25), channel_id=1, source_target_pairs={{0,4},{1,5},{2,6},{3,7},{4,0},{5,1},{6,2},{7,3},{8,12},{9,13},{10,... | collective-permute-start | bytes 24584 | tf_op jit(solution)/shard_map/ppermute | solution.py:183
  34.3 3.4 %collective-permute-start.6 = (f32[8,256]{1,0:T(8,128)S(1)}, f32[8,256]{1,0:T(8,128)S(1)}, u32[]{:S(2)}, u32[]{:S(2)}) collective-permute-start(f32[8,256]{1,0:T(8,128)S(1)} %add.26), channel_id=1, source_target_pairs={{0,8},{1,9},{2,10},{3,11},{4,12},{5,13},{6,14},{7,15},{8,0},{9,1},... | collective-permute-start | bytes 24584 | tf_op jit(solution)/shard_map/ppermute | solution.py:183
  37.7 2.5 %copy-start.1 = (f32[3,16,128,128]{3,2,1,0:T(8,128)S(1)}, f32[3,16,128,128]{3,2,1,0:T(8,128)}, u32[]{:S(2)}) copy-start(f32[3,16,128,128]{3,2,1,0:T(8,128)} %param.5) | copy-start | bytes 9437188
  42.2 43.4 %copy-start.3 = (f32[16,128,128]{2,1,0:T(8,128)S(1)}, f32[16,128,128]{2,1,0:T(8,128)}, u32[]{:S(2)}) copy-start(f32[16,128,128]{2,1,0:T(8,128)} %initial.1) | copy-start | bytes 3145732
  44.3 5.5 %collective-permute-start.7 = (f32[128,16,128]{2,1,0:T(8,128)S(1)}, f32[128,16,128]{2,1,0:T(8,128)S(1)}, u32[]{:S(2)}, u32[]{:S(2)}) collective-permute-start(f32[128,16,128]{2,1,0:T(8,128)S(1)} %get-tuple-element.34), channel_id=1, source_target_pairs={{0,1},{1,0},{2,3},{3,2},{4,5},{5,4},{6,7},{7,6},{8,9},{9,8},{10,11... | collective-permute-start | bytes 3145736 | tf_op jit(solution)/shard_map/ppermute | solution.py:365
  47.0 38.6 %collective-permute-start.8 = (f32[128,16,128]{2,1,0:T(8,128)S(1)}, f32[128,16,128]{2,1,0:T(8,128)S(1)}, u32[]{:S(2)}, u32[]{:S(2)}) collective-permute-start(f32[128,16,128]{2,1,0:T(8,128)S(1)} %get-tuple-element.35), channel_id=1, source_target_pairs={{3,4},{4,3},{7,8},{8,7},{11,12},{12,11},{1,2},{2,1},{5,6},{6,5},{9... | collective-permute-start | bytes 3145736 | tf_op jit(solution)/shard_map/ppermute | solution.py:365
  86.3 16.1 %collective-permute-start.10 = (f32[128,16,128]{2,1,0:T(8,128)S(1)}, f32[128,16,128]{2,1,0:T(8,128)S(1)}, u32[]{:S(2)}, u32[]{:S(2)}) collective-permute-start(f32[128,16,128]{2,1,0:T(8,128)S(1)} %multiply_multiply_fusion.own), channel_id=1, source_target_pairs={{3,4},{4,3},{7,8},{8,7},{11,12},{12,11},{1,2},{2,1},{5,6},{6,5},{9... | collective-permute-start | bytes 3145736 | tf_op jit(solution)/shard_map/ppermute | solution.py:365
  89.1 13.3 %collective-permute-start.9 = (f32[128,16,128]{2,1,0:T(8,128)S(1)}, f32[128,16,128]{2,1,0:T(8,128)S(1)}, u32[]{:S(2)}, u32[]{:S(2)}) collective-permute-start(f32[128,16,128]{2,1,0:T(8,128)S(1)} %multiply_multiply_fusion.own), channel_id=1, source_target_pairs={{0,1},{1,0},{2,3},{3,2},{4,5},{5,4},{6,7},{7,6},{8,9},{9,8},{10,11... | collective-permute-start | bytes 3145736 | tf_op jit(solution)/shard_map/ppermute | solution.py:365
  108.9 2.8 %collective-permute-start.11 = (f32[128,16,128]{2,1,0:T(8,128)S(1)}, f32[128,16,128]{2,1,0:T(8,128)S(1)}, u32[]{:S(2)}, u32[]{:S(2)}) collective-permute-start(f32[128,16,128]{2,1,0:T(8,128)S(1)} %get-tuple-element.37), channel_id=1, source_target_pairs={{0,1},{1,0},{2,3},{3,2},{4,5},{5,4},{6,7},{7,6},{8,9},{9,8},{10,11... | collective-permute-start | bytes 3145736 | tf_op jit(solution)/shard_map/ppermute | solution.py:365
  109.0 27.4 %collective-permute-start.12 = (f32[128,16,128]{2,1,0:T(8,128)S(1)}, f32[128,16,128]{2,1,0:T(8,128)S(1)}, u32[]{:S(2)}, u32[]{:S(2)}) collective-permute-start(f32[128,16,128]{2,1,0:T(8,128)S(1)} %get-tuple-element.38), channel_id=1, source_target_pairs={{3,4},{4,3},{7,8},{8,7},{11,12},{12,11},{1,2},{2,1},{5,6},{6,5},{9... | collective-permute-start | bytes 3145736 | tf_op jit(solution)/shard_map/ppermute | solution.py:365

commit v3 on v2

--- a/solution.py
+++ b/solution.py
@@ -39,10 +39,23 @@
     return values / jnp.sum(values, axis=1, keepdims=True)
 
 
-def matrices_kernel(
-    position, taps_x, taps_y, taps_z, fwd_x, bwd_x, fwd_y, bwd_y, fwd_z, bwd_z, sums_x, sums_y, sums_z, *, count
+def prepare_kernel(
+    position, taken_x, taken_y, taken_z, initial_in, recorded_in,
+    fwd_x, bwd_x, fwd_y, bwd_y, fwd_z, bwd_z, recorded, out,
+    taps_x, taps_y, taps_z, initial, sems, *, count,
 ):
     view_count, tap_count = taps_x.shape
+    block_len = initial.shape[0]
+    pairs = [(taken_x, taps_x), (taken_y, taps_y), (taken_z, taps_z), (initial_in, initial)]
+    for view in range(view_count):
+        part = pl.ds(view * block_len, block_len)
+        pairs.append((recorded_in.at[part], recorded.at[part]))
+    copies = [pltpu.make_async_copy(*pair, sems.at[i]) for i, pair in enumerate(pairs)]
+    for copy in copies:
+        copy.start()
+    for copy in copies[:3]:
+        copy.wait()
+    sums_x, sums_y, sums_z = [], [], []
     size = fwd_x.shape[1]
     rows = lax.broadcasted_iota(jnp.int32, (size, size), 0)
     cols = lax.broadcasted_iota(jnp.int32, (size, size), 1)
@@ -60,15 +73,14 @@
             if is_x:
                 fwd_x[view] = jnp.concatenate([high, high, low], axis=1)
                 bwd_x[view] = jnp.concatenate([high_t, high_t, low_t], axis=1)
-                sums_x[view : view + 1, :] = total
+                sums_x.append(total)
             else:
                 one = jnp.concatenate([high_t, low_t], axis=1)
                 fwd_y[view] = jnp.concatenate([one, one], axis=0)
                 one = jnp.concatenate([high, low], axis=1)
                 bwd_y[view] = jnp.concatenate([one, one], axis=0)
-                sums_y[view : view + 1, :] = total
-
-    block_len = sums_z.shape[1]
+                sums_y.append(total)
+
     planes = view_count * block_len
     reach = taps_z.shape[1] // 2
     place = position[0]
@@ -82,7 +94,7 @@
     for view in range(view_count):
         line = jnp.broadcast_to(values[view : view + 1, :], (block_len, size))
         total = jnp.sum(jnp.where(kept, line, 0.0), axis=1, keepdims=True)
-        sums_z[view] = jnp.broadcast_to(total, (block_len, size))
+        sums_z.append(jnp.broadcast_to(total, (block_len, size)))
 
         def moved(ahead):
             return pltpu.roll(line, (-ahead) % size, 1, stride=1, stride_axis=0)
@@ -105,73 +117,65 @@
     matrix = square.T[:planes]
     bwd_z[...] = spread(matrix, matrix, matrix)
 
-
-def matrices(kernel_x, kernel_y, kernel_z, size, block_len, axis):
+    copies[3].wait()
+    flats = [jnp.zeros((size, LANES), F32) for _ in range(view_count)]
+    for z in range(block_len):
+        plane = initial[z]
+        flats = [flat + plane * sums_z[view][z : z + 1, :] for view, flat in enumerate(flats)]
+    lanes = lax.broadcasted_iota(jnp.int32, out.shape, 1)
+    view_of = (lanes % planes) // block_len
+    row_of = lax.broadcasted_iota(jnp.int32, out.shape, 0)
+    result = jnp.zeros(out.shape, F32)
+    for view in range(view_count):
+        along_x = jnp.broadcast_to(sums_x[view], (8, size))
+        weighted = jnp.dot(along_x, flats[view], precision=PRECISE, preferred_element_type=F32)
+        blur_total = jnp.sum(weighted[:1] * sums_y[view])
+        copies[4 + view].wait()
+
+        def add(z, total):
+            return total + jnp.sum(recorded[view * block_len + z].reshape(-1, 8, LANES), axis=0)
+
+        data_total = jnp.sum(lax.fori_loop(0, block_len, add, jnp.zeros((8, LANES), F32), unroll=4))
+        value = jnp.where(row_of == 0, data_total, blur_total)
+        result = jnp.where(view_of == view, value, result)
+    out[...] = result
+
+
+def prepare(kernel_x, kernel_y, kernel_z, initial, recorded, axis):
     view_count, tap_count = kernel_x.shape
+    block_len, size, size_y = initial.shape
     planes = view_count * block_len
-    assert size == LANES and tap_count <= size and kernel_y.shape == kernel_x.shape
+    assert size == size_y == LANES and tap_count <= size and kernel_y.shape == kernel_x.shape
     assert view_count == 3 and 3 * block_len + kernel_z.shape[1] <= size
-    vmem = pl.BlockSpec(memory_space=pltpu.VMEM)
+    anywhere = pl.BlockSpec(memory_space=pltpu.HBM)
     out = jax.ShapeDtypeStruct
     return pl.pallas_call(
-        functools.partial(matrices_kernel, count=lax.axis_size(axis)),
-        in_specs=[pl.BlockSpec(memory_space=pltpu.SMEM), vmem, vmem, vmem],
+        functools.partial(prepare_kernel, count=lax.axis_size(axis)),
+        in_specs=[pl.BlockSpec(memory_space=pltpu.SMEM)] + [anywhere] * 5,
         out_shape=(
             out((view_count, size, 3 * size), BF16),
             out((view_count, size, 3 * size), BF16),
-            out((view_count, 2 * size, 2 * size), BF16),
+            pltpu.VMEM((view_count, 2 * size, 2 * size), BF16),
             out((view_count, 2 * size, 2 * size), BF16),
             out((planes, 2 * size), BF16),
             out((planes, 2 * size), F32),
-            out((view_count, size), F32),
-            out((view_count, size), F32),
-            out((view_count, block_len, size), F32),
+            pltpu.VMEM(recorded.shape, F32),
+            out((8, 2 * LANES), F32),
         ),
+        scratch_shapes=[
+            *(pltpu.VMEM(taps.shape, F32) for taps in (kernel_x, kernel_y, kernel_z)),
+            pltpu.VMEM(initial.shape, F32),
+            pltpu.SemaphoreType.DMA((4 + view_count,)),
+        ],
         compiler_params=pltpu.CompilerParams(vmem_limit_bytes=VMEM_LIMIT),
-        name="matrices",
-    )(lax.axis_index(axis).astype(jnp.int32).reshape(1), kernel_x, kernel_y, kernel_z)
-
-
-def totals_kernel(recorded, initial, sums_x, sums_y, sums_z, out, *, block_len):
-    view_count = sums_x.shape[0]
-    shape = out.shape
-    lanes = lax.broadcasted_iota(jnp.int32, shape, 1)
-    view_of = (lanes % (view_count * block_len)) // block_len
-    row_of = lax.broadcasted_iota(jnp.int32, shape, 0)
-    size_x = initial.shape[1]
-    flats = [jnp.zeros((size_x, LANES), F32) for _ in range(view_count)]
-    for z in range(block_len):
-        plane = initial[z]
-        flats = [flat + plane * sums_z[view, z : z + 1, :] for view, flat in enumerate(flats)]
-    weighted = jnp.concatenate(
-        [
-            jnp.dot(sums_x[...], flat, precision=PRECISE, preferred_element_type=F32)[view : view + 1]
-            for view, flat in enumerate(flats)
-        ],
-        axis=0,
+        name="prepare",
+    )(
+        lax.axis_index(axis).astype(jnp.int32).reshape(1),
+        *(
+            pltpu.with_memory_space_constraint(value, pltpu.HBM)
+            for value in (kernel_x, kernel_y, kernel_z, initial, recorded)
+        ),
     )
-    weighted = weighted * sums_y[...]
-    result = jnp.zeros(shape, F32)
-    for view in range(view_count):
-
-        def add(z, total):
-            return total + jnp.sum(recorded[view * block_len + z].reshape(-1, 8, LANES), axis=0)
-
-        data = lax.fori_loop(0, block_len, add, jnp.zeros((8, LANES), F32), unroll=4)
-        blur_total = jnp.sum(weighted[view : view + 1, :])
-        data_total = jnp.sum(data)
-        value = jnp.where(row_of == 0, data_total, blur_total)
-        result = jnp.where(view_of == view, value, result)
-    out[...] = result
-
-
-def totals(recorded, initial, sums_x, sums_y, sums_z):
-    return pl.pallas_call(
-        functools.partial(totals_kernel, block_len=initial.shape[0]),
-        out_shape=jax.ShapeDtypeStruct((8, 2 * LANES), F32),
-        compiler_params=pltpu.CompilerParams(vmem_limit_bytes=VMEM_LIMIT),
-        name="totals",
-    )(*in_vmem(recorded), initial, sums_x, sums_y, sums_z)
 
 
 def summed(value, axis):
@@ -368,10 +372,9 @@
     planes = recorded.reshape(view_count * block_len, size_x, size_y)
     fars = [swap(estimate, first_pairs)]
     near = swap(estimate, near_pairs)
-    fwd_x, bwd_x, fwd_y, bwd_y, fwd_z, bwd_z, sums_x, sums_y, sums_z = matrices(
-        kernel_x, kernel_y, kernel_z, size_x, block_len, "slab"
+    fwd_x, bwd_x, fwd_y, bwd_y, fwd_z, bwd_z, planes, sums = prepare(
+        kernel_x, kernel_y, kernel_z, initial, planes, "slab"
     )
-    sums = totals(planes, initial, sums_x, sums_y, sums_z)
     delayed, sums = lax.optimization_barrier((estimate, sums))
     sums = summed(sums, "slab")
     fars.append(swap(delayed, second_pairs))

time: 138 us -> 138 us (level)
  local copies, waits for them, and re-layouts: 8.29 us -> 3.13 us
  waiting for transfers between devices: 91.3 us -> 95.3 us
    unnamed x15 -> x3, local copies, waits for them, and re-layouts: 7 us -> 1.84 us
    ppermute x4, waiting for transfers between devices: 17.7 us -> 21.6 us  [summed(): lax.ppermute(value, axis, [(i, i ^ step) for i in range(count)])]
    pallas_call x2 -> x1, Pallas kernels: 1.91 us -> 3.13 us  [prepare(): pl.pallas_call(functools.partial(prepare_kernel, count=lax.axis_size(axis...]
  transfers between devices with their start and end apart: 13 -> 13, of which waited for: 7 -> 7; matrix products, arithmetic and copies ran while one was open for 0% -> 0% of each run, Pallas kernels for 1% -> 2%
where the time goes in v3:
time: 138 us
  waiting for transfers between devices  95.3 us (69%)
  starting transfers between devices  22.1 us (16%)
  Pallas kernels  16 us (12%)
  local copies, waits for them, and re-layouts  3.13 us (2%)
    ppermute x9, waiting for transfers between devices, swap(): return lax.ppermute(value, 'slab', pairs)  73.7 us
    ppermute x4, waiting for transfers between devices, summed(): lax.ppermute(value, axis, [(i, i ^ step) for i in range(count)])  21.6 us
    ppermute x9, starting transfers between devices, swap(): return lax.ppermute(value, 'slab', pairs)  18.4 us
    pallas_call x2, Pallas kernels, forward_part(): pl.pallas_call(functools.partial(forward_kernel, block_len=block_len), ou...  4.82 us
    pallas_call x2, Pallas kernels, backward_part(): pl.pallas_call(functools.partial(backward_kernel, block_len=block_len, of...  4.21 us
    pallas_call x2, Pallas kernels, quotient_part(): pl.pallas_call(functools.partial(quotient_kernel, chunks=len(parts), bloc...  3.81 us
    ppermute x4, starting transfers between devices, summed(): lax.ppermute(value, axis, [(i, i ^ step) for i in range(count)])  3.72 us
    pallas_call x1, Pallas kernels, prepare(): pl.pallas_call(functools.partial(prepare_kernel, count=lax.axis_size(axis...  3.13 us
  transfers between devices with their start and end apart: 13, of which 7 were waited for; matrix products, arithmetic and copies ran while one was open for 0% of the time, Pallas kernels for 2%

profile of v3, /device:TPU:11, one launch (start us, length us, event | category | flops | bytes accessed | tf_op | source)
XLA Modules:
  0.0 137.7 jit_solution(16521283785739872800)
XLA Ops:
  0.0 1.8 %copy.11 = f32[16,128,128]{2,0,1:T(8,128)S(1)} copy(f32[16,128,128]{2,1,0:T(8,128)} %initial_in.1) | data formatting | bytes 2097152 | tf_op args[1]
  1.8 0.7 collective-permute-start.1
  2.6 2.8 %collective-permute-start = (f32[128,16,128]{2,1,0:T(8,128)S(1)}, f32[128,16,128]{2,1,0:T(8,128)S(1)}, u32[]{:S(2)}, u32[]{:S(2)}) collective-permute-start(f32[128,16,128]{2,1,0:T(8,128)S(1)} %bitcast.10), channel_id=1, source_target_pairs={{0,1},{1,0},{2,3},{3,2},{4,5},{5,4},{6,7},{7,6},{8,9},{9,8},{10,11... | collective-permute-start | bytes 3145736 | tf_op jit(solution)/shard_map/ppermute | solution.py:369
  5.3 3.1 %prepare.1 = (bf16[3,128,384]{2,1,0:T(8,128)(2,1)S(1)}, bf16[3,128,384]{2,1,0:T(8,128)(2,1)S(1)}, bf16[3,256,256]{2,1,0:T(8,128)(2,1)S(1)}, bf16[3,256,256]{2,1,...) custom-call(s32[1]{0:T(128)} %bitcast.1.position, ...), custom_call_target="tpu_custom_call" | custom-call | tf_op jit(solution)/shard_map/prepare/pallas_call | solution.py:152
  8.5 3.8 %collective-permute-start.2 = (f32[128,16,128]{2,1,0:T(8,128)S(1)}, f32[128,16,128]{2,1,0:T(8,128)S(1)}, u32[]{:S(2)}, u32[]{:S(2)}) collective-permute-start(f32[128,16,128]{2,1,0:T(8,128)S(1)} %bitcast.11), channel_id=1, source_target_pairs={{1,2},{2,1},{5,6},{6,5},{9,10},{10,9},{13,14},{14,13},{17,18},{18,... | collective-permute-start | bytes 3145736 | tf_op jit(solution)/shard_map/ppermute | solution.py:369
  12.3 0.1 collective-permute-start.3
  12.4 17.2 %collective-permute-done.3 = f32[8,256]{1,0:T(8,128)S(1)} collective-permute-done((f32[8,256]{1,0:T(8,128)S(1)}, f32[8,256]{1,0:T(8,128)S(1)}, u32[]{:S(2)}, u32[]{:S(2)}) %collective-permute-start.3) | collective-permute-done | bytes 8224 | tf_op jit(solution)/shard_map/ppermute | solution.py:187
  29.6 1.3 collective-permute-start.4
  30.9 0.8 collective-permute-done.4
  31.8 0.0 collective-permute-start.5
  31.8 2.5 %collective-permute-done.5 = f32[8,256]{1,0:T(8,128)S(1)} collective-permute-done((f32[8,256]{1,0:T(8,128)S(1)}, f32[8,256]{1,0:T(8,128)S(1)}, u32[]{:S(2)}, u32[]{:S(2)}) %collective-permute-start.5) | collective-permute-done | bytes 8224 | tf_op jit(solution)/shard_map/ppermute | solution.py:187
  34.3 2.3 %collective-permute-start.6 = (f32[8,256]{1,0:T(8,128)S(1)}, f32[8,256]{1,0:T(8,128)S(1)}, u32[]{:S(2)}, u32[]{:S(2)}) collective-permute-start(f32[8,256]{1,0:T(8,128)S(1)} %add.26), channel_id=1, source_target_pairs={{0,8},{1,9},{2,10},{3,11},{4,12},{5,13},{6,14},{7,15},{8,0},{9,1},... | collective-permute-start | bytes 24584 | tf_op jit(solution)/shard_map/ppermute | solution.py:187
  36.6 1.1 collective-permute-done.6
  37.7 0.0 collective-permute-done.1.refs_0_
  37.7 0.0 collective-permute-done.near
  37.7 0.0 collective-permute-done.2.refs_1_
  37.7 2.4 %forward_part.2.refs_0_ = f32[6192,128]{1,0:T(8,128)S(1)} custom-call(f32[128,16,128]{2,1,0:T(8,128)S(1)} %bitcast.12, f32[128,16,128]{2,1,0:T(8,128)S(1)} %collective-permute-done.near, f32[128,16,128]{2,1,0:T(8,128)S(1)} %collective-permute-done.1.refs_0_, f32[128,16,128]{2,1,0:T(8,128)S(1)} %collective-permute-done.2.refs_1_, ...), custom_call_target="tpu_custom_call" | custom-call | tf_op jit(solution)/shard_map/forward_part/pallas_call | solution.py:239
  40.1 1.9 %quotient_part.2.field = f32[6272,128]{1,0:T(8,128)S(1)} custom-call(f32[6192,128]{1,0:T(8,128)S(1)} %forward_part.2.refs_0_, f32[48,128,128]{2,1,0:T(8,128)S(1)} %get-tuple-element.25.refs_1_, bf16[3,128,384]{2,1,0:T(8,128)(2,1)S(1)} %get-tuple-element.26.refs_2_, bf16[3,128,384]{2,1,0:T(8,128)(2,1)S(1)} %get-tuple-element.27.refs_3_), custom_call_target="tpu_custom_call" | custom-call | tf_op jit(solution)/shard_map/quotient_part/pallas_call | solution.py:293
  42.1 0.0 copy-start
  42.1 2.1 %backward_part.2 = (f32[128,16,128]{2,1,0:T(8,128)S(1)}, f32[128,16,128]{2,1,0:T(8,128)S(1)}, f32[128,16,128]{2,1,0:T(8,128)S(1)}) custom-call(f32[6272,128]{1,0:T(8,128)S(1)} %quotient_part.2.field, f32[48,256]{1,0:T(8,128)S(1)} %get-tuple-element.28.axial, f32[8,256]{1,0:T(8,128)S(1)} %add.27.sums, bf16[3,256,256]{2,1,0:T(8,128)(2,1)S(1)} %get-tuple-element.30.lateral), custom_call_target="tpu_custom_call" | custom-call | tf_op jit(solution)/shard_map/backward_part/pallas_call | solution.py:351
  44.2 2.7 %collective-permute-start.7 = (f32[128,16,128]{2,1,0:T(8,128)S(1)}, f32[128,16,128]{2,1,0:T(8,128)S(1)}, u32[]{:S(2)}, u32[]{:S(2)}) collective-permute-start(f32[128,16,128]{2,1,0:T(8,128)S(1)} %get-tuple-element.32), channel_id=1, source_target_pairs={{0,1},{1,0},{2,3},{3,2},{4,5},{5,4},{6,7},{7,6},{8,9},{9,8},{10,11... | collective-permute-start | bytes 3145736 | tf_op jit(solution)/shard_map/ppermute | solution.py:369
  46.9 2.7 %collective-permute-start.8 = (f32[128,16,128]{2,1,0:T(8,128)S(1)}, f32[128,16,128]{2,1,0:T(8,128)S(1)}, u32[]{:S(2)}, u32[]{:S(2)}) collective-permute-start(f32[128,16,128]{2,1,0:T(8,128)S(1)} %get-tuple-element.33), channel_id=1, source_target_pairs={{3,4},{4,3},{7,8},{8,7},{11,12},{12,11},{1,2},{2,1},{5,6},{6,5},{9... | collective-permute-start | bytes 3145736 | tf_op jit(solution)/shard_map/ppermute | solution.py:369
  49.7 0.0 collective-permute-done.7
  49.7 35.8 %collective-permute-done.8 = f32[128,16,128]{2,1,0:T(8,128)S(1)} collective-permute-done((f32[128,16,128]{2,1,0:T(8,128)S(1)}, f32[128,16,128]{2,1,0:T(8,128)S(1)}, u32[]{:S(2)}, u32[]{:S(2)}) %collective-permute-start.8) | collective-permute-done | bytes 1048608 | tf_op jit(solution)/shard_map/ppermute | solution.py:369
  85.5 0.0 copy-done
  85.5 0.7 multiply_multiply_fusion.own
  86.2 2.8 %collective-permute-start.10 = (f32[128,16,128]{2,1,0:T(8,128)S(1)}, f32[128,16,128]{2,1,0:T(8,128)S(1)}, u32[]{:S(2)}, u32[]{:S(2)}) collective-permute-start(f32[128,16,128]{2,1,0:T(8,128)S(1)} %multiply_multiply_fusion.own), channel_id=1, source_target_pairs={{3,4},{4,3},{7,8},{8,7},{11,12},{12,11},{1,2},{2,1},{5,6},{6,5},{9... | collective-permute-start | bytes 3145736 | tf_op jit(solution)/shard_map/ppermute | solution.py:369
  89.0 0.1 collective-permute-start.9
  89.1 13.3 %collective-permute-done.10.refs_0_ = f32[128,16,128]{2,1,0:T(8,128)S(1)} collective-permute-done((f32[128,16,128]{2,1,0:T(8,128)S(1)}, f32[128,16,128]{2,1,0:T(8,128)S(1)}, u32[]{:S(2)}, u32[]{:S(2)}) %collective-permute-start.10) | collective-permute-done | bytes 1048608 | tf_op jit(solution)/shard_map/ppermute | solution.py:369
  102.4 0.0 collective-permute-done.9.near
  102.4 2.4 %forward_part.3.refs_0_ = f32[6192,128]{1,0:T(8,128)S(1)} custom-call(f32[128,16,128]{2,1,0:T(8,128)S(1)} %multiply_multiply_fusion.own, f32[128,16,128]{2,1,0:T(8,128)S(1)} %collective-permute-done.9.near, f32[128,16,128]{2,1,0:T(8,128)S(1)} %collective-permute-done.10.refs_0_, bf16[48,256]{1,0:T(8,128)(2,1)S(1)} %get-tuple-element.23.refs_2_.refs_1_, ...), custom_call_target="tpu_custom_call" | custom-call | tf_op jit(solution)/shard_map/forward_part/pallas_call | solution.py:239
  104.8 1.9 %quotient_part.3.field = f32[6272,128]{1,0:T(8,128)S(1)} custom-call(f32[6192,128]{1,0:T(8,128)S(1)} %forward_part.3.refs_0_, f32[48,128,128]{2,1,0:T(8,128)S(1)} %get-tuple-element.25.refs_1_, bf16[3,128,384]{2,1,0:T(8,128)(2,1)S(1)} %get-tuple-element.26.refs_2_, bf16[3,128,384]{2,1,0:T(8,128)(2,1)S(1)} %get-tuple-element.27.refs_3_), custom_call_target="tpu_custom_call" | custom-call | tf_op jit(solution)/shard_map/quotient_part/pallas_call | solution.py:293
  106.6 2.1 %backward_part.3 = (f32[128,16,128]{2,1,0:T(8,128)S(1)}, f32[128,16,128]{2,1,0:T(8,128)S(1)}, f32[128,16,128]{2,1,0:T(8,128)S(1)}) custom-call(f32[6272,128]{1,0:T(8,128)S(1)} %quotient_part.3.field, f32[48,256]{1,0:T(8,128)S(1)} %get-tuple-element.28.axial, f32[8,256]{1,0:T(8,128)S(1)} %add.27.sums, bf16[3,256,256]{2,1,0:T(8,128)(2,1)S(1)} %get-tuple-element.30.lateral), custom_call_target="tpu_custom_call" | custom-call | tf_op jit(solution)/shard_map/backward_part/pallas_call | solution.py:351
  108.7 0.1 collective-permute-start.11
  108.8 2.8 %collective-permute-start.12 = (f32[128,16,128]{2,1,0:T(8,128)S(1)}, f32[128,16,128]{2,1,0:T(8,128)S(1)}, u32[]{:S(2)}, u32[]{:S(2)}) collective-permute-start(f32[128,16,128]{2,1,0:T(8,128)S(1)} %get-tuple-element.36), channel_id=1, source_target_pairs={{3,4},{4,3},{7,8},{8,7},{11,12},{12,11},{1,2},{2,1},{5,6},{6,5},{9... | collective-permute-start | bytes 3145736 | tf_op jit(solution)/shard_map/ppermute | solution.py:369
  111.6 0.0 collective-permute-done.11
  111.6 24.6 %collective-permute-done.12 = f32[128,16,128]{2,1,0:T(8,128)S(1)} collective-permute-done((f32[128,16,128]{2,1,0:T(8,128)S(1)}, f32[128,16,128]{2,1,0:T(8,128)S(1)}, u32[]{:S(2)}, u32[]{:S(2)}) %collective-permute-start.12) | collective-permute-done | bytes 1048608 | tf_op jit(solution)/shard_map/ppermute | solution.py:369
  136.2 0.3 multiply_bitcast_fusion
  136.4 1.3 copy.7
  (4 shorter events, 0.0 us)
Async XLA Ops:
  1.8 35.9 %collective-permute-start.1 = (f32[128,16,128]{2,1,0:T(8,128)S(1)}, f32[128,16,128]{2,1,0:T(8,128)S(1)}, u32[]{:S(2)}, u32[]{:S(2)}) collective-permute-start(f32[128,16,128]{2,1,0:T(8,128)S(1)} %bitcast.9), channel_id=1, source_target_pairs={{3,4},{4,3},{7,8},{8,7},{11,12},{12,11},{19,20},{20,19},{23,24},{2... | collective-permute-start | bytes 3145736 | tf_op jit(solution)/shard_map/ppermute | solution.py:369
  2.6 35.1 %collective-permute-start = (f32[128,16,128]{2,1,0:T(8,128)S(1)}, f32[128,16,128]{2,1,0:T(8,128)S(1)}, u32[]{:S(2)}, u32[]{:S(2)}) collective-permute-start(f32[128,16,128]{2,1,0:T(8,128)S(1)} %bitcast.10), channel_id=1, source_target_pairs={{0,1},{1,0},{2,3},{3,2},{4,5},{5,4},{6,7},{7,6},{8,9},{9,8},{10,11... | collective-permute-start | bytes 3145736 | tf_op jit(solution)/shard_map/ppermute | solution.py:369
  8.5 29.2 %collective-permute-start.2 = (f32[128,16,128]{2,1,0:T(8,128)S(1)}, f32[128,16,128]{2,1,0:T(8,128)S(1)}, u32[]{:S(2)}, u32[]{:S(2)}) collective-permute-start(f32[128,16,128]{2,1,0:T(8,128)S(1)} %bitcast.11), channel_id=1, source_target_pairs={{1,2},{2,1},{5,6},{6,5},{9,10},{10,9},{13,14},{14,13},{17,18},{18,... | collective-permute-start | bytes 3145736 | tf_op jit(solution)/shard_map/ppermute | solution.py:369
  12.3 17.3 %collective-permute-start.3 = (f32[8,256]{1,0:T(8,128)S(1)}, f32[8,256]{1,0:T(8,128)S(1)}, u32[]{:S(2)}, u32[]{:S(2)}) collective-permute-start(f32[8,256]{1,0:T(8,128)S(1)} %get-tuple-element.29), channel_id=1, source_target_pairs={{0,2},{1,3},{2,0},{3,1},{4,6},{5,7},{6,4},{7,5},{8,10},{9,11},{10,... | collective-permute-start | bytes 24584 | tf_op jit(solution)/shard_map/ppermute | solution.py:187
  29.6 2.2 %collective-permute-start.4 = (f32[8,256]{1,0:T(8,128)S(1)}, f32[8,256]{1,0:T(8,128)S(1)}, u32[]{:S(2)}, u32[]{:S(2)}) collective-permute-start(f32[8,256]{1,0:T(8,128)S(1)} %add.24), channel_id=1, source_target_pairs={{0,1},{1,0},{2,3},{3,2},{4,5},{5,4},{6,7},{7,6},{8,9},{9,8},{10,11... | collective-permute-start | bytes 24584 | tf_op jit(solution)/shard_map/ppermute | solution.py:187
  31.8 2.5 %collective-permute-start.5 = (f32[8,256]{1,0:T(8,128)S(1)}, f32[8,256]{1,0:T(8,128)S(1)}, u32[]{:S(2)}, u32[]{:S(2)}) collective-permute-start(f32[8,256]{1,0:T(8,128)S(1)} %add.25), channel_id=1, source_target_pairs={{0,4},{1,5},{2,6},{3,7},{4,0},{5,1},{6,2},{7,3},{8,12},{9,13},{10,... | collective-permute-start | bytes 24584 | tf_op jit(solution)/shard_map/ppermute | solution.py:187
  34.3 3.4 %collective-permute-start.6 = (f32[8,256]{1,0:T(8,128)S(1)}, f32[8,256]{1,0:T(8,128)S(1)}, u32[]{:S(2)}, u32[]{:S(2)}) collective-permute-start(f32[8,256]{1,0:T(8,128)S(1)} %add.26), channel_id=1, source_target_pairs={{0,8},{1,9},{2,10},{3,11},{4,12},{5,13},{6,14},{7,15},{8,0},{9,1},... | collective-permute-start | bytes 24584 | tf_op jit(solution)/shard_map/ppermute | solution.py:187
  42.1 43.4 %copy-start = (f32[16,128,128]{2,1,0:T(8,128)S(1)}, f32[16,128,128]{2,1,0:T(8,128)}, u32[]{:S(2)}) copy-start(f32[16,128,128]{2,1,0:T(8,128)} %initial_in.1) | copy-start | bytes 3145732
  44.2 5.5 %collective-permute-start.7 = (f32[128,16,128]{2,1,0:T(8,128)S(1)}, f32[128,16,128]{2,1,0:T(8,128)S(1)}, u32[]{:S(2)}, u32[]{:S(2)}) collective-permute-start(f32[128,16,128]{2,1,0:T(8,128)S(1)} %get-tuple-element.32), channel_id=1, source_target_pairs={{0,1},{1,0},{2,3},{3,2},{4,5},{5,4},{6,7},{7,6},{8,9},{9,8},{10,11... | collective-permute-start | bytes 3145736 | tf_op jit(solution)/shard_map/ppermute | solution.py:369
  46.9 38.6 %collective-permute-start.8 = (f32[128,16,128]{2,1,0:T(8,128)S(1)}, f32[128,16,128]{2,1,0:T(8,128)S(1)}, u32[]{:S(2)}, u32[]{:S(2)}) collective-permute-start(f32[128,16,128]{2,1,0:T(8,128)S(1)} %get-tuple-element.33), channel_id=1, source_target_pairs={{3,4},{4,3},{7,8},{8,7},{11,12},{12,11},{1,2},{2,1},{5,6},{6,5},{9... | collective-permute-start | bytes 3145736 | tf_op jit(solution)/shard_map/ppermute | solution.py:369
  86.2 16.1 %collective-permute-start.10 = (f32[128,16,128]{2,1,0:T(8,128)S(1)}, f32[128,16,128]{2,1,0:T(8,128)S(1)}, u32[]{:S(2)}, u32[]{:S(2)}) collective-permute-start(f32[128,16,128]{2,1,0:T(8,128)S(1)} %multiply_multiply_fusion.own), channel_id=1, source_target_pairs={{3,4},{4,3},{7,8},{8,7},{11,12},{12,11},{1,2},{2,1},{5,6},{6,5},{9... | collective-permute-start | bytes 3145736 | tf_op jit(solution)/shard_map/ppermute | solution.py:369
  89.0 13.4 %collective-permute-start.9 = (f32[128,16,128]{2,1,0:T(8,128)S(1)}, f32[128,16,128]{2,1,0:T(8,128)S(1)}, u32[]{:S(2)}, u32[]{:S(2)}) collective-permute-start(f32[128,16,128]{2,1,0:T(8,128)S(1)} %multiply_multiply_fusion.own), channel_id=1, source_target_pairs={{0,1},{1,0},{2,3},{3,2},{4,5},{5,4},{6,7},{7,6},{8,9},{9,8},{10,11... | collective-permute-start | bytes 3145736 | tf_op jit(solution)/shard_map/ppermute | solution.py:369
  108.7 2.8 %collective-permute-start.11 = (f32[128,16,128]{2,1,0:T(8,128)S(1)}, f32[128,16,128]{2,1,0:T(8,128)S(1)}, u32[]{:S(2)}, u32[]{:S(2)}) collective-permute-start(f32[128,16,128]{2,1,0:T(8,128)S(1)} %get-tuple-element.35), channel_id=1, source_target_pairs={{0,1},{1,0},{2,3},{3,2},{4,5},{5,4},{6,7},{7,6},{8,9},{9,8},{10,11... | collective-permute-start | bytes 3145736 | tf_op jit(solution)/shard_map/ppermute | solution.py:369
  108.8 27.4 %collective-permute-start.12 = (f32[128,16,128]{2,1,0:T(8,128)S(1)}, f32[128,16,128]{2,1,0:T(8,128)S(1)}, u32[]{:S(2)}, u32[]{:S(2)}) collective-permute-start(f32[128,16,128]{2,1,0:T(8,128)S(1)} %get-tuple-element.36), channel_id=1, source_target_pairs={{3,4},{4,3},{7,8},{8,7},{11,12},{12,11},{1,2},{2,1},{5,6},{6,5},{9... | collective-permute-start | bytes 3145736 | tf_op jit(solution)/shard_map/ppermute | solution.py:369

commit v4 on v3

--- a/solution.py
+++ b/solution.py
@@ -10,6 +10,7 @@
 
 ITERS = 2
 GROUP = 8
+CHUNKS = 2
 VMEM_LIMIT = 16 << 20
 ROWS = 64
 ALONG_Y = 1
@@ -192,18 +193,34 @@
     return [pltpu.with_memory_space_constraint(value, pltpu.VMEM) for value in values]
 
 
-def forward_kernel(own, near, *refs, block_len):
-    *fars, axial, lateral, out, fields = refs
-    chunk = own.shape[0]
+def forward_kernel(*refs, block_len, turned):
+    if turned:
+        own, near, *fars, axial, lateral, out, fields, planes = refs
+        size_x = own.shape[1]
+    else:
+        *parts, axial, lateral, out, fields = refs
+        count = len(parts) // 3
+        owns, nears, fars = parts[:count], parts[count : 2 * count], parts[2 * count :]
+        chunk = owns[0].shape[0]
+        size_x = chunk * count
     view_count = lateral.shape[0]
     axial_matrix = axial[:, : 3 * view_count * block_len]
-    spread = chunk + 1
-
-    def along_z(index, carry):
+    spread = size_x + 1
+    if turned:
+        for place, group in enumerate(([own], [near], fars)):
+            for z in range(block_len):
+                plane = sum(ref[z] for ref in group)
+                planes[pl.ds((place * block_len + z) * spread, size_x), :] = plane
+
+    def window(start, number):
+        if turned:
+            return jnp.stack([planes[pl.ds(start + i, 3 * block_len, stride=spread), :] for i in range(GROUP)])
+        local = pl.ds(start - number * chunk, GROUP)
+        return jnp.concatenate([refs_of[number][local] for refs_of in (owns, nears, fars)], axis=1)
+
+    def along_z(index, carry, number):
         start = index * GROUP
-        far = sum(ref[pl.ds(start, GROUP)] for ref in fars)
-        window = jnp.concatenate([own[pl.ds(start, GROUP)], near[pl.ds(start, GROUP)], far], axis=1)
-        high, low = split(window)
+        high, low = split(window(start, number))
         terms = jnp.concatenate([high, low, high], axis=1)
         for pair in range(0, GROUP, 2):
             result = dot(axial_matrix, jnp.concatenate([terms[pair], terms[pair + 1]], axis=1))
@@ -216,7 +233,10 @@
                     fields[view, pl.ds(row, block_len), LANES:] = low[part]
         return carry
 
-    lax.fori_loop(0, chunk // GROUP, along_z, 0, unroll=FORWARD_Z)
+    steps = size_x // GROUP // CHUNKS
+    for number in range(CHUNKS):
+        part_of = functools.partial(along_z, number=number)
+        lax.fori_loop(number * steps, (number + 1) * steps, part_of, 0, unroll=FORWARD_Z)
 
     def along_y(index, carry):
         start = index * ROWS
@@ -230,19 +250,22 @@
                 ]
         return carry
 
-    lax.fori_loop(0, chunk // ROWS, along_y, 0, unroll=ALONG_Y)
-
-
-def forward_part(own, near, fars, axial, lateral):
-    chunk, block_len, size_y = own.shape
+    lax.fori_loop(0, size_x // ROWS, along_y, 0, unroll=ALONG_Y)
+
+
+def forward_part(parts, axial, lateral, block_len, size_x, turned):
+    size_y = parts[0].shape[2]
     view_count = lateral.shape[0]
+    scratch = [pltpu.VMEM((view_count, size_x * block_len, 2 * size_y), BF16)]
+    if turned:
+        scratch.append(pltpu.VMEM((3 * block_len * (size_x + 1), size_y), F32))
     return pl.pallas_call(
-        functools.partial(forward_kernel, block_len=block_len),
-        out_shape=pltpu.VMEM((view_count * block_len * (chunk + 1), size_y), F32),
-        scratch_shapes=[pltpu.VMEM((view_count, chunk * block_len, 2 * size_y), BF16)],
+        functools.partial(forward_kernel, block_len=block_len, turned=turned),
+        out_shape=pltpu.VMEM((view_count * block_len * (size_x + 1), size_y), F32),
+        scratch_shapes=scratch,
         compiler_params=pltpu.CompilerParams(vmem_limit_bytes=VMEM_LIMIT),
         name="forward_part",
-    )(*in_vmem(own, near, *fars), axial, *in_vmem(lateral))
+    )(*in_vmem(*parts), axial, *in_vmem(lateral))
 
 
 def quotient_kernel(*refs, chunks, block_len):
@@ -299,8 +322,10 @@
     )(*in_vmem(*parts, recorded, fwd, bwd))
 
 
-def backward_kernel(field, axial, sums, lateral, own, near, far, terms, *, block_len, offset):
-    chunk = own.shape[0]
+def backward_kernel(field, axial, sums, lateral, own, near, *refs, block_len):
+    *fars, terms = refs
+    size_x = own.shape[0]
+    chunk = size_x // len(fars)
     view_count = lateral.shape[0]
     planes = view_count * block_len
     spread = planes + 1
@@ -314,7 +339,7 @@
         for view in range(view_count):
             rows = jnp.concatenate(
                 [
-                    field[pl.ds((offset + start + i) * spread + view * block_len, block_len), :]
+                    field[pl.ds((start + i) * spread + view * block_len, block_len), :]
                     for i in range(ROWS)
                 ],
                 axis=0,
@@ -327,34 +352,39 @@
                 terms[pl.ds(start, ROWS), row : row + block_len, :] = part
         return carry
 
-    lax.fori_loop(0, chunk // ROWS, along_y, 0, unroll=ALONG_Y)
-
-    def along_z(index, carry):
-        start = index * GROUP
-        for pair in range(0, GROUP, 2):
-            sent = dot(
-                axial_matrix, jnp.concatenate([terms[start + pair], terms[start + pair + 1]], axis=1)
-            )
-            for side in (0, 1):
-                lanes_of = slice(side * LANES, (side + 1) * LANES)
-                for place, ref in enumerate((own, near, far)):
-                    ref[start + pair + side] = sent[place * block_len : (place + 1) * block_len, lanes_of]
-        return carry
-
-    lax.fori_loop(0, chunk // GROUP, along_z, 0, unroll=BACKWARD_Z)
-
-
-def backward_part(field, axial, sums, lateral, block_len, chunk, offset):
+    lax.fori_loop(0, size_x // ROWS, along_y, 0, unroll=ALONG_Y)
+
+    for number, far in enumerate(fars):
+
+        def along_z(index, carry):
+            local = index * GROUP
+            start = number * chunk + local
+            for pair in range(0, GROUP, 2):
+                both = jnp.concatenate([terms[start + pair], terms[start + pair + 1]], axis=1)
+                sent = dot(axial_matrix, both)
+                for side in (0, 1):
+                    lanes_of = slice(side * LANES, (side + 1) * LANES)
+                    own[start + pair + side] = sent[:block_len, lanes_of]
+                    near[start + pair + side] = sent[block_len : 2 * block_len, lanes_of]
+                    far[local + pair + side] = sent[2 * block_len :, lanes_of]
+            return carry
+
+        lax.fori_loop(0, chunk // GROUP, along_z, 0, unroll=BACKWARD_Z)
+
+
+def backward_part(field, axial, sums, lateral, block_len, size_x):
     size_y = field.shape[1]
     planes = lateral.shape[0] * block_len
-    shape = pltpu.VMEM((chunk, block_len, size_y), F32)
-    return pl.pallas_call(
-        functools.partial(backward_kernel, block_len=block_len, offset=offset),
-        out_shape=(shape, shape, shape),
-        scratch_shapes=[pltpu.VMEM((chunk, 3 * planes, size_y), BF16)],
+    whole = pltpu.VMEM((size_x, block_len, size_y), F32)
+    part = pltpu.VMEM((size_x // CHUNKS, block_len, size_y), F32)
+    own, near, *fars = pl.pallas_call(
+        functools.partial(backward_kernel, block_len=block_len),
+        out_shape=(whole, whole) + (part,) * CHUNKS,
+        scratch_shapes=[pltpu.VMEM((size_x, 3 * planes, size_y), BF16)],
         compiler_params=pltpu.CompilerParams(vmem_limit_bytes=VMEM_LIMIT),
         name="backward_part",
     )(*in_vmem(field), axial, sums, *in_vmem(lateral))
+    return own, near, fars
 
 
 def body(recorded, initial, kernel_x, kernel_y, kernel_z):
@@ -368,27 +398,36 @@
     def swap(value, pairs):
         return lax.ppermute(value, "slab", pairs)
 
-    estimate = jnp.transpose(initial, (1, 0, 2))
     planes = recorded.reshape(view_count * block_len, size_x, size_y)
-    fars = [swap(estimate, first_pairs)]
-    near = swap(estimate, near_pairs)
+    first = swap(initial, first_pairs)
+    near = swap(initial, near_pairs)
     fwd_x, bwd_x, fwd_y, bwd_y, fwd_z, bwd_z, planes, sums = prepare(
         kernel_x, kernel_y, kernel_z, initial, planes, "slab"
     )
-    delayed, sums = lax.optimization_barrier((estimate, sums))
+    delayed, sums = lax.optimization_barrier((initial, sums))
     sums = summed(sums, "slab")
-    fars.append(swap(delayed, second_pairs))
+    parts = [initial, near, first, swap(delayed, second_pairs)]
+    chunk = size_x // CHUNKS
+    far_pairs = first_pairs + second_pairs
     for iteration in range(ITERS):
-        if iteration:
-            fars = [swap(estimate, first_pairs + second_pairs)]
-            near = swap(estimate, near_pairs)
-        part = forward_part(estimate, near, fars, fwd_z, fwd_y)
+        last = iteration == ITERS - 1
+        part = forward_part(parts, fwd_z, fwd_y, block_len, size_x, not iteration)
         field = quotient_part([part], planes, fwd_x, bwd_x)
-        own, near, far = backward_part(field, bwd_z, sums, bwd_y, block_len, size_x, 0)
-        far = swap(far, first_pairs + second_pairs)
+        own, near, fars = backward_part(field, bwd_z, sums, bwd_y, block_len, size_x)
+        fars = [swap(far, far_pairs) for far in fars]
         near = swap(near, near_pairs)
-        estimate = estimate * (own + near + far) / view_count
-    return jnp.transpose(estimate, (1, 0, 2))
+        estimate, near_halos, far_halos = [], [], []
+        for i, far in enumerate(fars):
+            rows = slice(i * chunk, (i + 1) * chunk)
+            if i:
+                estimate[-1], far = lax.optimization_barrier((estimate[-1], far))
+            before = parts[i] if iteration else jnp.transpose(initial[:, rows], (1, 0, 2))
+            estimate.append(before * (own[rows] + near[rows] + far) / view_count)
+            if not last:
+                near_halos.append(swap(estimate[i], near_pairs))
+                far_halos.append(swap(estimate[i], far_pairs))
+        parts = estimate + near_halos + far_halos
+    return jnp.transpose(jnp.concatenate(estimate, axis=0), (1, 0, 2))
 
 
 def solution(mesh):

time: 138 us -> 138 us (level)
  starting transfers between devices: 22.1 us -> 33.6 us
  waiting for transfers between devices: 95.3 us -> 85.6 us
  local copies, waits for them, and re-layouts: 3.13 us -> 1.38 us
    ppermute x9 -> x13, waiting for transfers between devices: 73.7 us -> 62.9 us  [swap(): return lax.ppermute(value, 'slab', pairs)]
    ppermute x9 -> x13, starting transfers between devices: 18.4 us -> 25.7 us  [swap(): return lax.ppermute(value, 'slab', pairs)]
    ppermute x4, starting transfers between devices: 3.72 us -> 7.84 us  [summed(): lax.ppermute(value, axis, [(i, i ^ step) for i in range(count)])]
    unnamed x3 -> x2, local copies, waits for them, and re-layouts: 1.84 us -> 0.01 us
  transfers between devices with their start and end apart: 13 -> 17, of which waited for: 7 -> 10; matrix products, arithmetic and copies ran while one was open for 0% -> 0% of each run, Pallas kernels for 2% -> 0%
where the time goes in v4:
time: 138 us
  waiting for transfers between devices  85.6 us (62%)
  starting transfers between devices  33.6 us (24%)
  Pallas kernels  16 us (12%)
    ppermute x13, waiting for transfers between devices, swap(): return lax.ppermute(value, 'slab', pairs)  62.9 us
    ppermute x13, starting transfers between devices, swap(): return lax.ppermute(value, 'slab', pairs)  25.7 us
    ppermute x4, waiting for transfers between devices, summed(): lax.ppermute(value, axis, [(i, i ^ step) for i in range(count)])  22.6 us
    ppermute x4, starting transfers between devices, summed(): lax.ppermute(value, axis, [(i, i ^ step) for i in range(count)])  7.84 us
    pallas_call x2, Pallas kernels, forward_part(): pl.pallas_call(functools.partial(forward_kernel, block_len=block_len, tur...  4.88 us
    pallas_call x2, Pallas kernels, quotient_part(): pl.pallas_call(functools.partial(quotient_kernel, chunks=len(parts), bloc...  3.95 us
    pallas_call x2, Pallas kernels, backward_part(): pl.pallas_call(functools.partial(backward_kernel, block_len=block_len), o...  3.92 us
    pallas_call x1, Pallas kernels, prepare(): pl.pallas_call(functools.partial(prepare_kernel, count=lax.axis_size(axis...  3.22 us
  transfers between devices with their start and end apart: 17, of which 10 were waited for; matrix products, arithmetic and copies ran while one was open for 0% of the time, Pallas kernels for 0%

profile of v4, /device:TPU:11, one launch (start us, length us, event | category | flops | bytes accessed | tf_op | source)
XLA Modules:
  0.0 137.9 jit_solution(17727798135571954907)
XLA Ops:
  0.0 3.2 %prepare.1 = (bf16[3,128,384]{2,1,0:T(8,128)(2,1)S(1)}, bf16[3,128,384]{2,1,0:T(8,128)(2,1)S(1)}, bf16[3,256,256]{2,1,0:T(8,128)(2,1)S(1)}, bf16[3,256,256]{2,1,...) custom-call(s32[1]{0:T(128)} %bitcast.1.position, ...), custom_call_target="tpu_custom_call" | custom-call | tf_op jit(solution)/shard_map/prepare/pallas_call | solution.py:153
  3.2 3.7 %collective-permute-start.2 = (f32[16,128,128]{2,1,0:T(8,128)S(1)}, f32[16,128,128]{2,1,0:T(8,128)S(1)}, u32[]{:S(2)}, u32[]{:S(2)}) collective-permute-start(f32[16,128,128]{2,1,0:T(8,128)S(1)} %copy-done), channel_id=1, source_target_pairs={{1,2},{2,1},{5,6},{6,5},{9,10},{10,9},{13,14},{14,13},{17,18},{18,... | collective-permute-start | bytes 3145736 | tf_op jit(solution)/shard_map/ppermute | solution.py:399
  7.0 0.1 collective-permute-start
  7.0 0.7 collective-permute-start.1
  7.8 4.1 %collective-permute-start.3 = (f32[8,256]{1,0:T(8,128)S(1)}, f32[8,256]{1,0:T(8,128)S(1)}, u32[]{:S(2)}, u32[]{:S(2)}) collective-permute-start(f32[8,256]{1,0:T(8,128)S(1)} %get-tuple-element.35), channel_id=1, source_target_pairs={{0,2},{1,3},{2,0},{3,1},{4,6},{5,7},{6,4},{7,5},{8,10},{9,11},{10,... | collective-permute-start | bytes 24584 | tf_op jit(solution)/shard_map/ppermute | solution.py:188
  11.9 18.2 %collective-permute-done.3 = f32[8,256]{1,0:T(8,128)S(1)} collective-permute-done((f32[8,256]{1,0:T(8,128)S(1)}, f32[8,256]{1,0:T(8,128)S(1)}, u32[]{:S(2)}, u32[]{:S(2)}) %collective-permute-start.3) | collective-permute-done | bytes 8224 | tf_op jit(solution)/shard_map/ppermute | solution.py:188
  30.1 1.4 %collective-permute-start.4 = (f32[8,256]{1,0:T(8,128)S(1)}, f32[8,256]{1,0:T(8,128)S(1)}, u32[]{:S(2)}, u32[]{:S(2)}) collective-permute-start(f32[8,256]{1,0:T(8,128)S(1)} %add.36), channel_id=1, source_target_pairs={{0,1},{1,0},{2,3},{3,2},{4,5},{5,4},{6,7},{7,6},{8,9},{9,8},{10,11... | collective-permute-start | bytes 24584 | tf_op jit(solution)/shard_map/ppermute | solution.py:188
  31.5 0.8 collective-permute-done.4
  32.4 0.0 collective-permute-start.5
  32.4 2.5 %collective-permute-done.5 = f32[8,256]{1,0:T(8,128)S(1)} collective-permute-done((f32[8,256]{1,0:T(8,128)S(1)}, f32[8,256]{1,0:T(8,128)S(1)}, u32[]{:S(2)}, u32[]{:S(2)}) %collective-permute-start.5) | collective-permute-done | bytes 8224 | tf_op jit(solution)/shard_map/ppermute | solution.py:188
  34.9 2.3 %collective-permute-start.6 = (f32[8,256]{1,0:T(8,128)S(1)}, f32[8,256]{1,0:T(8,128)S(1)}, u32[]{:S(2)}, u32[]{:S(2)}) collective-permute-start(f32[8,256]{1,0:T(8,128)S(1)} %add.38), channel_id=1, source_target_pairs={{0,8},{1,9},{2,10},{3,11},{4,12},{5,13},{6,14},{7,15},{8,0},{9,1},... | collective-permute-start | bytes 24584 | tf_op jit(solution)/shard_map/ppermute | solution.py:188
  37.2 1.1 collective-permute-done.6
  38.3 0.0 collective-permute-done.2.refs_3_
  38.3 0.0 collective-permute-done.refs_1_
  38.3 0.0 collective-permute-done.1.refs_2_
  38.3 2.7 %forward_part.2.refs_0_ = f32[6192,128]{1,0:T(8,128)S(1)} custom-call(f32[16,128,128]{2,1,0:T(8,128)S(1)} %copy-done, f32[16,128,128]{2,1,0:T(8,128)S(1)} %collective-permute-done.refs_1_, f32[16,128,128]{2,1,0:T(8,128)S(1)} %collective-permute-done.1.refs_2_, f32[16,128,128]{2,1,0:T(8,128)S(1)} %collective-permute-done.2.refs_3_, ...), custom_call_target="tpu_custom_call" | custom-call | tf_op jit(solution)/shard_map/forward_part/pallas_call | solution.py:262
  41.0 2.0 %quotient_part.2.field = f32[6272,128]{1,0:T(8,128)S(1)} custom-call(f32[6192,128]{1,0:T(8,128)S(1)} %forward_part.2.refs_0_, f32[48,128,128]{2,1,0:T(8,128)S(1)} %get-tuple-element.31.refs_1_, bf16[3,128,384]{2,1,0:T(8,128)(2,1)S(1)} %get-tuple-element.32.refs_2_, bf16[3,128,384]{2,1,0:T(8,128)(2,1)S(1)} %get-tuple-element.33.refs_3_), custom_call_target="tpu_custom_call" | custom-call | tf_op jit(solution)/shard_map/quotient_part/pallas_call | solution.py:316
  43.0 2.0 %backward_part.2 = (f32[128,16,128]{2,1,0:T(8,128)S(1)}, f32[128,16,128]{2,1,0:T(8,128)S(1)}, f32[64,16,128]{2,1,0:T(8,128)S(1)}, f32[64,16,128]{2,1,0:T(8,128)S(1)}) custom-call(f32[6272,128]{1,0:T(8,128)S(1)} %quotient_part.2.field, f32[48,256]{1,0:T(8,128)S(1)} %get-tuple-element.34.axial, f32[8,256]{1,0:T(8,128)S(1)} %add.39.sums, ...), custom_call_target="tpu_custom_call" | custom-call | tf_op jit(solution)/shard_map/backward_part/pallas_call | solution.py:380
  44.9 2.7 %collective-permute-start.7 = (f32[128,16,128]{2,1,0:T(8,128)S(1)}, f32[128,16,128]{2,1,0:T(8,128)S(1)}, u32[]{:S(2)}, u32[]{:S(2)}) collective-permute-start(f32[128,16,128]{2,1,0:T(8,128)S(1)} %get-tuple-element.38), channel_id=1, source_target_pairs={{0,1},{1,0},{2,3},{3,2},{4,5},{5,4},{6,7},{7,6},{8,9},{9,8},{10,11... | collective-permute-start | bytes 3145736 | tf_op jit(solution)/shard_map/ppermute | solution.py:399
  47.6 2.6 %collective-permute-start.8 = (f32[64,16,128]{2,1,0:T(8,128)S(1)}, f32[64,16,128]{2,1,0:T(8,128)S(1)}, u32[]{:S(2)}, u32[]{:S(2)}) collective-permute-start(f32[64,16,128]{2,1,0:T(8,128)S(1)} %get-tuple-element.39), channel_id=1, source_target_pairs={{3,4},{4,3},{7,8},{8,7},{11,12},{12,11},{1,2},{2,1},{5,6},{6,5},{9... | collective-permute-start | bytes 1572872 | tf_op jit(solution)/shard_map/ppermute | solution.py:399
  50.3 2.9 %collective-permute-start.9 = (f32[64,16,128]{2,1,0:T(8,128)S(1)}, f32[64,16,128]{2,1,0:T(8,128)S(1)}, u32[]{:S(2)}, u32[]{:S(2)}) collective-permute-start(f32[64,16,128]{2,1,0:T(8,128)S(1)} %get-tuple-element.40), channel_id=1, source_target_pairs={{3,4},{4,3},{7,8},{8,7},{11,12},{12,11},{1,2},{2,1},{5,6},{6,5},{9... | collective-permute-start | bytes 1572872 | tf_op jit(solution)/shard_map/ppermute | solution.py:399
  53.2 0.1 fusion.12
  53.3 16.1 %collective-permute-done.8 = f32[64,16,128]{2,1,0:T(8,128)S(1)} collective-permute-done((f32[64,16,128]{2,1,0:T(8,128)S(1)}, f32[64,16,128]{2,1,0:T(8,128)S(1)}, u32[]{:S(2)}, u32[]{:S(2)}) %collective-permute-start.8) | collective-permute-done | bytes 524320 | tf_op jit(solution)/shard_map/ppermute | solution.py:399
  69.4 0.0 collective-permute-done.7
  69.4 0.4 fusion.11.refs_0_
  69.8 5.2 %collective-permute-done.9 = f32[64,16,128]{2,1,0:T(8,128)S(1)} collective-permute-done((f32[64,16,128]{2,1,0:T(8,128)S(1)}, f32[64,16,128]{2,1,0:T(8,128)S(1)}, u32[]{:S(2)}, u32[]{:S(2)}) %collective-permute-start.9) | collective-permute-done | bytes 524320 | tf_op jit(solution)/shard_map/ppermute | solution.py:399
  75.0 0.4 fusion.8.refs_1_
  75.4 0.1 collective-permute-start.11
  75.5 2.7 %collective-permute-start.13 = (f32[64,16,128]{2,1,0:T(8,128)S(1)}, f32[64,16,128]{2,1,0:T(8,128)S(1)}, u32[]{:S(2)}, u32[]{:S(2)}) collective-permute-start(f32[64,16,128]{2,1,0:T(8,128)S(1)} %fusion.8.refs_1_), channel_id=1, source_target_pairs={{3,4},{4,3},{7,8},{8,7},{11,12},{12,11},{1,2},{2,1},{5,6},{6,5},{9... | collective-permute-start | bytes 1572872 | tf_op jit(solution)/shard_map/ppermute | solution.py:399
  78.2 0.4 collective-permute-start.10
  78.6 4.2 %collective-permute-start.12 = (f32[64,16,128]{2,1,0:T(8,128)S(1)}, f32[64,16,128]{2,1,0:T(8,128)S(1)}, u32[]{:S(2)}, u32[]{:S(2)}) collective-permute-start(f32[64,16,128]{2,1,0:T(8,128)S(1)} %fusion.11.refs_0_), channel_id=1, source_target_pairs={{3,4},{4,3},{7,8},{8,7},{11,12},{12,11},{1,2},{2,1},{5,6},{6,5},{9... | collective-permute-start | bytes 1572872 | tf_op jit(solution)/shard_map/ppermute | solution.py:399
  82.8 0.0 collective-permute-done.11.refs_3_
  82.8 14.4 %collective-permute-done.13.refs_5_ = f32[64,16,128]{2,1,0:T(8,128)S(1)} collective-permute-done((f32[64,16,128]{2,1,0:T(8,128)S(1)}, f32[64,16,128]{2,1,0:T(8,128)S(1)}, u32[]{:S(2)}, u32[]{:S(2)}) %collective-permute-start.13) | collective-permute-done | bytes 524320 | tf_op jit(solution)/shard_map/ppermute | solution.py:399
  97.2 0.0 collective-permute-done.10.refs_2_
  97.2 5.6 %collective-permute-done.12.refs_4_ = f32[64,16,128]{2,1,0:T(8,128)S(1)} collective-permute-done((f32[64,16,128]{2,1,0:T(8,128)S(1)}, f32[64,16,128]{2,1,0:T(8,128)S(1)}, u32[]{:S(2)}, u32[]{:S(2)}) %collective-permute-start.12) | collective-permute-done | bytes 524320 | tf_op jit(solution)/shard_map/ppermute | solution.py:399
  102.9 2.2 %forward_part.3.refs_0_ = f32[6192,128]{1,0:T(8,128)S(1)} custom-call(f32[64,16,128]{2,1,0:T(8,128)S(1)} %fusion.11.refs_0_, f32[64,16,128]{2,1,0:T(8,128)S(1)} %fusion.8.refs_1_, f32[64,16,128]{2,1,0:T(8,128)S(1)} %collective-permute-done.10.refs_2_, f32[64,16,128]{2,1,0:T(8,128)S(1)} %collective-permute-done.11.refs_3_, ...), custom_call_target="tpu_custom_call" | custom-call | tf_op jit(solution)/shard_map/forward_part/pallas_call | solution.py:262
  105.1 1.9 %quotient_part.3.field = f32[6272,128]{1,0:T(8,128)S(1)} custom-call(f32[6192,128]{1,0:T(8,128)S(1)} %forward_part.3.refs_0_, f32[48,128,128]{2,1,0:T(8,128)S(1)} %get-tuple-element.31.refs_1_, bf16[3,128,384]{2,1,0:T(8,128)(2,1)S(1)} %get-tuple-element.32.refs_2_, bf16[3,128,384]{2,1,0:T(8,128)(2,1)S(1)} %get-tuple-element.33.refs_3_), custom_call_target="tpu_custom_call" | custom-call | tf_op jit(solution)/shard_map/quotient_part/pallas_call | solution.py:316
  107.0 2.0 %backward_part.3 = (f32[128,16,128]{2,1,0:T(8,128)S(1)}, f32[128,16,128]{2,1,0:T(8,128)S(1)}, f32[64,16,128]{2,1,0:T(8,128)S(1)}, f32[64,16,128]{2,1,0:T(8,128)S(1)}) custom-call(f32[6272,128]{1,0:T(8,128)S(1)} %quotient_part.3.field, f32[48,256]{1,0:T(8,128)S(1)} %get-tuple-element.34.axial, f32[8,256]{1,0:T(8,128)S(1)} %add.39.sums, ...), custom_call_target="tpu_custom_call" | custom-call | tf_op jit(solution)/shard_map/backward_part/pallas_call | solution.py:380
  109.0 0.1 collective-permute-start.14
  109.0 2.7 %collective-permute-start.15 = (f32[64,16,128]{2,1,0:T(8,128)S(1)}, f32[64,16,128]{2,1,0:T(8,128)S(1)}, u32[]{:S(2)}, u32[]{:S(2)}) collective-permute-start(f32[64,16,128]{2,1,0:T(8,128)S(1)} %get-tuple-element.45), channel_id=1, source_target_pairs={{3,4},{4,3},{7,8},{8,7},{11,12},{12,11},{1,2},{2,1},{5,6},{6,5},{9... | collective-permute-start | bytes 1572872 | tf_op jit(solution)/shard_map/ppermute | solution.py:399
  111.7 2.9 %collective-permute-start.16 = (f32[64,16,128]{2,1,0:T(8,128)S(1)}, f32[64,16,128]{2,1,0:T(8,128)S(1)}, u32[]{:S(2)}, u32[]{:S(2)}) collective-permute-start(f32[64,16,128]{2,1,0:T(8,128)S(1)} %get-tuple-element.46), channel_id=1, source_target_pairs={{3,4},{4,3},{7,8},{8,7},{11,12},{12,11},{1,2},{2,1},{5,6},{6,5},{9... | collective-permute-start | bytes 1572872 | tf_op jit(solution)/shard_map/ppermute | solution.py:399
  114.6 16.2 %collective-permute-done.15 = f32[64,16,128]{2,1,0:T(8,128)S(1)} collective-permute-done((f32[64,16,128]{2,1,0:T(8,128)S(1)}, f32[64,16,128]{2,1,0:T(8,128)S(1)}, u32[]{:S(2)}, u32[]{:S(2)}) %collective-permute-start.15) | collective-permute-done | bytes 524320 | tf_op jit(solution)/shard_map/ppermute | solution.py:399
  130.8 0.0 collective-permute-done.14
  130.8 0.2 fusion.5
  131.0 5.4 %collective-permute-done.16 = f32[64,16,128]{2,1,0:T(8,128)S(1)} collective-permute-done((f32[64,16,128]{2,1,0:T(8,128)S(1)}, f32[64,16,128]{2,1,0:T(8,128)S(1)}, u32[]{:S(2)}, u32[]{:S(2)}) %collective-permute-start.16) | collective-permute-done | bytes 524320 | tf_op jit(solution)/shard_map/ppermute | solution.py:399
  136.4 0.2 fusion.2
  136.6 0.1 maximum_bitcast_fusion
  136.6 1.3 copy.8
  (6 shorter events, 0.0 us)
Async XLA Ops:
  0.0 3.2 %copy-start = (f32[16,128,128]{2,1,0:T(8,128)S(1)}, f32[16,128,128]{2,1,0:T(8,128)}, u32[]{:S(2)}) copy-start(f32[16,128,128]{2,1,0:T(8,128)} %refs_0_.1) | copy-start | bytes 3145732
  3.2 35.0 %collective-permute-start.2 = (f32[16,128,128]{2,1,0:T(8,128)S(1)}, f32[16,128,128]{2,1,0:T(8,128)S(1)}, u32[]{:S(2)}, u32[]{:S(2)}) collective-permute-start(f32[16,128,128]{2,1,0:T(8,128)S(1)} %copy-done), channel_id=1, source_target_pairs={{1,2},{2,1},{5,6},{6,5},{9,10},{10,9},{13,14},{14,13},{17,18},{18,... | collective-permute-start | bytes 3145736 | tf_op jit(solution)/shard_map/ppermute | solution.py:399
  7.0 31.3 %collective-permute-start = (f32[16,128,128]{2,1,0:T(8,128)S(1)}, f32[16,128,128]{2,1,0:T(8,128)S(1)}, u32[]{:S(2)}, u32[]{:S(2)}) collective-permute-start(f32[16,128,128]{2,1,0:T(8,128)S(1)} %copy-done), channel_id=1, source_target_pairs={{0,1},{1,0},{2,3},{3,2},{4,5},{5,4},{6,7},{7,6},{8,9},{9,8},{10,11... | collective-permute-start | bytes 3145736 | tf_op jit(solution)/shard_map/ppermute | solution.py:399
  7.0 31.2 %collective-permute-start.1 = (f32[16,128,128]{2,1,0:T(8,128)S(1)}, f32[16,128,128]{2,1,0:T(8,128)S(1)}, u32[]{:S(2)}, u32[]{:S(2)}) collective-permute-start(f32[16,128,128]{2,1,0:T(8,128)S(1)} %copy-done), channel_id=1, source_target_pairs={{3,4},{4,3},{7,8},{8,7},{11,12},{12,11},{19,20},{20,19},{23,24},{2... | collective-permute-start | bytes 3145736 | tf_op jit(solution)/shard_map/ppermute | solution.py:399
  7.8 22.3 %collective-permute-start.3 = (f32[8,256]{1,0:T(8,128)S(1)}, f32[8,256]{1,0:T(8,128)S(1)}, u32[]{:S(2)}, u32[]{:S(2)}) collective-permute-start(f32[8,256]{1,0:T(8,128)S(1)} %get-tuple-element.35), channel_id=1, source_target_pairs={{0,2},{1,3},{2,0},{3,1},{4,6},{5,7},{6,4},{7,5},{8,10},{9,11},{10,... | collective-permute-start | bytes 24584 | tf_op jit(solution)/shard_map/ppermute | solution.py:188
  30.1 2.3 %collective-permute-start.4 = (f32[8,256]{1,0:T(8,128)S(1)}, f32[8,256]{1,0:T(8,128)S(1)}, u32[]{:S(2)}, u32[]{:S(2)}) collective-permute-start(f32[8,256]{1,0:T(8,128)S(1)} %add.36), channel_id=1, source_target_pairs={{0,1},{1,0},{2,3},{3,2},{4,5},{5,4},{6,7},{7,6},{8,9},{9,8},{10,11... | collective-permute-start | bytes 24584 | tf_op jit(solution)/shard_map/ppermute | solution.py:188
  32.4 2.5 %collective-permute-start.5 = (f32[8,256]{1,0:T(8,128)S(1)}, f32[8,256]{1,0:T(8,128)S(1)}, u32[]{:S(2)}, u32[]{:S(2)}) collective-permute-start(f32[8,256]{1,0:T(8,128)S(1)} %add.37), channel_id=1, source_target_pairs={{0,4},{1,5},{2,6},{3,7},{4,0},{5,1},{6,2},{7,3},{8,12},{9,13},{10,... | collective-permute-start | bytes 24584 | tf_op jit(solution)/shard_map/ppermute | solution.py:188
  34.9 3.4 %collective-permute-start.6 = (f32[8,256]{1,0:T(8,128)S(1)}, f32[8,256]{1,0:T(8,128)S(1)}, u32[]{:S(2)}, u32[]{:S(2)}) collective-permute-start(f32[8,256]{1,0:T(8,128)S(1)} %add.38), channel_id=1, source_target_pairs={{0,8},{1,9},{2,10},{3,11},{4,12},{5,13},{6,14},{7,15},{8,0},{9,1},... | collective-permute-start | bytes 24584 | tf_op jit(solution)/shard_map/ppermute | solution.py:188
  44.9 24.4 %collective-permute-start.7 = (f32[128,16,128]{2,1,0:T(8,128)S(1)}, f32[128,16,128]{2,1,0:T(8,128)S(1)}, u32[]{:S(2)}, u32[]{:S(2)}) collective-permute-start(f32[128,16,128]{2,1,0:T(8,128)S(1)} %get-tuple-element.38), channel_id=1, source_target_pairs={{0,1},{1,0},{2,3},{3,2},{4,5},{5,4},{6,7},{7,6},{8,9},{9,8},{10,11... | collective-permute-start | bytes 3145736 | tf_op jit(solution)/shard_map/ppermute | solution.py:399
  47.6 21.7 %collective-permute-start.8 = (f32[64,16,128]{2,1,0:T(8,128)S(1)}, f32[64,16,128]{2,1,0:T(8,128)S(1)}, u32[]{:S(2)}, u32[]{:S(2)}) collective-permute-start(f32[64,16,128]{2,1,0:T(8,128)S(1)} %get-tuple-element.39), channel_id=1, source_target_pairs={{3,4},{4,3},{7,8},{8,7},{11,12},{12,11},{1,2},{2,1},{5,6},{6,5},{9... | collective-permute-start | bytes 1572872 | tf_op jit(solution)/shard_map/ppermute | solution.py:399
  50.3 24.7 %collective-permute-start.9 = (f32[64,16,128]{2,1,0:T(8,128)S(1)}, f32[64,16,128]{2,1,0:T(8,128)S(1)}, u32[]{:S(2)}, u32[]{:S(2)}) collective-permute-start(f32[64,16,128]{2,1,0:T(8,128)S(1)} %get-tuple-element.40), channel_id=1, source_target_pairs={{3,4},{4,3},{7,8},{8,7},{11,12},{12,11},{1,2},{2,1},{5,6},{6,5},{9... | collective-permute-start | bytes 1572872 | tf_op jit(solution)/shard_map/ppermute | solution.py:399
  75.4 7.4 %collective-permute-start.11 = (f32[64,16,128]{2,1,0:T(8,128)S(1)}, f32[64,16,128]{2,1,0:T(8,128)S(1)}, u32[]{:S(2)}, u32[]{:S(2)}) collective-permute-start(f32[64,16,128]{2,1,0:T(8,128)S(1)} %fusion.8.refs_1_), channel_id=1, source_target_pairs={{0,1},{1,0},{2,3},{3,2},{4,5},{5,4},{6,7},{7,6},{8,9},{9,8},{10,11... | collective-permute-start | bytes 1572872 | tf_op jit(solution)/shard_map/ppermute | solution.py:399
  75.5 21.7 %collective-permute-start.13 = (f32[64,16,128]{2,1,0:T(8,128)S(1)}, f32[64,16,128]{2,1,0:T(8,128)S(1)}, u32[]{:S(2)}, u32[]{:S(2)}) collective-permute-start(f32[64,16,128]{2,1,0:T(8,128)S(1)} %fusion.8.refs_1_), channel_id=1, source_target_pairs={{3,4},{4,3},{7,8},{8,7},{11,12},{12,11},{1,2},{2,1},{5,6},{6,5},{9... | collective-permute-start | bytes 1572872 | tf_op jit(solution)/shard_map/ppermute | solution.py:399
  78.2 19.1 %collective-permute-start.10 = (f32[64,16,128]{2,1,0:T(8,128)S(1)}, f32[64,16,128]{2,1,0:T(8,128)S(1)}, u32[]{:S(2)}, u32[]{:S(2)}) collective-permute-start(f32[64,16,128]{2,1,0:T(8,128)S(1)} %fusion.11.refs_0_), channel_id=1, source_target_pairs={{0,1},{1,0},{2,3},{3,2},{4,5},{5,4},{6,7},{7,6},{8,9},{9,8},{10,11... | collective-permute-start | bytes 1572872 | tf_op jit(solution)/shard_map/ppermute | solution.py:399
  78.6 24.2 %collective-permute-start.12 = (f32[64,16,128]{2,1,0:T(8,128)S(1)}, f32[64,16,128]{2,1,0:T(8,128)S(1)}, u32[]{:S(2)}, u32[]{:S(2)}) collective-permute-start(f32[64,16,128]{2,1,0:T(8,128)S(1)} %fusion.11.refs_0_), channel_id=1, source_target_pairs={{3,4},{4,3},{7,8},{8,7},{11,12},{12,11},{1,2},{2,1},{5,6},{6,5},{9... | collective-permute-start | bytes 1572872 | tf_op jit(solution)/shard_map/ppermute | solution.py:399
  109.0 21.8 %collective-permute-start.14 = (f32[128,16,128]{2,1,0:T(8,128)S(1)}, f32[128,16,128]{2,1,0:T(8,128)S(1)}, u32[]{:S(2)}, u32[]{:S(2)}) collective-permute-start(f32[128,16,128]{2,1,0:T(8,128)S(1)} %get-tuple-element.44), channel_id=1, source_target_pairs={{0,1},{1,0},{2,3},{3,2},{4,5},{5,4},{6,7},{7,6},{8,9},{9,8},{10,11... | collective-permute-start | bytes 3145736 | tf_op jit(solution)/shard_map/ppermute | solution.py:399
  109.0 21.7 %collective-permute-start.15 = (f32[64,16,128]{2,1,0:T(8,128)S(1)}, f32[64,16,128]{2,1,0:T(8,128)S(1)}, u32[]{:S(2)}, u32[]{:S(2)}) collective-permute-start(f32[64,16,128]{2,1,0:T(8,128)S(1)} %get-tuple-element.45), channel_id=1, source_target_pairs={{3,4},{4,3},{7,8},{8,7},{11,12},{12,11},{1,2},{2,1},{5,6},{6,5},{9... | collective-permute-start | bytes 1572872 | tf_op jit(solution)/shard_map/ppermute | solution.py:399
  111.7 24.7 %collective-permute-start.16 = (f32[64,16,128]{2,1,0:T(8,128)S(1)}, f32[64,16,128]{2,1,0:T(8,128)S(1)}, u32[]{:S(2)}, u32[]{:S(2)}) collective-permute-start(f32[64,16,128]{2,1,0:T(8,128)S(1)} %get-tuple-element.46), channel_id=1, source_target_pairs={{3,4},{4,3},{7,8},{8,7},{11,12},{12,11},{1,2},{2,1},{5,6},{6,5},{9... | collective-permute-start | bytes 1572872 | tf_op jit(solution)/shard_map/ppermute | solution.py:399

commit v5 on v4

--- a/solution.py
+++ b/solution.py
@@ -184,7 +184,7 @@
     if count & (count - 1):
         return lax.psum(value, axis)
     steps = [1 << bit for bit in range(count.bit_length() - 1)]
-    for step in steps[1:2] + steps[:1] + steps[2:]:
+    for step in steps:
         value = value + lax.ppermute(value, axis, [(i, i ^ step) for i in range(count)])
     return value
 
@@ -322,10 +322,8 @@
     )(*in_vmem(*parts, recorded, fwd, bwd))
 
 
-def backward_kernel(field, axial, sums, lateral, own, near, *refs, block_len):
-    *fars, terms = refs
-    size_x = own.shape[0]
-    chunk = size_x // len(fars)
+def backward_kernel(field, axial, sums, lateral, own, near, far, terms, *, block_len, offset):
+    chunk = own.shape[0]
     view_count = lateral.shape[0]
     planes = view_count * block_len
     spread = planes + 1
@@ -339,7 +337,7 @@
         for view in range(view_count):
             rows = jnp.concatenate(
                 [
-                    field[pl.ds((start + i) * spread + view * block_len, block_len), :]
+                    field[pl.ds((offset + start + i) * spread + view * block_len, block_len), :]
                     for i in range(ROWS)
                 ],
                 axis=0,
@@ -352,39 +350,68 @@
                 terms[pl.ds(start, ROWS), row : row + block_len, :] = part
         return carry
 
-    lax.fori_loop(0, size_x // ROWS, along_y, 0, unroll=ALONG_Y)
-
-    for number, far in enumerate(fars):
-
-        def along_z(index, carry):
-            local = index * GROUP
-            start = number * chunk + local
-            for pair in range(0, GROUP, 2):
-                both = jnp.concatenate([terms[start + pair], terms[start + pair + 1]], axis=1)
-                sent = dot(axial_matrix, both)
-                for side in (0, 1):
-                    lanes_of = slice(side * LANES, (side + 1) * LANES)
-                    own[start + pair + side] = sent[:block_len, lanes_of]
-                    near[start + pair + side] = sent[block_len : 2 * block_len, lanes_of]
-                    far[local + pair + side] = sent[2 * block_len :, lanes_of]
-            return carry
-
-        lax.fori_loop(0, chunk // GROUP, along_z, 0, unroll=BACKWARD_Z)
-
-
-def backward_part(field, axial, sums, lateral, block_len, size_x):
+    lax.fori_loop(0, chunk // ROWS, along_y, 0, unroll=ALONG_Y)
+
+    def along_z(index, carry):
+        start = index * GROUP
+        for pair in range(0, GROUP, 2):
+            both = jnp.concatenate([terms[start + pair], terms[start + pair + 1]], axis=1)
+            sent = dot(axial_matrix, both)
+            for side in (0, 1):
+                lanes_of = slice(side * LANES, (side + 1) * LANES)
+                for place, ref in enumerate((own, near, far)):
+                    ref[start + pair + side] = sent[place * block_len : (place + 1) * block_len, lanes_of]
+        return carry
+
+    lax.fori_loop(0, chunk // GROUP, along_z, 0, unroll=BACKWARD_Z)
+
+
+def backward_part(field, axial, sums, lateral, block_len, chunk, offset):
     size_y = field.shape[1]
     planes = lateral.shape[0] * block_len
-    whole = pltpu.VMEM((size_x, block_len, size_y), F32)
-    part = pltpu.VMEM((size_x // CHUNKS, block_len, size_y), F32)
-    own, near, *fars = pl.pallas_call(
-        functools.partial(backward_kernel, block_len=block_len),
-        out_shape=(whole, whole) + (part,) * CHUNKS,
-        scratch_shapes=[pltpu.VMEM((size_x, 3 * planes, size_y), BF16)],
+    shape = pltpu.VMEM((chunk, block_len, size_y), F32)
+    return pl.pallas_call(
+        functools.partial(backward_kernel, block_len=block_len, offset=offset),
+        out_shape=(shape,) * 3,
+        scratch_shapes=[pltpu.VMEM((chunk, 3 * planes, size_y), BF16)],
         compiler_params=pltpu.CompilerParams(vmem_limit_bytes=VMEM_LIMIT),
         name="backward_part",
     )(*in_vmem(field), axial, sums, *in_vmem(lateral))
-    return own, near, fars
+
+
+def finish_kernel(before, own, near, far, *refs, first, view_count):
+    out, spread_out, turned, sem = refs[-4:]
+    chunk, block_len, _ = before.shape
+    spread = chunk + 1
+    for i in range(chunk):
+        total = own[i] + near[i] + far[i]
+        spread_out[pl.ds(i, block_len, stride=spread), :] = before[i] * total / view_count
+    for z in range(block_len):
+        turned[z] = spread_out[pl.ds(z * spread, chunk), :]
+    copy = pltpu.make_async_copy(turned, out.at[:, pl.ds(first, chunk), :], sem)
+    copy.start()
+    copy.wait()
+
+
+def finish_part(before, own, near, far, result, first, size_x, view_count):
+    chunk, block_len, size_y = before.shape
+    vmem = pl.BlockSpec(memory_space=pltpu.VMEM)
+    anywhere = pl.BlockSpec(memory_space=pl.ANY)
+    extra = [] if result is None else [result]
+    return pl.pallas_call(
+        functools.partial(finish_kernel, first=first, view_count=view_count),
+        in_specs=[vmem] * 4 + [anywhere] * len(extra),
+        out_specs=anywhere,
+        out_shape=jax.ShapeDtypeStruct((block_len, size_x, size_y), F32),
+        scratch_shapes=[
+            pltpu.VMEM((block_len * (chunk + 1), size_y), F32),
+            pltpu.VMEM((block_len, chunk, size_y), F32),
+            pltpu.SemaphoreType.DMA,
+        ],
+        input_output_aliases={4: 0} if extra else {},
+        compiler_params=pltpu.CompilerParams(vmem_limit_bytes=VMEM_LIMIT),
+        name="finish_part",
+    )(*in_vmem(before, own, near, far), *extra)
 
 
 def body(recorded, initial, kernel_x, kernel_y, kernel_z):
@@ -409,25 +436,30 @@
     parts = [initial, near, first, swap(delayed, second_pairs)]
     chunk = size_x // CHUNKS
     far_pairs = first_pairs + second_pairs
+    result = None
     for iteration in range(ITERS):
         last = iteration == ITERS - 1
         part = forward_part(parts, fwd_z, fwd_y, block_len, size_x, not iteration)
         field = quotient_part([part], planes, fwd_x, bwd_x)
-        own, near, fars = backward_part(field, bwd_z, sums, bwd_y, block_len, size_x)
-        fars = [swap(far, far_pairs) for far in fars]
-        near = swap(near, near_pairs)
         estimate, near_halos, far_halos = [], [], []
-        for i, far in enumerate(fars):
+        sent = []
+        for i in range(CHUNKS):
+            sent.append(backward_part(field, bwd_z, sums, bwd_y, block_len, chunk, i * chunk))
+        fars = [swap(far, far_pairs) for _, _, far in sent]
+        nears = [swap(near, near_pairs) for _, near, _ in sent]
+        for i, ((own, _, _), near, far) in enumerate(zip(sent, nears, fars)):
             rows = slice(i * chunk, (i + 1) * chunk)
+            if last:
+                result = finish_part(parts[i], own, near, far, result, i * chunk, size_x, view_count)
+                continue
             if i:
                 estimate[-1], far = lax.optimization_barrier((estimate[-1], far))
             before = parts[i] if iteration else jnp.transpose(initial[:, rows], (1, 0, 2))
-            estimate.append(before * (own[rows] + near[rows] + far) / view_count)
-            if not last:
-                near_halos.append(swap(estimate[i], near_pairs))
-                far_halos.append(swap(estimate[i], far_pairs))
+            estimate.append(before * (own + near + far) / view_count)
+            near_halos.append(swap(estimate[i], near_pairs))
+            far_halos.append(swap(estimate[i], far_pairs))
         parts = estimate + near_halos + far_halos
-    return jnp.transpose(jnp.concatenate(estimate, axis=0), (1, 0, 2))
+    return result
 
 
 def solution(mesh):

time: 138 us -> 136 us (0.986)
  waiting for transfers between devices: 85.6 us -> 81.1 us
  Pallas kernels: 16 us -> 18.1 us
  starting transfers between devices: 33.6 us -> 35 us
    ppermute x13 -> x15, waiting for transfers between devices: 62.9 us -> 58.5 us  [swap(): return lax.ppermute(value, 'slab', pairs)]
    ppermute x13 -> x15, starting transfers between devices: 25.7 us -> 29.4 us  [swap(): return lax.ppermute(value, 'slab', pairs)]
    ppermute x4, starting transfers between devices: 7.84 us -> 5.62 us  [summed(): lax.ppermute(value, axis, [(i, i ^ step) for i in range(count)])]
    pallas_call x2 -> x6, Pallas kernels: 3.92 us -> 6.1 us  [the longest x4 4.16 us: backward_part(): pl.pallas_call(functools.partial(backward_kernel, block_len=block_len, of...]
  transfers between devices with their start and end apart: 17 -> 19, of which waited for: 10 -> 10; matrix products, arithmetic and copies ran while one was open for 0% -> 0% of each run, Pallas kernels for 0% -> 1%
where the time goes in v5:
time: 136 us
  waiting for transfers between devices  81.1 us (60%)
  starting transfers between devices  35 us (26%)
  Pallas kernels  18.1 us (13%)
    ppermute x15, waiting for transfers between devices, swap(): return lax.ppermute(value, 'slab', pairs)  58.5 us
    ppermute x15, starting transfers between devices, swap(): return lax.ppermute(value, 'slab', pairs)  29.4 us
    ppermute x4, waiting for transfers between devices, summed(): lax.ppermute(value, axis, [(i, i ^ step) for i in range(count)])  22.6 us
    ppermute x4, starting transfers between devices, summed(): lax.ppermute(value, axis, [(i, i ^ step) for i in range(count)])  5.62 us
    pallas_call x2, Pallas kernels, forward_part(): pl.pallas_call(functools.partial(forward_kernel, block_len=block_len, tur...  4.88 us
    pallas_call x4, Pallas kernels, backward_part(): pl.pallas_call(functools.partial(backward_kernel, block_len=block_len, of...  4.16 us
    pallas_call x2, Pallas kernels, quotient_part(): pl.pallas_call(functools.partial(quotient_kernel, chunks=len(parts), bloc...  3.94 us
    pallas_call x1, Pallas kernels, prepare(): pl.pallas_call(functools.partial(prepare_kernel, count=lax.axis_size(axis...  3.22 us
  transfers between devices with their start and end apart: 19, of which 10 were waited for; matrix products, arithmetic and copies ran while one was open for 0% of the time, Pallas kernels for 1%

profile of v5, /device:TPU:11, one launch (start us, length us, event | category | flops | bytes accessed | tf_op | source)
XLA Modules:
  0.0 135.6 jit_solution(11408079714210076918)
XLA Ops:
  0.0 3.2 %prepare.1 = (bf16[3,128,384]{2,1,0:T(8,128)(2,1)S(1)}, bf16[3,128,384]{2,1,0:T(8,128)(2,1)S(1)}, bf16[3,256,256]{2,1,0:T(8,128)(2,1)S(1)}, bf16[3,256,256]{2,1,...) custom-call(s32[1]{0:T(128)} %bitcast.1.position, ...), custom_call_target="tpu_custom_call" | custom-call | tf_op jit(solution)/shard_map/prepare/pallas_call | solution.py:153
  3.2 3.7 %collective-permute-start.2 = (f32[16,128,128]{2,1,0:T(8,128)S(1)}, f32[16,128,128]{2,1,0:T(8,128)S(1)}, u32[]{:S(2)}, u32[]{:S(2)}) collective-permute-start(f32[16,128,128]{2,1,0:T(8,128)S(1)} %copy-done), channel_id=1, source_target_pairs={{1,2},{2,1},{5,6},{6,5},{9,10},{10,9},{13,14},{14,13},{17,18},{18,... | collective-permute-start | bytes 3145736 | tf_op jit(solution)/shard_map/ppermute | solution.py:426
  7.0 0.1 collective-permute-start
  7.0 0.7 collective-permute-start.1
  7.8 1.7 %collective-permute-start.3 = (f32[8,256]{1,0:T(8,128)S(1)}, f32[8,256]{1,0:T(8,128)S(1)}, u32[]{:S(2)}, u32[]{:S(2)}) collective-permute-start(f32[8,256]{1,0:T(8,128)S(1)} %get-tuple-element.37), channel_id=1, source_target_pairs={{0,1},{1,0},{2,3},{3,2},{4,5},{5,4},{6,7},{7,6},{8,9},{9,8},{10,11... | collective-permute-start | bytes 24584 | tf_op jit(solution)/shard_map/ppermute | solution.py:188
  9.5 0.8 collective-permute-done.3
  10.3 2.7 %collective-permute-start.4 = (f32[8,256]{1,0:T(8,128)S(1)}, f32[8,256]{1,0:T(8,128)S(1)}, u32[]{:S(2)}, u32[]{:S(2)}) collective-permute-start(f32[8,256]{1,0:T(8,128)S(1)} %add.24), channel_id=1, source_target_pairs={{0,2},{1,3},{2,0},{3,1},{4,6},{5,7},{6,4},{7,5},{8,10},{9,11},{10,... | collective-permute-start | bytes 24584 | tf_op jit(solution)/shard_map/ppermute | solution.py:188
  13.0 17.0 %collective-permute-done.4 = f32[8,256]{1,0:T(8,128)S(1)} collective-permute-done((f32[8,256]{1,0:T(8,128)S(1)}, f32[8,256]{1,0:T(8,128)S(1)}, u32[]{:S(2)}, u32[]{:S(2)}) %collective-permute-start.4) | collective-permute-done | bytes 8224 | tf_op jit(solution)/shard_map/ppermute | solution.py:188
  30.1 0.2 collective-permute-start.5
  30.3 2.3 %collective-permute-done.5 = f32[8,256]{1,0:T(8,128)S(1)} collective-permute-done((f32[8,256]{1,0:T(8,128)S(1)}, f32[8,256]{1,0:T(8,128)S(1)}, u32[]{:S(2)}, u32[]{:S(2)}) %collective-permute-start.5) | collective-permute-done | bytes 8224 | tf_op jit(solution)/shard_map/ppermute | solution.py:188
  32.6 1.0 collective-permute-start.6
  33.6 2.4 %collective-permute-done.6 = f32[8,256]{1,0:T(8,128)S(1)} collective-permute-done((f32[8,256]{1,0:T(8,128)S(1)}, f32[8,256]{1,0:T(8,128)S(1)}, u32[]{:S(2)}, u32[]{:S(2)}) %collective-permute-start.6) | collective-permute-done | bytes 8224 | tf_op jit(solution)/shard_map/ppermute | solution.py:188
  36.0 0.0 collective-permute-done.2.refs_3_
  36.0 0.0 collective-permute-done.refs_1_
  36.0 0.0 collective-permute-done.1.refs_2_
  36.0 2.7 %forward_part.2.refs_0_ = f32[6192,128]{1,0:T(8,128)S(1)} custom-call(f32[16,128,128]{2,1,0:T(8,128)S(1)} %copy-done, f32[16,128,128]{2,1,0:T(8,128)S(1)} %collective-permute-done.refs_1_, f32[16,128,128]{2,1,0:T(8,128)S(1)} %collective-permute-done.1.refs_2_, f32[16,128,128]{2,1,0:T(8,128)S(1)} %collective-permute-done.2.refs_3_, ...), custom_call_target="tpu_custom_call" | custom-call | tf_op jit(solution)/shard_map/forward_part/pallas_call | solution.py:262
  38.7 2.0 %quotient_part.2.field = f32[6272,128]{1,0:T(8,128)S(1)} custom-call(f32[6192,128]{1,0:T(8,128)S(1)} %forward_part.2.refs_0_, f32[48,128,128]{2,1,0:T(8,128)S(1)} %get-tuple-element.33.refs_1_, bf16[3,128,384]{2,1,0:T(8,128)(2,1)S(1)} %get-tuple-element.34.refs_2_, bf16[3,128,384]{2,1,0:T(8,128)(2,1)S(1)} %get-tuple-element.35.refs_3_), custom_call_target="tpu_custom_call" | custom-call | tf_op jit(solution)/shard_map/quotient_part/pallas_call | solution.py:316
  40.7 1.0 backward_part.5
  41.8 3.8 %collective-permute-start.8 = (f32[64,16,128]{2,1,0:T(8,128)S(1)}, f32[64,16,128]{2,1,0:T(8,128)S(1)}, u32[]{:S(2)}, u32[]{:S(2)}) collective-permute-start(f32[64,16,128]{2,1,0:T(8,128)S(1)} %get-tuple-element.42), channel_id=1, source_target_pairs={{0,1},{1,0},{2,3},{3,2},{4,5},{5,4},{6,7},{7,6},{8,9},{9,8},{10,11... | collective-permute-start | bytes 1572872 | tf_op jit(solution)/shard_map/ppermute | solution.py:426
  45.5 1.9 %collective-permute-start.9 = (f32[64,16,128]{2,1,0:T(8,128)S(1)}, f32[64,16,128]{2,1,0:T(8,128)S(1)}, u32[]{:S(2)}, u32[]{:S(2)}) collective-permute-start(f32[64,16,128]{2,1,0:T(8,128)S(1)} %get-tuple-element.43), channel_id=1, source_target_pairs={{3,4},{4,3},{7,8},{8,7},{11,12},{12,11},{1,2},{2,1},{5,6},{6,5},{9... | collective-permute-start | bytes 1572872 | tf_op jit(solution)/shard_map/ppermute | solution.py:426
  47.5 1.0 backward_part.4
  48.5 3.6 %collective-permute-start.10 = (f32[64,16,128]{2,1,0:T(8,128)S(1)}, f32[64,16,128]{2,1,0:T(8,128)S(1)}, u32[]{:S(2)}, u32[]{:S(2)}) collective-permute-start(f32[64,16,128]{2,1,0:T(8,128)S(1)} %get-tuple-element.44), channel_id=1, source_target_pairs={{3,4},{4,3},{7,8},{8,7},{11,12},{12,11},{1,2},{2,1},{5,6},{6,5},{9... | collective-permute-start | bytes 1572872 | tf_op jit(solution)/shard_map/ppermute | solution.py:426
  52.1 1.0 collective-permute-start.7
  53.1 0.1 fusion.4
  53.3 14.0 %collective-permute-done.9 = f32[64,16,128]{2,1,0:T(8,128)S(1)} collective-permute-done((f32[64,16,128]{2,1,0:T(8,128)S(1)}, f32[64,16,128]{2,1,0:T(8,128)S(1)}, u32[]{:S(2)}, u32[]{:S(2)}) %collective-permute-start.9) | collective-permute-done | bytes 524320 | tf_op jit(solution)/shard_map/ppermute | solution.py:426
  67.3 0.4 fusion.1.refs_0_.before
  67.7 5.2 %collective-permute-done.10 = f32[64,16,128]{2,1,0:T(8,128)S(1)} collective-permute-done((f32[64,16,128]{2,1,0:T(8,128)S(1)}, f32[64,16,128]{2,1,0:T(8,128)S(1)}, u32[]{:S(2)}, u32[]{:S(2)}) %collective-permute-start.10) | collective-permute-done | bytes 524320 | tf_op jit(solution)/shard_map/ppermute | solution.py:426
  72.9 0.0 collective-permute-done.7
  72.9 0.4 fusion.3.refs_1_.before
  73.3 0.1 collective-permute-start.12
  73.4 1.9 %collective-permute-start.14 = (f32[64,16,128]{2,1,0:T(8,128)S(1)}, f32[64,16,128]{2,1,0:T(8,128)S(1)}, u32[]{:S(2)}, u32[]{:S(2)}) collective-permute-start(f32[64,16,128]{2,1,0:T(8,128)S(1)} %fusion.3.refs_1_.before), channel_id=1, source_target_pairs={{3,4},{4,3},{7,8},{8,7},{11,12},{12,11},{1,2},{2,1},{5,6},{6,5},{9... | collective-permute-start | bytes 1572872 | tf_op jit(solution)/shard_map/ppermute | solution.py:426
  75.3 0.6 collective-permute-start.11
  75.9 4.8 %collective-permute-start.13 = (f32[64,16,128]{2,1,0:T(8,128)S(1)}, f32[64,16,128]{2,1,0:T(8,128)S(1)}, u32[]{:S(2)}, u32[]{:S(2)}) collective-permute-start(f32[64,16,128]{2,1,0:T(8,128)S(1)} %fusion.1.refs_0_.before), channel_id=1, source_target_pairs={{3,4},{4,3},{7,8},{8,7},{11,12},{12,11},{1,2},{2,1},{5,6},{6,5},{9... | collective-permute-start | bytes 1572872 | tf_op jit(solution)/shard_map/ppermute | solution.py:426
  80.7 14.4 %collective-permute-done.14.refs_5_ = f32[64,16,128]{2,1,0:T(8,128)S(1)} collective-permute-done((f32[64,16,128]{2,1,0:T(8,128)S(1)}, f32[64,16,128]{2,1,0:T(8,128)S(1)}, u32[]{:S(2)}, u32[]{:S(2)}) %collective-permute-start.14) | collective-permute-done | bytes 524320 | tf_op jit(solution)/shard_map/ppermute | solution.py:426
  95.2 5.6 %collective-permute-done.13.refs_4_ = f32[64,16,128]{2,1,0:T(8,128)S(1)} collective-permute-done((f32[64,16,128]{2,1,0:T(8,128)S(1)}, f32[64,16,128]{2,1,0:T(8,128)S(1)}, u32[]{:S(2)}, u32[]{:S(2)}) %collective-permute-start.13) | collective-permute-done | bytes 524320 | tf_op jit(solution)/shard_map/ppermute | solution.py:426
  100.8 2.2 %forward_part.3.refs_0_ = f32[6192,128]{1,0:T(8,128)S(1)} custom-call(f32[64,16,128]{2,1,0:T(8,128)S(1)} %fusion.1.refs_0_.before, f32[64,16,128]{2,1,0:T(8,128)S(1)} %fusion.3.refs_1_.before, f32[64,16,128]{2,1,0:T(8,128)S(1)} %collective-permute-done.11.refs_2_, f32[64,16,128]{2,1,0:T(8,128)S(1)} %collective-permute-done.12.refs_3_, ...), custom_call_target="tpu_custom_call" | custom-call | tf_op jit(solution)/shard_map/forward_part/pallas_call | solution.py:262
  103.0 1.9 %quotient_part.3.field = f32[6272,128]{1,0:T(8,128)S(1)} custom-call(f32[6192,128]{1,0:T(8,128)S(1)} %forward_part.3.refs_0_, f32[48,128,128]{2,1,0:T(8,128)S(1)} %get-tuple-element.33.refs_1_, bf16[3,128,384]{2,1,0:T(8,128)(2,1)S(1)} %get-tuple-element.34.refs_2_, bf16[3,128,384]{2,1,0:T(8,128)(2,1)S(1)} %get-tuple-element.35.refs_3_), custom_call_target="tpu_custom_call" | custom-call | tf_op jit(solution)/shard_map/quotient_part/pallas_call | solution.py:316
  104.9 1.0 backward_part.7
  106.0 1.0 backward_part.6
  107.0 0.1 collective-permute-start.17
  107.1 1.9 %collective-permute-start.18 = (f32[64,16,128]{2,1,0:T(8,128)S(1)}, f32[64,16,128]{2,1,0:T(8,128)S(1)}, u32[]{:S(2)}, u32[]{:S(2)}) collective-permute-start(f32[64,16,128]{2,1,0:T(8,128)S(1)} %get-tuple-element.52), channel_id=1, source_target_pairs={{3,4},{4,3},{7,8},{8,7},{11,12},{12,11},{1,2},{2,1},{5,6},{6,5},{9... | collective-permute-start | bytes 1572872 | tf_op jit(solution)/shard_map/ppermute | solution.py:426
  109.0 0.6 collective-permute-start.15
  109.6 4.6 %collective-permute-start.16 = (f32[64,16,128]{2,1,0:T(8,128)S(1)}, f32[64,16,128]{2,1,0:T(8,128)S(1)}, u32[]{:S(2)}, u32[]{:S(2)}) collective-permute-start(f32[64,16,128]{2,1,0:T(8,128)S(1)} %get-tuple-element.49), channel_id=1, source_target_pairs={{3,4},{4,3},{7,8},{8,7},{11,12},{12,11},{1,2},{2,1},{5,6},{6,5},{9... | collective-permute-start | bytes 1572872 | tf_op jit(solution)/shard_map/ppermute | solution.py:426
  114.2 0.0 collective-permute-done.17.near
  114.2 14.6 %collective-permute-done.18.far = f32[64,16,128]{2,1,0:T(8,128)S(1)} collective-permute-done((f32[64,16,128]{2,1,0:T(8,128)S(1)}, f32[64,16,128]{2,1,0:T(8,128)S(1)}, u32[]{:S(2)}, u32[]{:S(2)}) %collective-permute-start.18) | collective-permute-done | bytes 524320 | tf_op jit(solution)/shard_map/ppermute | solution.py:426
  128.8 1.0 finish_part.2.refs_0_
  129.8 4.6 %collective-permute-done.16.far = f32[64,16,128]{2,1,0:T(8,128)S(1)} collective-permute-done((f32[64,16,128]{2,1,0:T(8,128)S(1)}, f32[64,16,128]{2,1,0:T(8,128)S(1)}, u32[]{:S(2)}, u32[]{:S(2)}) %collective-permute-start.16) | collective-permute-done | bytes 524320 | tf_op jit(solution)/shard_map/ppermute | solution.py:426
  134.4 1.0 finish_part.3
  (10 shorter events, 0.0 us)
Async XLA Ops:
  0.0 3.2 %copy-start = (f32[16,128,128]{2,1,0:T(8,128)S(1)}, f32[16,128,128]{2,1,0:T(8,128)}, u32[]{:S(2)}) copy-start(f32[16,128,128]{2,1,0:T(8,128)} %refs_0_.1) | copy-start | bytes 3145732
  3.2 32.8 %collective-permute-start.2 = (f32[16,128,128]{2,1,0:T(8,128)S(1)}, f32[16,128,128]{2,1,0:T(8,128)S(1)}, u32[]{:S(2)}, u32[]{:S(2)}) collective-permute-start(f32[16,128,128]{2,1,0:T(8,128)S(1)} %copy-done), channel_id=1, source_target_pairs={{1,2},{2,1},{5,6},{6,5},{9,10},{10,9},{13,14},{14,13},{17,18},{18,... | collective-permute-start | bytes 3145736 | tf_op jit(solution)/shard_map/ppermute | solution.py:426
  7.0 29.1 %collective-permute-start = (f32[16,128,128]{2,1,0:T(8,128)S(1)}, f32[16,128,128]{2,1,0:T(8,128)S(1)}, u32[]{:S(2)}, u32[]{:S(2)}) collective-permute-start(f32[16,128,128]{2,1,0:T(8,128)S(1)} %copy-done), channel_id=1, source_target_pairs={{0,1},{1,0},{2,3},{3,2},{4,5},{5,4},{6,7},{7,6},{8,9},{9,8},{10,11... | collective-permute-start | bytes 3145736 | tf_op jit(solution)/shard_map/ppermute | solution.py:426
  7.0 29.0 %collective-permute-start.1 = (f32[16,128,128]{2,1,0:T(8,128)S(1)}, f32[16,128,128]{2,1,0:T(8,128)S(1)}, u32[]{:S(2)}, u32[]{:S(2)}) collective-permute-start(f32[16,128,128]{2,1,0:T(8,128)S(1)} %copy-done), channel_id=1, source_target_pairs={{3,4},{4,3},{7,8},{8,7},{11,12},{12,11},{19,20},{20,19},{23,24},{2... | collective-permute-start | bytes 3145736 | tf_op jit(solution)/shard_map/ppermute | solution.py:426
  7.8 2.6 %collective-permute-start.3 = (f32[8,256]{1,0:T(8,128)S(1)}, f32[8,256]{1,0:T(8,128)S(1)}, u32[]{:S(2)}, u32[]{:S(2)}) collective-permute-start(f32[8,256]{1,0:T(8,128)S(1)} %get-tuple-element.37), channel_id=1, source_target_pairs={{0,1},{1,0},{2,3},{3,2},{4,5},{5,4},{6,7},{7,6},{8,9},{9,8},{10,11... | collective-permute-start | bytes 24584 | tf_op jit(solution)/shard_map/ppermute | solution.py:188
  10.3 19.7 %collective-permute-start.4 = (f32[8,256]{1,0:T(8,128)S(1)}, f32[8,256]{1,0:T(8,128)S(1)}, u32[]{:S(2)}, u32[]{:S(2)}) collective-permute-start(f32[8,256]{1,0:T(8,128)S(1)} %add.24), channel_id=1, source_target_pairs={{0,2},{1,3},{2,0},{3,1},{4,6},{5,7},{6,4},{7,5},{8,10},{9,11},{10,... | collective-permute-start | bytes 24584 | tf_op jit(solution)/shard_map/ppermute | solution.py:188
  30.1 2.5 %collective-permute-start.5 = (f32[8,256]{1,0:T(8,128)S(1)}, f32[8,256]{1,0:T(8,128)S(1)}, u32[]{:S(2)}, u32[]{:S(2)}) collective-permute-start(f32[8,256]{1,0:T(8,128)S(1)} %add.25), channel_id=1, source_target_pairs={{0,4},{1,5},{2,6},{3,7},{4,0},{5,1},{6,2},{7,3},{8,12},{9,13},{10,... | collective-permute-start | bytes 24584 | tf_op jit(solution)/shard_map/ppermute | solution.py:188
  32.6 3.4 %collective-permute-start.6 = (f32[8,256]{1,0:T(8,128)S(1)}, f32[8,256]{1,0:T(8,128)S(1)}, u32[]{:S(2)}, u32[]{:S(2)}) collective-permute-start(f32[8,256]{1,0:T(8,128)S(1)} %add.26), channel_id=1, source_target_pairs={{0,8},{1,9},{2,10},{3,11},{4,12},{5,13},{6,14},{7,15},{8,0},{9,1},... | collective-permute-start | bytes 24584 | tf_op jit(solution)/shard_map/ppermute | solution.py:188
  41.8 11.5 %collective-permute-start.8 = (f32[64,16,128]{2,1,0:T(8,128)S(1)}, f32[64,16,128]{2,1,0:T(8,128)S(1)}, u32[]{:S(2)}, u32[]{:S(2)}) collective-permute-start(f32[64,16,128]{2,1,0:T(8,128)S(1)} %get-tuple-element.42), channel_id=1, source_target_pairs={{0,1},{1,0},{2,3},{3,2},{4,5},{5,4},{6,7},{7,6},{8,9},{9,8},{10,11... | collective-permute-start | bytes 1572872 | tf_op jit(solution)/shard_map/ppermute | solution.py:426
  45.5 21.7 %collective-permute-start.9 = (f32[64,16,128]{2,1,0:T(8,128)S(1)}, f32[64,16,128]{2,1,0:T(8,128)S(1)}, u32[]{:S(2)}, u32[]{:S(2)}) collective-permute-start(f32[64,16,128]{2,1,0:T(8,128)S(1)} %get-tuple-element.43), channel_id=1, source_target_pairs={{3,4},{4,3},{7,8},{8,7},{11,12},{12,11},{1,2},{2,1},{5,6},{6,5},{9... | collective-permute-start | bytes 1572872 | tf_op jit(solution)/shard_map/ppermute | solution.py:426
  48.5 24.4 %collective-permute-start.10 = (f32[64,16,128]{2,1,0:T(8,128)S(1)}, f32[64,16,128]{2,1,0:T(8,128)S(1)}, u32[]{:S(2)}, u32[]{:S(2)}) collective-permute-start(f32[64,16,128]{2,1,0:T(8,128)S(1)} %get-tuple-element.44), channel_id=1, source_target_pairs={{3,4},{4,3},{7,8},{8,7},{11,12},{12,11},{1,2},{2,1},{5,6},{6,5},{9... | collective-permute-start | bytes 1572872 | tf_op jit(solution)/shard_map/ppermute | solution.py:426
  52.1 20.7 %collective-permute-start.7 = (f32[64,16,128]{2,1,0:T(8,128)S(1)}, f32[64,16,128]{2,1,0:T(8,128)S(1)}, u32[]{:S(2)}, u32[]{:S(2)}) collective-permute-start(f32[64,16,128]{2,1,0:T(8,128)S(1)} %get-tuple-element.40), channel_id=1, source_target_pairs={{0,1},{1,0},{2,3},{3,2},{4,5},{5,4},{6,7},{7,6},{8,9},{9,8},{10,11... | collective-permute-start | bytes 1572872 | tf_op jit(solution)/shard_map/ppermute | solution.py:426
  73.3 7.4 %collective-permute-start.12 = (f32[64,16,128]{2,1,0:T(8,128)S(1)}, f32[64,16,128]{2,1,0:T(8,128)S(1)}, u32[]{:S(2)}, u32[]{:S(2)}) collective-permute-start(f32[64,16,128]{2,1,0:T(8,128)S(1)} %fusion.3.refs_1_.before), channel_id=1, source_target_pairs={{0,1},{1,0},{2,3},{3,2},{4,5},{5,4},{6,7},{7,6},{8,9},{9,8},{10,11... | collective-permute-start | bytes 1572872 | tf_op jit(solution)/shard_map/ppermute | solution.py:426
  73.4 21.7 %collective-permute-start.14 = (f32[64,16,128]{2,1,0:T(8,128)S(1)}, f32[64,16,128]{2,1,0:T(8,128)S(1)}, u32[]{:S(2)}, u32[]{:S(2)}) collective-permute-start(f32[64,16,128]{2,1,0:T(8,128)S(1)} %fusion.3.refs_1_.before), channel_id=1, source_target_pairs={{3,4},{4,3},{7,8},{8,7},{11,12},{12,11},{1,2},{2,1},{5,6},{6,5},{9... | collective-permute-start | bytes 1572872 | tf_op jit(solution)/shard_map/ppermute | solution.py:426
  75.3 19.8 %collective-permute-start.11 = (f32[64,16,128]{2,1,0:T(8,128)S(1)}, f32[64,16,128]{2,1,0:T(8,128)S(1)}, u32[]{:S(2)}, u32[]{:S(2)}) collective-permute-start(f32[64,16,128]{2,1,0:T(8,128)S(1)} %fusion.1.refs_0_.before), channel_id=1, source_target_pairs={{0,1},{1,0},{2,3},{3,2},{4,5},{5,4},{6,7},{7,6},{8,9},{9,8},{10,11... | collective-permute-start | bytes 1572872 | tf_op jit(solution)/shard_map/ppermute | solution.py:426
  75.9 24.9 %collective-permute-start.13 = (f32[64,16,128]{2,1,0:T(8,128)S(1)}, f32[64,16,128]{2,1,0:T(8,128)S(1)}, u32[]{:S(2)}, u32[]{:S(2)}) collective-permute-start(f32[64,16,128]{2,1,0:T(8,128)S(1)} %fusion.1.refs_0_.before), channel_id=1, source_target_pairs={{3,4},{4,3},{7,8},{8,7},{11,12},{12,11},{1,2},{2,1},{5,6},{6,5},{9... | collective-permute-start | bytes 1572872 | tf_op jit(solution)/shard_map/ppermute | solution.py:426
  107.0 7.2 %collective-permute-start.17 = (f32[64,16,128]{2,1,0:T(8,128)S(1)}, f32[64,16,128]{2,1,0:T(8,128)S(1)}, u32[]{:S(2)}, u32[]{:S(2)}) collective-permute-start(f32[64,16,128]{2,1,0:T(8,128)S(1)} %get-tuple-element.51), channel_id=1, source_target_pairs={{0,1},{1,0},{2,3},{3,2},{4,5},{5,4},{6,7},{7,6},{8,9},{9,8},{10,11... | collective-permute-start | bytes 1572872 | tf_op jit(solution)/shard_map/ppermute | solution.py:426
  107.1 21.7 %collective-permute-start.18 = (f32[64,16,128]{2,1,0:T(8,128)S(1)}, f32[64,16,128]{2,1,0:T(8,128)S(1)}, u32[]{:S(2)}, u32[]{:S(2)}) collective-permute-start(f32[64,16,128]{2,1,0:T(8,128)S(1)} %get-tuple-element.52), channel_id=1, source_target_pairs={{3,4},{4,3},{7,8},{8,7},{11,12},{12,11},{1,2},{2,1},{5,6},{6,5},{9... | collective-permute-start | bytes 1572872 | tf_op jit(solution)/shard_map/ppermute | solution.py:426
  109.0 20.8 %collective-permute-start.15 = (f32[64,16,128]{2,1,0:T(8,128)S(1)}, f32[64,16,128]{2,1,0:T(8,128)S(1)}, u32[]{:S(2)}, u32[]{:S(2)}) collective-permute-start(f32[64,16,128]{2,1,0:T(8,128)S(1)} %get-tuple-element.48), channel_id=1, source_target_pairs={{0,1},{1,0},{2,3},{3,2},{4,5},{5,4},{6,7},{7,6},{8,9},{9,8},{10,11... | collective-permute-start | bytes 1572872 | tf_op jit(solution)/shard_map/ppermute | solution.py:426
  109.6 24.9 %collective-permute-start.16 = (f32[64,16,128]{2,1,0:T(8,128)S(1)}, f32[64,16,128]{2,1,0:T(8,128)S(1)}, u32[]{:S(2)}, u32[]{:S(2)}) collective-permute-start(f32[64,16,128]{2,1,0:T(8,128)S(1)} %get-tuple-element.49), channel_id=1, source_target_pairs={{3,4},{4,3},{7,8},{8,7},{11,12},{12,11},{1,2},{2,1},{5,6},{6,5},{9... | collective-permute-start | bytes 1572872 | tf_op jit(solution)/shard_map/ppermute | solution.py:426

commit v6 on v5

--- a/solution.py
+++ b/solution.py
@@ -42,7 +42,7 @@
 
 def prepare_kernel(
     position, taken_x, taken_y, taken_z, initial_in, recorded_in,
-    fwd_x, bwd_x, fwd_y, bwd_y, fwd_z, bwd_z, recorded, out,
+    fwd_x, bwd_x, fwd_y, bwd_y, local_z, far_z, bwd_z, recorded, out,
     taps_x, taps_y, taps_z, initial, sems, *, count,
 ):
     view_count, tap_count = taps_x.shape
@@ -108,15 +108,18 @@
     square = jnp.concatenate([matrix, jnp.zeros((size - planes, size), F32)], axis=0)
     blank = jnp.zeros((planes, size), F32)
 
-    def spread(one, two, three):
+    def spread(step, one, two, three):
         wide = [jnp.concatenate([value, blank], axis=1) for value in (one, two, three)]
-        return wide[0] + pltpu.roll(wide[1], planes, 1) + pltpu.roll(wide[2], 2 * planes, 1)
-
-    high, low = split(matrix)
-    high = high.astype(F32)
-    fwd_z[...] = spread(high, high, low.astype(F32)).astype(BF16)
+        return wide[0] + pltpu.roll(wide[1], step, 1) + pltpu.roll(wide[2], 2 * step, 1)
+
+    lanes = lax.broadcasted_iota(jnp.int32, matrix.shape, 1)
+    ahead = pltpu.roll(matrix, size - 2 * block_len, 1)
+    for ref, value, width in ((local_z, matrix, 2 * block_len), (far_z, ahead, block_len)):
+        high, low = split(jnp.where(lanes < width, value, 0.0))
+        high = high.astype(F32)
+        ref[...] = spread(width, high, high, low.astype(F32)).astype(BF16)
     matrix = square.T[:planes]
-    bwd_z[...] = spread(matrix, matrix, matrix)
+    bwd_z[...] = spread(planes, matrix, matrix, matrix)
 
     copies[3].wait()
     flats = [jnp.zeros((size, LANES), F32) for _ in range(view_count)]
@@ -158,6 +161,7 @@
             out((view_count, size, 3 * size), BF16),
             pltpu.VMEM((view_count, 2 * size, 2 * size), BF16),
             out((view_count, 2 * size, 2 * size), BF16),
+            out((planes, 2 * size), BF16),
             out((planes, 2 * size), BF16),
             out((planes, 2 * size), F32),
             pltpu.VMEM(recorded.shape, F32),
@@ -193,50 +197,98 @@
     return [pltpu.with_memory_space_constraint(value, pltpu.VMEM) for value in values]
 
 
-def forward_kernel(*refs, block_len, turned):
-    if turned:
-        own, near, *fars, axial, lateral, out, fields, planes = refs
-        size_x = own.shape[1]
-    else:
-        *parts, axial, lateral, out, fields = refs
-        count = len(parts) // 3
-        owns, nears, fars = parts[:count], parts[count : 2 * count], parts[2 * count :]
-        chunk = owns[0].shape[0]
-        size_x = chunk * count
-    view_count = lateral.shape[0]
-    axial_matrix = axial[:, : 3 * view_count * block_len]
+def windows(groups, scratch, turned):
+    if not turned:
+        chunk = groups[0][0].shape[0]
+
+        def read(start, number):
+            local = pl.ds(start - number * chunk, GROUP)
+            return jnp.concatenate([group[number][local] for group in groups], axis=1)
+
+        return read
+    block_len, size_x, _ = groups[0][0].shape
     spread = size_x + 1
-    if turned:
-        for place, group in enumerate(([own], [near], fars)):
-            for z in range(block_len):
-                plane = sum(ref[z] for ref in group)
-                planes[pl.ds((place * block_len + z) * spread, size_x), :] = plane
-
-    def window(start, number):
-        if turned:
-            return jnp.stack([planes[pl.ds(start + i, 3 * block_len, stride=spread), :] for i in range(GROUP)])
-        local = pl.ds(start - number * chunk, GROUP)
-        return jnp.concatenate([refs_of[number][local] for refs_of in (owns, nears, fars)], axis=1)
+    for place, group in enumerate(groups):
+        for z in range(block_len):
+            plane = sum(ref[z] for ref in group)
+            scratch[pl.ds((place * block_len + z) * spread, size_x), :] = plane
+    depth = len(groups) * block_len
+
+    def read_turned(start, number):
+        return jnp.stack([scratch[pl.ds(start + i, depth, stride=spread), :] for i in range(GROUP)])
+
+    return read_turned
+
+
+def by_groups(body, size_x, unroll):
+    steps = size_x // GROUP // CHUNKS
+    for number in range(CHUNKS):
+        lax.fori_loop(
+            number * steps, (number + 1) * steps, functools.partial(body, number=number), 0, unroll=unroll
+        )
+
+
+def axial_terms(values):
+    high, low = split(values)
+    return jnp.concatenate([high, low, high], axis=1)
+
+
+def local_kernel(*refs, turned):
+    *parts, axial, out = refs[:-1] if turned else refs
+    half = len(parts) // 2
+    read = windows((parts[:half], parts[half:]), refs[-1], turned)
+    size_x = out.shape[0]
+    depth = parts[0].shape[0 if turned else 1]
+    matrix = axial[:, : 6 * depth]
 
     def along_z(index, carry, number):
         start = index * GROUP
-        high, low = split(window(start, number))
-        terms = jnp.concatenate([high, low, high], axis=1)
+        terms = axial_terms(read(start, number))
         for pair in range(0, GROUP, 2):
-            result = dot(axial_matrix, jnp.concatenate([terms[pair], terms[pair + 1]], axis=1))
+            result = dot(matrix, jnp.concatenate([terms[pair], terms[pair + 1]], axis=1))
+            out[start + pair] = result[:, :LANES]
+            out[start + pair + 1] = result[:, LANES:]
+        return carry
+
+    by_groups(along_z, size_x, FORWARD_Z)
+
+
+def local_part(parts, axial, block_len, size_x, turned):
+    size_y = parts[0].shape[2]
+    return pl.pallas_call(
+        functools.partial(local_kernel, turned=turned),
+        out_shape=pltpu.VMEM((size_x, axial.shape[0], size_y), F32),
+        scratch_shapes=[pltpu.VMEM((2 * block_len * (size_x + 1), size_y), F32)] * turned,
+        compiler_params=pltpu.CompilerParams(vmem_limit_bytes=VMEM_LIMIT),
+        name="local_part",
+    )(*in_vmem(*parts), axial)
+
+
+def forward_kernel(*refs, block_len, turned):
+    scratch = refs[-1]
+    *fars, local, axial, lateral, out, fields = refs[:-1] if turned else refs
+    size_x = local.shape[0]
+    view_count = lateral.shape[0]
+    matrix = axial[:, : 3 * block_len]
+    spread = size_x + 1
+    read = windows((fars,), scratch, turned)
+
+    def along_z(index, carry, number):
+        start = index * GROUP
+        terms = axial_terms(read(start, number))
+        for pair in range(0, GROUP, 2):
+            result = dot(matrix, jnp.concatenate([terms[pair], terms[pair + 1]], axis=1))
             for side in (0, 1):
                 row = (start + pair + side) * block_len
-                high, low = split(result[:, side * LANES : (side + 1) * LANES])
+                mine = result[:, side * LANES : (side + 1) * LANES] + local[start + pair + side]
+                high, low = split(mine)
                 for view in range(view_count):
                     part = slice(view * block_len, (view + 1) * block_len)
                     fields[view, pl.ds(row, block_len), :LANES] = high[part]
                     fields[view, pl.ds(row, block_len), LANES:] = low[part]
         return carry
 
-    steps = size_x // GROUP // CHUNKS
-    for number in range(CHUNKS):
-        part_of = functools.partial(along_z, number=number)
-        lax.fori_loop(number * steps, (number + 1) * steps, part_of, 0, unroll=FORWARD_Z)
+    by_groups(along_z, size_x, FORWARD_Z)
 
     def along_y(index, carry):
         start = index * ROWS
@@ -253,19 +305,19 @@
     lax.fori_loop(0, size_x // ROWS, along_y, 0, unroll=ALONG_Y)
 
 
-def forward_part(parts, axial, lateral, block_len, size_x, turned):
-    size_y = parts[0].shape[2]
+def forward_part(fars, local, axial, lateral, block_len, size_x, turned):
+    size_y = local.shape[2]
     view_count = lateral.shape[0]
     scratch = [pltpu.VMEM((view_count, size_x * block_len, 2 * size_y), BF16)]
     if turned:
-        scratch.append(pltpu.VMEM((3 * block_len * (size_x + 1), size_y), F32))
+        scratch.append(pltpu.VMEM((block_len * (size_x + 1), size_y), F32))
     return pl.pallas_call(
         functools.partial(forward_kernel, block_len=block_len, turned=turned),
         out_shape=pltpu.VMEM((view_count * block_len * (size_x + 1), size_y), F32),
         scratch_shapes=scratch,
         compiler_params=pltpu.CompilerParams(vmem_limit_bytes=VMEM_LIMIT),
         name="forward_part",
-    )(*in_vmem(*parts), axial, *in_vmem(lateral))
+    )(*in_vmem(*fars, local), axial, *in_vmem(lateral))
 
 
 def quotient_kernel(*refs, chunks, block_len):
@@ -428,18 +480,20 @@
     planes = recorded.reshape(view_count * block_len, size_x, size_y)
     first = swap(initial, first_pairs)
     near = swap(initial, near_pairs)
-    fwd_x, bwd_x, fwd_y, bwd_y, fwd_z, bwd_z, planes, sums = prepare(
+    fwd_x, bwd_x, fwd_y, bwd_y, local_z, far_z, bwd_z, planes, sums = prepare(
         kernel_x, kernel_y, kernel_z, initial, planes, "slab"
     )
     delayed, sums = lax.optimization_barrier((initial, sums))
     sums = summed(sums, "slab")
-    parts = [initial, near, first, swap(delayed, second_pairs)]
+    inner = [initial, near]
+    far_halos = [first, swap(delayed, second_pairs)]
     chunk = size_x // CHUNKS
     far_pairs = first_pairs + second_pairs
     result = None
     for iteration in range(ITERS):
         last = iteration == ITERS - 1
-        part = forward_part(parts, fwd_z, fwd_y, block_len, size_x, not iteration)
+        local = local_part(inner, local_z, block_len, size_x, not iteration)
+        part = forward_part(far_halos, local, far_z, fwd_y, block_len, size_x, not iteration)
         field = quotient_part([part], planes, fwd_x, bwd_x)
         estimate, near_halos, far_halos = [], [], []
         sent = []
@@ -450,15 +504,15 @@
         for i, ((own, _, _), near, far) in enumerate(zip(sent, nears, fars)):
             rows = slice(i * chunk, (i + 1) * chunk)
             if last:
-                result = finish_part(parts[i], own, near, far, result, i * chunk, size_x, view_count)
+                result = finish_part(inner[i], own, near, far, result, i * chunk, size_x, view_count)
                 continue
             if i:
                 estimate[-1], far = lax.optimization_barrier((estimate[-1], far))
-            before = parts[i] if iteration else jnp.transpose(initial[:, rows], (1, 0, 2))
+            before = inner[i] if iteration else jnp.transpose(initial[:, rows], (1, 0, 2))
             estimate.append(before * (own + near + far) / view_count)
             near_halos.append(swap(estimate[i], near_pairs))
             far_halos.append(swap(estimate[i], far_pairs))
-        parts = estimate + near_halos + far_halos
+        inner = estimate + near_halos
     return result
 
 

time: 136 us -> 137 us (level)
  waiting for transfers between devices: 81.1 us -> 84.7 us
  starting transfers between devices: 35 us -> 32 us
    ppermute x4, waiting for transfers between devices: 22.6 us -> 25.3 us  [summed(): lax.ppermute(value, axis, [(i, i ^ step) for i in range(count)])]
    ppermute x4, starting transfers between devices: 5.62 us -> 3.09 us  [summed(): lax.ppermute(value, axis, [(i, i ^ step) for i in range(count)])]
  transfers between devices with their start and end apart: 19 -> 19, of which waited for: 10 -> 10; matrix products, arithmetic and copies ran while one was open for 0% -> 0% of each run, Pallas kernels for 1% -> 5%
where the time goes in v6:
time: 137 us; the launch traced here: 136 us
  waiting for transfers between devices  84.7 us (62%)
  starting transfers between devices  32 us (23%)
  Pallas kernels  18.2 us (13%)
    ppermute x15, waiting for transfers between devices, swap(): return lax.ppermute(value, 'slab', pairs)  59.4 us
    ppermute x15, starting transfers between devices, swap(): return lax.ppermute(value, 'slab', pairs)  28.9 us
    ppermute x4, waiting for transfers between devices, summed(): lax.ppermute(value, axis, [(i, i ^ step) for i in range(count)])  25.3 us
    pallas_call x4, Pallas kernels, backward_part(): pl.pallas_call(functools.partial(backward_kernel, block_len=block_len, of...  4.12 us
    pallas_call x2, Pallas kernels, forward_part(): pl.pallas_call(functools.partial(forward_kernel, block_len=block_len, tur...  4.03 us
    pallas_call x2, Pallas kernels, quotient_part(): pl.pallas_call(functools.partial(quotient_kernel, chunks=len(parts), bloc...  3.87 us
    pallas_call x1, Pallas kernels, prepare(): pl.pallas_call(functools.partial(prepare_kernel, count=lax.axis_size(axis...  3.13 us
    ppermute x4, starting transfers between devices, summed(): lax.ppermute(value, axis, [(i, i ^ step) for i in range(count)])  3.09 us
  transfers between devices with their start and end apart: 19, of which 10 were waited for; matrix products, arithmetic and copies ran while one was open for 0% of the time, Pallas kernels for 5%

profile of v6, /device:TPU:11, one launch (start us, length us, event | category | flops | bytes accessed | tf_op | source)
XLA Modules:
  0.0 136.2 jit_solution(17786587930551240722)
XLA Ops:
  0.0 0.7 collective-permute-start.2
  0.7 3.1 %prepare.1 = (bf16[3,128,384]{2,1,0:T(8,128)(2,1)S(1)}, bf16[3,128,384]{2,1,0:T(8,128)(2,1)S(1)}, bf16[3,256,256]{2,1,0:T(8,128)(2,1)S(1)}, bf16[3,256,256]{2,1,...) custom-call(s32[1]{0:T(128)} %bitcast.1.position, ...), custom_call_target="tpu_custom_call" | custom-call | tf_op jit(solution)/shard_map/prepare/pallas_call | solution.py:156
  3.8 3.1 %collective-permute-start.1 = (f32[16,128,128]{2,1,0:T(8,128)S(1)}, f32[16,128,128]{2,1,0:T(8,128)S(1)}, u32[]{:S(2)}, u32[]{:S(2)}) collective-permute-start(f32[16,128,128]{2,1,0:T(8,128)S(1)} %copy-done), channel_id=1, source_target_pairs={{1,2},{2,1},{5,6},{6,5},{9,10},{10,9},{13,14},{14,13},{17,18},{18,... | collective-permute-start | bytes 3145736 | tf_op jit(solution)/shard_map/ppermute | solution.py:478
  7.0 0.7 collective-permute-start
  7.7 0.4 collective-permute-start.3
  8.1 0.9 collective-permute-done.3
  8.9 1.2 collective-permute-start.4
  10.2 19.9 %collective-permute-done.4 = f32[8,256]{1,0:T(8,128)S(1)} collective-permute-done((f32[8,256]{1,0:T(8,128)S(1)}, f32[8,256]{1,0:T(8,128)S(1)}, u32[]{:S(2)}, u32[]{:S(2)}) %collective-permute-start.4) | collective-permute-done | bytes 8224 | tf_op jit(solution)/shard_map/ppermute | solution.py:192
  30.1 0.2 collective-permute-start.5
  30.3 2.3 %collective-permute-done.5 = f32[8,256]{1,0:T(8,128)S(1)} collective-permute-done((f32[8,256]{1,0:T(8,128)S(1)}, f32[8,256]{1,0:T(8,128)S(1)}, u32[]{:S(2)}, u32[]{:S(2)}) %collective-permute-start.5) | collective-permute-done | bytes 8224 | tf_op jit(solution)/shard_map/ppermute | solution.py:192
  32.6 1.3 collective-permute-start.6
  33.9 2.2 %collective-permute-done.6 = f32[8,256]{1,0:T(8,128)S(1)} collective-permute-done((f32[8,256]{1,0:T(8,128)S(1)}, f32[8,256]{1,0:T(8,128)S(1)}, u32[]{:S(2)}, u32[]{:S(2)}) %collective-permute-start.6) | collective-permute-done | bytes 8224 | tf_op jit(solution)/shard_map/ppermute | solution.py:192
  36.1 0.6 local_part.2.refs_2_
  36.7 0.0 collective-permute-done.refs_0_
  36.8 2.1 %forward_part.2.refs_0_ = f32[6192,128]{1,0:T(8,128)S(1)} custom-call(f32[16,128,128]{2,1,0:T(8,128)S(1)} %collective-permute-done.refs_0_, f32[16,128,128]{2,1,0:T(8,128)S(1)} %collective-permute-done.1.refs_1_, f32[128,48,128]{2,1,0:T(8,128)S(1)} %local_part.2.refs_2_, bf16[48,256]{1,0:T(8,128)(2,1)S(1)} %get-tuple-element.33.refs_3_, ...), custom_call_target="tpu_custom_call" | custom-call | tf_op jit(solution)/shard_map/forward_part/pallas_call | solution.py:314
  38.9 1.9 %quotient_part.2.field = f32[6272,128]{1,0:T(8,128)S(1)} custom-call(f32[6192,128]{1,0:T(8,128)S(1)} %forward_part.2.refs_0_, f32[48,128,128]{2,1,0:T(8,128)S(1)} %get-tuple-element.35.refs_1_, bf16[3,128,384]{2,1,0:T(8,128)(2,1)S(1)} %get-tuple-element.36.refs_2_, bf16[3,128,384]{2,1,0:T(8,128)(2,1)S(1)} %get-tuple-element.37.refs_3_), custom_call_target="tpu_custom_call" | custom-call | tf_op jit(solution)/shard_map/quotient_part/pallas_call | solution.py:368
  40.8 1.0 backward_part.5
  41.9 4.2 %collective-permute-start.8 = (f32[64,16,128]{2,1,0:T(8,128)S(1)}, f32[64,16,128]{2,1,0:T(8,128)S(1)}, u32[]{:S(2)}, u32[]{:S(2)}) collective-permute-start(f32[64,16,128]{2,1,0:T(8,128)S(1)} %get-tuple-element.44), channel_id=1, source_target_pairs={{0,1},{1,0},{2,3},{3,2},{4,5},{5,4},{6,7},{7,6},{8,9},{9,8},{10,11... | collective-permute-start | bytes 1572872 | tf_op jit(solution)/shard_map/ppermute | solution.py:478
  46.1 1.9 %collective-permute-start.9 = (f32[64,16,128]{2,1,0:T(8,128)S(1)}, f32[64,16,128]{2,1,0:T(8,128)S(1)}, u32[]{:S(2)}, u32[]{:S(2)}) collective-permute-start(f32[64,16,128]{2,1,0:T(8,128)S(1)} %get-tuple-element.45), channel_id=1, source_target_pairs={{3,4},{4,3},{7,8},{8,7},{11,12},{12,11},{1,2},{2,1},{5,6},{6,5},{9... | collective-permute-start | bytes 1572872 | tf_op jit(solution)/shard_map/ppermute | solution.py:478
  48.0 1.0 backward_part.4
  49.0 3.6 %collective-permute-start.10 = (f32[64,16,128]{2,1,0:T(8,128)S(1)}, f32[64,16,128]{2,1,0:T(8,128)S(1)}, u32[]{:S(2)}, u32[]{:S(2)}) collective-permute-start(f32[64,16,128]{2,1,0:T(8,128)S(1)} %get-tuple-element.46), channel_id=1, source_target_pairs={{3,4},{4,3},{7,8},{8,7},{11,12},{12,11},{1,2},{2,1},{5,6},{6,5},{9... | collective-permute-start | bytes 1572872 | tf_op jit(solution)/shard_map/ppermute | solution.py:478
  52.7 1.0 collective-permute-start.7
  53.7 0.1 fusion.4
  53.8 0.0 collective-permute-done.8
  53.8 14.0 %collective-permute-done.9 = f32[64,16,128]{2,1,0:T(8,128)S(1)} collective-permute-done((f32[64,16,128]{2,1,0:T(8,128)S(1)}, f32[64,16,128]{2,1,0:T(8,128)S(1)}, u32[]{:S(2)}, u32[]{:S(2)}) %collective-permute-start.9) | collective-permute-done | bytes 524320 | tf_op jit(solution)/shard_map/ppermute | solution.py:478
  67.8 0.4 fusion.1.refs_0_.before
  68.2 5.2 %collective-permute-done.10 = f32[64,16,128]{2,1,0:T(8,128)S(1)} collective-permute-done((f32[64,16,128]{2,1,0:T(8,128)S(1)}, f32[64,16,128]{2,1,0:T(8,128)S(1)}, u32[]{:S(2)}, u32[]{:S(2)}) %collective-permute-start.10) | collective-permute-done | bytes 524320 | tf_op jit(solution)/shard_map/ppermute | solution.py:478
  73.4 0.0 collective-permute-done.7
  73.4 0.4 fusion.3.refs_1_.before
  73.9 0.1 collective-permute-start.14
  73.9 0.5 collective-permute-start.13
  74.4 1.9 %collective-permute-start.12 = (f32[64,16,128]{2,1,0:T(8,128)S(1)}, f32[64,16,128]{2,1,0:T(8,128)S(1)}, u32[]{:S(2)}, u32[]{:S(2)}) collective-permute-start(f32[64,16,128]{2,1,0:T(8,128)S(1)} %fusion.3.refs_1_.before), channel_id=1, source_target_pairs={{3,4},{4,3},{7,8},{8,7},{11,12},{12,11},{1,2},{2,1},{5,6},{6,5},{9... | collective-permute-start | bytes 1572872 | tf_op jit(solution)/shard_map/ppermute | solution.py:478
  76.3 3.8 %collective-permute-start.11 = (f32[64,16,128]{2,1,0:T(8,128)S(1)}, f32[64,16,128]{2,1,0:T(8,128)S(1)}, u32[]{:S(2)}, u32[]{:S(2)}) collective-permute-start(f32[64,16,128]{2,1,0:T(8,128)S(1)} %fusion.1.refs_0_.before), channel_id=1, source_target_pairs={{3,4},{4,3},{7,8},{8,7},{11,12},{12,11},{1,2},{2,1},{5,6},{6,5},{9... | collective-permute-start | bytes 1572872 | tf_op jit(solution)/shard_map/ppermute | solution.py:478
  80.2 0.6 local_part.3.refs_2_
  80.8 15.4 %collective-permute-done.12.refs_1_ = f32[64,16,128]{2,1,0:T(8,128)S(1)} collective-permute-done((f32[64,16,128]{2,1,0:T(8,128)S(1)}, f32[64,16,128]{2,1,0:T(8,128)S(1)}, u32[]{:S(2)}, u32[]{:S(2)}) %collective-permute-start.12) | collective-permute-done | bytes 524320 | tf_op jit(solution)/shard_map/ppermute | solution.py:478
  96.2 5.6 %collective-permute-done.11.refs_0_ = f32[64,16,128]{2,1,0:T(8,128)S(1)} collective-permute-done((f32[64,16,128]{2,1,0:T(8,128)S(1)}, f32[64,16,128]{2,1,0:T(8,128)S(1)}, u32[]{:S(2)}, u32[]{:S(2)}) %collective-permute-start.11) | collective-permute-done | bytes 524320 | tf_op jit(solution)/shard_map/ppermute | solution.py:478
  101.8 1.9 %forward_part.3.refs_0_ = f32[6192,128]{1,0:T(8,128)S(1)} custom-call(f32[64,16,128]{2,1,0:T(8,128)S(1)} %collective-permute-done.11.refs_0_, f32[64,16,128]{2,1,0:T(8,128)S(1)} %collective-permute-done.12.refs_1_, f32[128,48,128]{2,1,0:T(8,128)S(1)} %local_part.3.refs_2_, bf16[48,256]{1,0:T(8,128)(2,1)S(1)} %get-tuple-element.33.refs_3_, ...), custom_call_target="tpu_custom_call" | custom-call | tf_op jit(solution)/shard_map/forward_part/pallas_call | solution.py:314
  103.7 1.9 %quotient_part.3.field = f32[6272,128]{1,0:T(8,128)S(1)} custom-call(f32[6192,128]{1,0:T(8,128)S(1)} %forward_part.3.refs_0_, f32[48,128,128]{2,1,0:T(8,128)S(1)} %get-tuple-element.35.refs_1_, bf16[3,128,384]{2,1,0:T(8,128)(2,1)S(1)} %get-tuple-element.36.refs_2_, bf16[3,128,384]{2,1,0:T(8,128)(2,1)S(1)} %get-tuple-element.37.refs_3_), custom_call_target="tpu_custom_call" | custom-call | tf_op jit(solution)/shard_map/quotient_part/pallas_call | solution.py:368
  105.6 1.0 backward_part.7
  106.7 1.0 backward_part.6
  107.7 0.1 collective-permute-start.17
  107.8 1.9 %collective-permute-start.18 = (f32[64,16,128]{2,1,0:T(8,128)S(1)}, f32[64,16,128]{2,1,0:T(8,128)S(1)}, u32[]{:S(2)}, u32[]{:S(2)}) collective-permute-start(f32[64,16,128]{2,1,0:T(8,128)S(1)} %get-tuple-element.54), channel_id=1, source_target_pairs={{3,4},{4,3},{7,8},{8,7},{11,12},{12,11},{1,2},{2,1},{5,6},{6,5},{9... | collective-permute-start | bytes 1572872 | tf_op jit(solution)/shard_map/ppermute | solution.py:478
  109.7 0.6 collective-permute-start.15
  110.2 4.7 %collective-permute-start.16 = (f32[64,16,128]{2,1,0:T(8,128)S(1)}, f32[64,16,128]{2,1,0:T(8,128)S(1)}, u32[]{:S(2)}, u32[]{:S(2)}) collective-permute-start(f32[64,16,128]{2,1,0:T(8,128)S(1)} %get-tuple-element.51), channel_id=1, source_target_pairs={{3,4},{4,3},{7,8},{8,7},{11,12},{12,11},{1,2},{2,1},{5,6},{6,5},{9... | collective-permute-start | bytes 1572872 | tf_op jit(solution)/shard_map/ppermute | solution.py:478
  115.0 14.5 %collective-permute-done.18.far = f32[64,16,128]{2,1,0:T(8,128)S(1)} collective-permute-done((f32[64,16,128]{2,1,0:T(8,128)S(1)}, f32[64,16,128]{2,1,0:T(8,128)S(1)}, u32[]{:S(2)}, u32[]{:S(2)}) %collective-permute-start.18) | collective-permute-done | bytes 524320 | tf_op jit(solution)/shard_map/ppermute | solution.py:478
  129.5 0.9 finish_part.2.refs_0_
  130.5 4.7 %collective-permute-done.16.far = f32[64,16,128]{2,1,0:T(8,128)S(1)} collective-permute-done((f32[64,16,128]{2,1,0:T(8,128)S(1)}, f32[64,16,128]{2,1,0:T(8,128)S(1)}, u32[]{:S(2)}, u32[]{:S(2)}) %collective-permute-start.16) | collective-permute-done | bytes 524320 | tf_op jit(solution)/shard_map/ppermute | solution.py:478
  135.1 0.9 finish_part.3
  (12 shorter events, 0.0 us)
Async XLA Ops:
  0.0 3.8 %copy-start = (f32[16,128,128]{2,1,0:T(8,128)S(1)}, f32[16,128,128]{2,1,0:T(8,128)}, u32[]{:S(2)}) copy-start(f32[16,128,128]{2,1,0:T(8,128)} %refs_0_.1) | copy-start | bytes 3145732
  0.0 36.1 %collective-permute-start.2 = (f32[16,128,128]{2,1,0:T(8,128)}, f32[16,128,128]{2,1,0:T(8,128)S(1)}, u32[]{:S(2)}, u32[]{:S(2)}) collective-permute-start(f32[16,128,128]{2,1,0:T(8,128)} %refs_0_.1), channel_id=1, source_target_pairs={{0,1},{1,0},{2,3},{3,2},{4,5},{5,4},{6,7},{7,6},{8,9},{9,8},{10,11... | collective-permute-start | bytes 3145736 | tf_op jit(solution)/shard_map/ppermute | solution.py:478
  3.8 32.9 %collective-permute-start.1 = (f32[16,128,128]{2,1,0:T(8,128)S(1)}, f32[16,128,128]{2,1,0:T(8,128)S(1)}, u32[]{:S(2)}, u32[]{:S(2)}) collective-permute-start(f32[16,128,128]{2,1,0:T(8,128)S(1)} %copy-done), channel_id=1, source_target_pairs={{1,2},{2,1},{5,6},{6,5},{9,10},{10,9},{13,14},{14,13},{17,18},{18,... | collective-permute-start | bytes 3145736 | tf_op jit(solution)/shard_map/ppermute | solution.py:478
  7.0 29.8 %collective-permute-start = (f32[16,128,128]{2,1,0:T(8,128)S(1)}, f32[16,128,128]{2,1,0:T(8,128)S(1)}, u32[]{:S(2)}, u32[]{:S(2)}) collective-permute-start(f32[16,128,128]{2,1,0:T(8,128)S(1)} %copy-done), channel_id=1, source_target_pairs={{3,4},{4,3},{7,8},{8,7},{11,12},{12,11},{19,20},{20,19},{23,24},{2... | collective-permute-start | bytes 3145736 | tf_op jit(solution)/shard_map/ppermute | solution.py:478
  7.7 1.2 collective-permute-start.3
  8.9 21.2 %collective-permute-start.4 = (f32[8,256]{1,0:T(8,128)S(1)}, f32[8,256]{1,0:T(8,128)S(1)}, u32[]{:S(2)}, u32[]{:S(2)}) collective-permute-start(f32[8,256]{1,0:T(8,128)S(1)} %add.24), channel_id=1, source_target_pairs={{0,2},{1,3},{2,0},{3,1},{4,6},{5,7},{6,4},{7,5},{8,10},{9,11},{10,... | collective-permute-start | bytes 24584 | tf_op jit(solution)/shard_map/ppermute | solution.py:192
  30.1 2.5 %collective-permute-start.5 = (f32[8,256]{1,0:T(8,128)S(1)}, f32[8,256]{1,0:T(8,128)S(1)}, u32[]{:S(2)}, u32[]{:S(2)}) collective-permute-start(f32[8,256]{1,0:T(8,128)S(1)} %add.25), channel_id=1, source_target_pairs={{0,4},{1,5},{2,6},{3,7},{4,0},{5,1},{6,2},{7,3},{8,12},{9,13},{10,... | collective-permute-start | bytes 24584 | tf_op jit(solution)/shard_map/ppermute | solution.py:192
  32.6 3.5 %collective-permute-start.6 = (f32[8,256]{1,0:T(8,128)S(1)}, f32[8,256]{1,0:T(8,128)S(1)}, u32[]{:S(2)}, u32[]{:S(2)}) collective-permute-start(f32[8,256]{1,0:T(8,128)S(1)} %add.26), channel_id=1, source_target_pairs={{0,8},{1,9},{2,10},{3,11},{4,12},{5,13},{6,14},{7,15},{8,0},{9,1},... | collective-permute-start | bytes 24584 | tf_op jit(solution)/shard_map/ppermute | solution.py:192
  41.9 11.9 %collective-permute-start.8 = (f32[64,16,128]{2,1,0:T(8,128)S(1)}, f32[64,16,128]{2,1,0:T(8,128)S(1)}, u32[]{:S(2)}, u32[]{:S(2)}) collective-permute-start(f32[64,16,128]{2,1,0:T(8,128)S(1)} %get-tuple-element.44), channel_id=1, source_target_pairs={{0,1},{1,0},{2,3},{3,2},{4,5},{5,4},{6,7},{7,6},{8,9},{9,8},{10,11... | collective-permute-start | bytes 1572872 | tf_op jit(solution)/shard_map/ppermute | solution.py:478
  46.1 21.7 %collective-permute-start.9 = (f32[64,16,128]{2,1,0:T(8,128)S(1)}, f32[64,16,128]{2,1,0:T(8,128)S(1)}, u32[]{:S(2)}, u32[]{:S(2)}) collective-permute-start(f32[64,16,128]{2,1,0:T(8,128)S(1)} %get-tuple-element.45), channel_id=1, source_target_pairs={{3,4},{4,3},{7,8},{8,7},{11,12},{12,11},{1,2},{2,1},{5,6},{6,5},{9... | collective-permute-start | bytes 1572872 | tf_op jit(solution)/shard_map/ppermute | solution.py:478
  49.0 24.4 %collective-permute-start.10 = (f32[64,16,128]{2,1,0:T(8,128)S(1)}, f32[64,16,128]{2,1,0:T(8,128)S(1)}, u32[]{:S(2)}, u32[]{:S(2)}) collective-permute-start(f32[64,16,128]{2,1,0:T(8,128)S(1)} %get-tuple-element.46), channel_id=1, source_target_pairs={{3,4},{4,3},{7,8},{8,7},{11,12},{12,11},{1,2},{2,1},{5,6},{6,5},{9... | collective-permute-start | bytes 1572872 | tf_op jit(solution)/shard_map/ppermute | solution.py:478
  52.7 20.8 %collective-permute-start.7 = (f32[64,16,128]{2,1,0:T(8,128)S(1)}, f32[64,16,128]{2,1,0:T(8,128)S(1)}, u32[]{:S(2)}, u32[]{:S(2)}) collective-permute-start(f32[64,16,128]{2,1,0:T(8,128)S(1)} %get-tuple-element.42), channel_id=1, source_target_pairs={{0,1},{1,0},{2,3},{3,2},{4,5},{5,4},{6,7},{7,6},{8,9},{9,8},{10,11... | collective-permute-start | bytes 1572872 | tf_op jit(solution)/shard_map/ppermute | solution.py:478
  73.9 6.3 %collective-permute-start.14 = (f32[64,16,128]{2,1,0:T(8,128)S(1)}, f32[64,16,128]{2,1,0:T(8,128)S(1)}, u32[]{:S(2)}, u32[]{:S(2)}) collective-permute-start(f32[64,16,128]{2,1,0:T(8,128)S(1)} %fusion.3.refs_1_.before), channel_id=1, source_target_pairs={{0,1},{1,0},{2,3},{3,2},{4,5},{5,4},{6,7},{7,6},{8,9},{9,8},{10,11... | collective-permute-start | bytes 1572872 | tf_op jit(solution)/shard_map/ppermute | solution.py:478
  73.9 6.3 %collective-permute-start.13 = (f32[64,16,128]{2,1,0:T(8,128)S(1)}, f32[64,16,128]{2,1,0:T(8,128)S(1)}, u32[]{:S(2)}, u32[]{:S(2)}) collective-permute-start(f32[64,16,128]{2,1,0:T(8,128)S(1)} %fusion.1.refs_0_.before), channel_id=1, source_target_pairs={{0,1},{1,0},{2,3},{3,2},{4,5},{5,4},{6,7},{7,6},{8,9},{9,8},{10,11... | collective-permute-start | bytes 1572872 | tf_op jit(solution)/shard_map/ppermute | solution.py:478
  74.4 21.7 %collective-permute-start.12 = (f32[64,16,128]{2,1,0:T(8,128)S(1)}, f32[64,16,128]{2,1,0:T(8,128)S(1)}, u32[]{:S(2)}, u32[]{:S(2)}) collective-permute-start(f32[64,16,128]{2,1,0:T(8,128)S(1)} %fusion.3.refs_1_.before), channel_id=1, source_target_pairs={{3,4},{4,3},{7,8},{8,7},{11,12},{12,11},{1,2},{2,1},{5,6},{6,5},{9... | collective-permute-start | bytes 1572872 | tf_op jit(solution)/shard_map/ppermute | solution.py:478
  76.3 25.4 %collective-permute-start.11 = (f32[64,16,128]{2,1,0:T(8,128)S(1)}, f32[64,16,128]{2,1,0:T(8,128)S(1)}, u32[]{:S(2)}, u32[]{:S(2)}) collective-permute-start(f32[64,16,128]{2,1,0:T(8,128)S(1)} %fusion.1.refs_0_.before), channel_id=1, source_target_pairs={{3,4},{4,3},{7,8},{8,7},{11,12},{12,11},{1,2},{2,1},{5,6},{6,5},{9... | collective-permute-start | bytes 1572872 | tf_op jit(solution)/shard_map/ppermute | solution.py:478
  107.7 7.3 %collective-permute-start.17 = (f32[64,16,128]{2,1,0:T(8,128)S(1)}, f32[64,16,128]{2,1,0:T(8,128)S(1)}, u32[]{:S(2)}, u32[]{:S(2)}) collective-permute-start(f32[64,16,128]{2,1,0:T(8,128)S(1)} %get-tuple-element.53), channel_id=1, source_target_pairs={{0,1},{1,0},{2,3},{3,2},{4,5},{5,4},{6,7},{7,6},{8,9},{9,8},{10,11... | collective-permute-start | bytes 1572872 | tf_op jit(solution)/shard_map/ppermute | solution.py:478
  107.8 21.7 %collective-permute-start.18 = (f32[64,16,128]{2,1,0:T(8,128)S(1)}, f32[64,16,128]{2,1,0:T(8,128)S(1)}, u32[]{:S(2)}, u32[]{:S(2)}) collective-permute-start(f32[64,16,128]{2,1,0:T(8,128)S(1)} %get-tuple-element.54), channel_id=1, source_target_pairs={{3,4},{4,3},{7,8},{8,7},{11,12},{12,11},{1,2},{2,1},{5,6},{6,5},{9... | collective-permute-start | bytes 1572872 | tf_op jit(solution)/shard_map/ppermute | solution.py:478
  109.7 20.8 %collective-permute-start.15 = (f32[64,16,128]{2,1,0:T(8,128)S(1)}, f32[64,16,128]{2,1,0:T(8,128)S(1)}, u32[]{:S(2)}, u32[]{:S(2)}) collective-permute-start(f32[64,16,128]{2,1,0:T(8,128)S(1)} %get-tuple-element.50), channel_id=1, source_target_pairs={{0,1},{1,0},{2,3},{3,2},{4,5},{5,4},{6,7},{7,6},{8,9},{9,8},{10,11... | collective-permute-start | bytes 1572872 | tf_op jit(solution)/shard_map/ppermute | solution.py:478
  110.2 24.9 %collective-permute-start.16 = (f32[64,16,128]{2,1,0:T(8,128)S(1)}, f32[64,16,128]{2,1,0:T(8,128)S(1)}, u32[]{:S(2)}, u32[]{:S(2)}) collective-permute-start(f32[64,16,128]{2,1,0:T(8,128)S(1)} %get-tuple-element.51), channel_id=1, source_target_pairs={{3,4},{4,3},{7,8},{8,7},{11,12},{12,11},{1,2},{2,1},{5,6},{6,5},{9... | collective-permute-start | bytes 1572872 | tf_op jit(solution)/shard_map/ppermute | solution.py:478

commit v7 on v6

--- a/solution.py
+++ b/solution.py
@@ -10,6 +10,7 @@
 
 ITERS = 2
 GROUP = 8
+SENT = 4
 CHUNKS = 2
 VMEM_LIMIT = 16 << 20
 ROWS = 64
@@ -438,11 +439,16 @@
     for i in range(chunk):
         total = own[i] + near[i] + far[i]
         spread_out[pl.ds(i, block_len, stride=spread), :] = before[i] * total / view_count
+    copies = []
     for z in range(block_len):
         turned[z] = spread_out[pl.ds(z * spread, chunk), :]
-    copy = pltpu.make_async_copy(turned, out.at[:, pl.ds(first, chunk), :], sem)
-    copy.start()
-    copy.wait()
+        if (z + 1) % SENT == 0:
+            part = pl.ds(z + 1 - SENT, SENT)
+            target = out.at[part, pl.ds(first, chunk), :]
+            copies.append(pltpu.make_async_copy(turned.at[part], target, sem.at[len(copies)]))
+            copies[-1].start()
+    for copy in copies:
+        copy.wait()
 
 
 def finish_part(before, own, near, far, result, first, size_x, view_count):
@@ -458,7 +464,7 @@
         scratch_shapes=[
             pltpu.VMEM((block_len * (chunk + 1), size_y), F32),
             pltpu.VMEM((block_len, chunk, size_y), F32),
-            pltpu.SemaphoreType.DMA,
+            pltpu.SemaphoreType.DMA((block_len // SENT,)),
         ],
         input_output_aliases={4: 0} if extra else {},
         compiler_params=pltpu.CompilerParams(vmem_limit_bytes=VMEM_LIMIT),

time: 137 us -> 137 us (level)
  no operation moved by 1% of the time
where the time goes in v7:
time: 137 us; the launch traced here: 136 us
  waiting for transfers between devices  84.7 us (62%)
  starting transfers between devices  32 us (23%)
  Pallas kernels  18.2 us (13%)
    ppermute x15, waiting for transfers between devices, swap(): return lax.ppermute(value, 'slab', pairs)  59.4 us
    ppermute x15, starting transfers between devices, swap(): return lax.ppermute(value, 'slab', pairs)  28.9 us
    ppermute x4, waiting for transfers between devices, summed(): lax.ppermute(value, axis, [(i, i ^ step) for i in range(count)])  25.3 us
    pallas_call x4, Pallas kernels, backward_part(): pl.pallas_call(functools.partial(backward_kernel, block_len=block_len, of...  4.12 us
    pallas_call x2, Pallas kernels, forward_part(): pl.pallas_call(functools.partial(forward_kernel, block_len=block_len, tur...  4.03 us
    pallas_call x2, Pallas kernels, quotient_part(): pl.pallas_call(functools.partial(quotient_kernel, chunks=len(parts), bloc...  3.87 us
    pallas_call x1, Pallas kernels, prepare(): pl.pallas_call(functools.partial(prepare_kernel, count=lax.axis_size(axis...  3.13 us
    ppermute x4, starting transfers between devices, summed(): lax.ppermute(value, axis, [(i, i ^ step) for i in range(count)])  3.09 us
  transfers between devices with their start and end apart: 19, of which 10 were waited for; matrix products, arithmetic and copies ran while one was open for 0% of the time, Pallas kernels for 5%

profile of v7, /device:TPU:11, one launch (start us, length us, event | category | flops | bytes accessed | tf_op | source)
XLA Modules:
  0.0 136.2 jit_solution(14029958069725985186)
XLA Ops:
  0.0 0.7 collective-permute-start.2
  0.7 3.1 %prepare.1 = (bf16[3,128,384]{2,1,0:T(8,128)(2,1)S(1)}, bf16[3,128,384]{2,1,0:T(8,128)(2,1)S(1)}, bf16[3,256,256]{2,1,0:T(8,128)(2,1)S(1)}, bf16[3,256,256]{2,1,...) custom-call(s32[1]{0:T(128)} %bitcast.1.position, ...), custom_call_target="tpu_custom_call" | custom-call | tf_op jit(solution)/shard_map/prepare/pallas_call | solution.py:157
  3.8 3.1 %collective-permute-start.1 = (f32[16,128,128]{2,1,0:T(8,128)S(1)}, f32[16,128,128]{2,1,0:T(8,128)S(1)}, u32[]{:S(2)}, u32[]{:S(2)}) collective-permute-start(f32[16,128,128]{2,1,0:T(8,128)S(1)} %copy-done), channel_id=1, source_target_pairs={{1,2},{2,1},{5,6},{6,5},{9,10},{10,9},{13,14},{14,13},{17,18},{18,... | collective-permute-start | bytes 3145736 | tf_op jit(solution)/shard_map/ppermute | solution.py:484
  7.0 0.7 collective-permute-start
  7.7 0.4 collective-permute-start.3
  8.1 0.9 collective-permute-done.3
  8.9 1.2 collective-permute-start.4
  10.2 19.9 %collective-permute-done.4 = f32[8,256]{1,0:T(8,128)S(1)} collective-permute-done((f32[8,256]{1,0:T(8,128)S(1)}, f32[8,256]{1,0:T(8,128)S(1)}, u32[]{:S(2)}, u32[]{:S(2)}) %collective-permute-start.4) | collective-permute-done | bytes 8224 | tf_op jit(solution)/shard_map/ppermute | solution.py:193
  30.1 0.2 collective-permute-start.5
  30.3 2.3 %collective-permute-done.5 = f32[8,256]{1,0:T(8,128)S(1)} collective-permute-done((f32[8,256]{1,0:T(8,128)S(1)}, f32[8,256]{1,0:T(8,128)S(1)}, u32[]{:S(2)}, u32[]{:S(2)}) %collective-permute-start.5) | collective-permute-done | bytes 8224 | tf_op jit(solution)/shard_map/ppermute | solution.py:193
  32.6 1.3 collective-permute-start.6
  33.9 2.2 %collective-permute-done.6 = f32[8,256]{1,0:T(8,128)S(1)} collective-permute-done((f32[8,256]{1,0:T(8,128)S(1)}, f32[8,256]{1,0:T(8,128)S(1)}, u32[]{:S(2)}, u32[]{:S(2)}) %collective-permute-start.6) | collective-permute-done | bytes 8224 | tf_op jit(solution)/shard_map/ppermute | solution.py:193
  36.1 0.6 local_part.2.refs_2_
  36.7 0.0 collective-permute-done.refs_0_
  36.8 2.1 %forward_part.2.refs_0_ = f32[6192,128]{1,0:T(8,128)S(1)} custom-call(f32[16,128,128]{2,1,0:T(8,128)S(1)} %collective-permute-done.refs_0_, f32[16,128,128]{2,1,0:T(8,128)S(1)} %collective-permute-done.1.refs_1_, f32[128,48,128]{2,1,0:T(8,128)S(1)} %local_part.2.refs_2_, bf16[48,256]{1,0:T(8,128)(2,1)S(1)} %get-tuple-element.33.refs_3_, ...), custom_call_target="tpu_custom_call" | custom-call | tf_op jit(solution)/shard_map/forward_part/pallas_call | solution.py:315
  38.9 1.9 %quotient_part.2.field = f32[6272,128]{1,0:T(8,128)S(1)} custom-call(f32[6192,128]{1,0:T(8,128)S(1)} %forward_part.2.refs_0_, f32[48,128,128]{2,1,0:T(8,128)S(1)} %get-tuple-element.35.refs_1_, bf16[3,128,384]{2,1,0:T(8,128)(2,1)S(1)} %get-tuple-element.36.refs_2_, bf16[3,128,384]{2,1,0:T(8,128)(2,1)S(1)} %get-tuple-element.37.refs_3_), custom_call_target="tpu_custom_call" | custom-call | tf_op jit(solution)/shard_map/quotient_part/pallas_call | solution.py:369
  40.8 1.0 backward_part.5
  41.9 4.2 %collective-permute-start.8 = (f32[64,16,128]{2,1,0:T(8,128)S(1)}, f32[64,16,128]{2,1,0:T(8,128)S(1)}, u32[]{:S(2)}, u32[]{:S(2)}) collective-permute-start(f32[64,16,128]{2,1,0:T(8,128)S(1)} %get-tuple-element.44), channel_id=1, source_target_pairs={{0,1},{1,0},{2,3},{3,2},{4,5},{5,4},{6,7},{7,6},{8,9},{9,8},{10,11... | collective-permute-start | bytes 1572872 | tf_op jit(solution)/shard_map/ppermute | solution.py:484
  46.1 1.9 %collective-permute-start.9 = (f32[64,16,128]{2,1,0:T(8,128)S(1)}, f32[64,16,128]{2,1,0:T(8,128)S(1)}, u32[]{:S(2)}, u32[]{:S(2)}) collective-permute-start(f32[64,16,128]{2,1,0:T(8,128)S(1)} %get-tuple-element.45), channel_id=1, source_target_pairs={{3,4},{4,3},{7,8},{8,7},{11,12},{12,11},{1,2},{2,1},{5,6},{6,5},{9... | collective-permute-start | bytes 1572872 | tf_op jit(solution)/shard_map/ppermute | solution.py:484
  48.0 1.0 backward_part.4
  49.0 3.6 %collective-permute-start.10 = (f32[64,16,128]{2,1,0:T(8,128)S(1)}, f32[64,16,128]{2,1,0:T(8,128)S(1)}, u32[]{:S(2)}, u32[]{:S(2)}) collective-permute-start(f32[64,16,128]{2,1,0:T(8,128)S(1)} %get-tuple-element.46), channel_id=1, source_target_pairs={{3,4},{4,3},{7,8},{8,7},{11,12},{12,11},{1,2},{2,1},{5,6},{6,5},{9... | collective-permute-start | bytes 1572872 | tf_op jit(solution)/shard_map/ppermute | solution.py:484
  52.7 1.0 collective-permute-start.7
  53.7 0.1 fusion.4
  53.8 0.0 collective-permute-done.8
  53.8 14.0 %collective-permute-done.9 = f32[64,16,128]{2,1,0:T(8,128)S(1)} collective-permute-done((f32[64,16,128]{2,1,0:T(8,128)S(1)}, f32[64,16,128]{2,1,0:T(8,128)S(1)}, u32[]{:S(2)}, u32[]{:S(2)}) %collective-permute-start.9) | collective-permute-done | bytes 524320 | tf_op jit(solution)/shard_map/ppermute | solution.py:484
  67.8 0.4 fusion.1.refs_0_.before
  68.2 5.2 %collective-permute-done.10 = f32[64,16,128]{2,1,0:T(8,128)S(1)} collective-permute-done((f32[64,16,128]{2,1,0:T(8,128)S(1)}, f32[64,16,128]{2,1,0:T(8,128)S(1)}, u32[]{:S(2)}, u32[]{:S(2)}) %collective-permute-start.10) | collective-permute-done | bytes 524320 | tf_op jit(solution)/shard_map/ppermute | solution.py:484
  73.4 0.0 collective-permute-done.7
  73.4 0.4 fusion.3.refs_1_.before
  73.9 0.1 collective-permute-start.14
  73.9 0.5 collective-permute-start.13
  74.4 1.9 %collective-permute-start.12 = (f32[64,16,128]{2,1,0:T(8,128)S(1)}, f32[64,16,128]{2,1,0:T(8,128)S(1)}, u32[]{:S(2)}, u32[]{:S(2)}) collective-permute-start(f32[64,16,128]{2,1,0:T(8,128)S(1)} %fusion.3.refs_1_.before), channel_id=1, source_target_pairs={{3,4},{4,3},{7,8},{8,7},{11,12},{12,11},{1,2},{2,1},{5,6},{6,5},{9... | collective-permute-start | bytes 1572872 | tf_op jit(solution)/shard_map/ppermute | solution.py:484
  76.3 3.8 %collective-permute-start.11 = (f32[64,16,128]{2,1,0:T(8,128)S(1)}, f32[64,16,128]{2,1,0:T(8,128)S(1)}, u32[]{:S(2)}, u32[]{:S(2)}) collective-permute-start(f32[64,16,128]{2,1,0:T(8,128)S(1)} %fusion.1.refs_0_.before), channel_id=1, source_target_pairs={{3,4},{4,3},{7,8},{8,7},{11,12},{12,11},{1,2},{2,1},{5,6},{6,5},{9... | collective-permute-start | bytes 1572872 | tf_op jit(solution)/shard_map/ppermute | solution.py:484
  80.2 0.6 local_part.3.refs_2_
  80.8 15.4 %collective-permute-done.12.refs_1_ = f32[64,16,128]{2,1,0:T(8,128)S(1)} collective-permute-done((f32[64,16,128]{2,1,0:T(8,128)S(1)}, f32[64,16,128]{2,1,0:T(8,128)S(1)}, u32[]{:S(2)}, u32[]{:S(2)}) %collective-permute-start.12) | collective-permute-done | bytes 524320 | tf_op jit(solution)/shard_map/ppermute | solution.py:484
  96.2 5.6 %collective-permute-done.11.refs_0_ = f32[64,16,128]{2,1,0:T(8,128)S(1)} collective-permute-done((f32[64,16,128]{2,1,0:T(8,128)S(1)}, f32[64,16,128]{2,1,0:T(8,128)S(1)}, u32[]{:S(2)}, u32[]{:S(2)}) %collective-permute-start.11) | collective-permute-done | bytes 524320 | tf_op jit(solution)/shard_map/ppermute | solution.py:484
  101.8 1.9 %forward_part.3.refs_0_ = f32[6192,128]{1,0:T(8,128)S(1)} custom-call(f32[64,16,128]{2,1,0:T(8,128)S(1)} %collective-permute-done.11.refs_0_, f32[64,16,128]{2,1,0:T(8,128)S(1)} %collective-permute-done.12.refs_1_, f32[128,48,128]{2,1,0:T(8,128)S(1)} %local_part.3.refs_2_, bf16[48,256]{1,0:T(8,128)(2,1)S(1)} %get-tuple-element.33.refs_3_, ...), custom_call_target="tpu_custom_call" | custom-call | tf_op jit(solution)/shard_map/forward_part/pallas_call | solution.py:315
  103.7 1.9 %quotient_part.3.field = f32[6272,128]{1,0:T(8,128)S(1)} custom-call(f32[6192,128]{1,0:T(8,128)S(1)} %forward_part.3.refs_0_, f32[48,128,128]{2,1,0:T(8,128)S(1)} %get-tuple-element.35.refs_1_, bf16[3,128,384]{2,1,0:T(8,128)(2,1)S(1)} %get-tuple-element.36.refs_2_, bf16[3,128,384]{2,1,0:T(8,128)(2,1)S(1)} %get-tuple-element.37.refs_3_), custom_call_target="tpu_custom_call" | custom-call | tf_op jit(solution)/shard_map/quotient_part/pallas_call | solution.py:369
  105.6 1.0 backward_part.7
  106.7 1.0 backward_part.6
  107.7 0.1 collective-permute-start.17
  107.8 1.9 %collective-permute-start.18 = (f32[64,16,128]{2,1,0:T(8,128)S(1)}, f32[64,16,128]{2,1,0:T(8,128)S(1)}, u32[]{:S(2)}, u32[]{:S(2)}) collective-permute-start(f32[64,16,128]{2,1,0:T(8,128)S(1)} %get-tuple-element.54), channel_id=1, source_target_pairs={{3,4},{4,3},{7,8},{8,7},{11,12},{12,11},{1,2},{2,1},{5,6},{6,5},{9... | collective-permute-start | bytes 1572872 | tf_op jit(solution)/shard_map/ppermute | solution.py:484
  109.7 0.6 collective-permute-start.15
  110.2 4.7 %collective-permute-start.16 = (f32[64,16,128]{2,1,0:T(8,128)S(1)}, f32[64,16,128]{2,1,0:T(8,128)S(1)}, u32[]{:S(2)}, u32[]{:S(2)}) collective-permute-start(f32[64,16,128]{2,1,0:T(8,128)S(1)} %get-tuple-element.51), channel_id=1, source_target_pairs={{3,4},{4,3},{7,8},{8,7},{11,12},{12,11},{1,2},{2,1},{5,6},{6,5},{9... | collective-permute-start | bytes 1572872 | tf_op jit(solution)/shard_map/ppermute | solution.py:484
  115.0 14.5 %collective-permute-done.18.far = f32[64,16,128]{2,1,0:T(8,128)S(1)} collective-permute-done((f32[64,16,128]{2,1,0:T(8,128)S(1)}, f32[64,16,128]{2,1,0:T(8,128)S(1)}, u32[]{:S(2)}, u32[]{:S(2)}) %collective-permute-start.18) | collective-permute-done | bytes 524320 | tf_op jit(solution)/shard_map/ppermute | solution.py:484
  129.5 0.9 finish_part.2.refs_0_
  130.5 4.7 %collective-permute-done.16.far = f32[64,16,128]{2,1,0:T(8,128)S(1)} collective-permute-done((f32[64,16,128]{2,1,0:T(8,128)S(1)}, f32[64,16,128]{2,1,0:T(8,128)S(1)}, u32[]{:S(2)}, u32[]{:S(2)}) %collective-permute-start.16) | collective-permute-done | bytes 524320 | tf_op jit(solution)/shard_map/ppermute | solution.py:484
  135.1 0.9 finish_part.3
  (12 shorter events, 0.0 us)
Async XLA Ops:
  0.0 3.8 %copy-start = (f32[16,128,128]{2,1,0:T(8,128)S(1)}, f32[16,128,128]{2,1,0:T(8,128)}, u32[]{:S(2)}) copy-start(f32[16,128,128]{2,1,0:T(8,128)} %refs_0_.1) | copy-start | bytes 3145732
  0.0 36.1 %collective-permute-start.2 = (f32[16,128,128]{2,1,0:T(8,128)}, f32[16,128,128]{2,1,0:T(8,128)S(1)}, u32[]{:S(2)}, u32[]{:S(2)}) collective-permute-start(f32[16,128,128]{2,1,0:T(8,128)} %refs_0_.1), channel_id=1, source_target_pairs={{0,1},{1,0},{2,3},{3,2},{4,5},{5,4},{6,7},{7,6},{8,9},{9,8},{10,11... | collective-permute-start | bytes 3145736 | tf_op jit(solution)/shard_map/ppermute | solution.py:484
  3.8 32.9 %collective-permute-start.1 = (f32[16,128,128]{2,1,0:T(8,128)S(1)}, f32[16,128,128]{2,1,0:T(8,128)S(1)}, u32[]{:S(2)}, u32[]{:S(2)}) collective-permute-start(f32[16,128,128]{2,1,0:T(8,128)S(1)} %copy-done), channel_id=1, source_target_pairs={{1,2},{2,1},{5,6},{6,5},{9,10},{10,9},{13,14},{14,13},{17,18},{18,... | collective-permute-start | bytes 3145736 | tf_op jit(solution)/shard_map/ppermute | solution.py:484
  7.0 29.8 %collective-permute-start = (f32[16,128,128]{2,1,0:T(8,128)S(1)}, f32[16,128,128]{2,1,0:T(8,128)S(1)}, u32[]{:S(2)}, u32[]{:S(2)}) collective-permute-start(f32[16,128,128]{2,1,0:T(8,128)S(1)} %copy-done), channel_id=1, source_target_pairs={{3,4},{4,3},{7,8},{8,7},{11,12},{12,11},{19,20},{20,19},{23,24},{2... | collective-permute-start | bytes 3145736 | tf_op jit(solution)/shard_map/ppermute | solution.py:484
  7.7 1.2 collective-permute-start.3
  8.9 21.2 %collective-permute-start.4 = (f32[8,256]{1,0:T(8,128)S(1)}, f32[8,256]{1,0:T(8,128)S(1)}, u32[]{:S(2)}, u32[]{:S(2)}) collective-permute-start(f32[8,256]{1,0:T(8,128)S(1)} %add.24), channel_id=1, source_target_pairs={{0,2},{1,3},{2,0},{3,1},{4,6},{5,7},{6,4},{7,5},{8,10},{9,11},{10,... | collective-permute-start | bytes 24584 | tf_op jit(solution)/shard_map/ppermute | solution.py:193
  30.1 2.5 %collective-permute-start.5 = (f32[8,256]{1,0:T(8,128)S(1)}, f32[8,256]{1,0:T(8,128)S(1)}, u32[]{:S(2)}, u32[]{:S(2)}) collective-permute-start(f32[8,256]{1,0:T(8,128)S(1)} %add.25), channel_id=1, source_target_pairs={{0,4},{1,5},{2,6},{3,7},{4,0},{5,1},{6,2},{7,3},{8,12},{9,13},{10,... | collective-permute-start | bytes 24584 | tf_op jit(solution)/shard_map/ppermute | solution.py:193
  32.6 3.5 %collective-permute-start.6 = (f32[8,256]{1,0:T(8,128)S(1)}, f32[8,256]{1,0:T(8,128)S(1)}, u32[]{:S(2)}, u32[]{:S(2)}) collective-permute-start(f32[8,256]{1,0:T(8,128)S(1)} %add.26), channel_id=1, source_target_pairs={{0,8},{1,9},{2,10},{3,11},{4,12},{5,13},{6,14},{7,15},{8,0},{9,1},... | collective-permute-start | bytes 24584 | tf_op jit(solution)/shard_map/ppermute | solution.py:193
  41.9 11.9 %collective-permute-start.8 = (f32[64,16,128]{2,1,0:T(8,128)S(1)}, f32[64,16,128]{2,1,0:T(8,128)S(1)}, u32[]{:S(2)}, u32[]{:S(2)}) collective-permute-start(f32[64,16,128]{2,1,0:T(8,128)S(1)} %get-tuple-element.44), channel_id=1, source_target_pairs={{0,1},{1,0},{2,3},{3,2},{4,5},{5,4},{6,7},{7,6},{8,9},{9,8},{10,11... | collective-permute-start | bytes 1572872 | tf_op jit(solution)/shard_map/ppermute | solution.py:484
  46.1 21.7 %collective-permute-start.9 = (f32[64,16,128]{2,1,0:T(8,128)S(1)}, f32[64,16,128]{2,1,0:T(8,128)S(1)}, u32[]{:S(2)}, u32[]{:S(2)}) collective-permute-start(f32[64,16,128]{2,1,0:T(8,128)S(1)} %get-tuple-element.45), channel_id=1, source_target_pairs={{3,4},{4,3},{7,8},{8,7},{11,12},{12,11},{1,2},{2,1},{5,6},{6,5},{9... | collective-permute-start | bytes 1572872 | tf_op jit(solution)/shard_map/ppermute | solution.py:484
  49.0 24.4 %collective-permute-start.10 = (f32[64,16,128]{2,1,0:T(8,128)S(1)}, f32[64,16,128]{2,1,0:T(8,128)S(1)}, u32[]{:S(2)}, u32[]{:S(2)}) collective-permute-start(f32[64,16,128]{2,1,0:T(8,128)S(1)} %get-tuple-element.46), channel_id=1, source_target_pairs={{3,4},{4,3},{7,8},{8,7},{11,12},{12,11},{1,2},{2,1},{5,6},{6,5},{9... | collective-permute-start | bytes 1572872 | tf_op jit(solution)/shard_map/ppermute | solution.py:484
  52.7 20.8 %collective-permute-start.7 = (f32[64,16,128]{2,1,0:T(8,128)S(1)}, f32[64,16,128]{2,1,0:T(8,128)S(1)}, u32[]{:S(2)}, u32[]{:S(2)}) collective-permute-start(f32[64,16,128]{2,1,0:T(8,128)S(1)} %get-tuple-element.42), channel_id=1, source_target_pairs={{0,1},{1,0},{2,3},{3,2},{4,5},{5,4},{6,7},{7,6},{8,9},{9,8},{10,11... | collective-permute-start | bytes 1572872 | tf_op jit(solution)/shard_map/ppermute | solution.py:484
  73.9 6.3 %collective-permute-start.14 = (f32[64,16,128]{2,1,0:T(8,128)S(1)}, f32[64,16,128]{2,1,0:T(8,128)S(1)}, u32[]{:S(2)}, u32[]{:S(2)}) collective-permute-start(f32[64,16,128]{2,1,0:T(8,128)S(1)} %fusion.3.refs_1_.before), channel_id=1, source_target_pairs={{0,1},{1,0},{2,3},{3,2},{4,5},{5,4},{6,7},{7,6},{8,9},{9,8},{10,11... | collective-permute-start | bytes 1572872 | tf_op jit(solution)/shard_map/ppermute | solution.py:484
  73.9 6.3 %collective-permute-start.13 = (f32[64,16,128]{2,1,0:T(8,128)S(1)}, f32[64,16,128]{2,1,0:T(8,128)S(1)}, u32[]{:S(2)}, u32[]{:S(2)}) collective-permute-start(f32[64,16,128]{2,1,0:T(8,128)S(1)} %fusion.1.refs_0_.before), channel_id=1, source_target_pairs={{0,1},{1,0},{2,3},{3,2},{4,5},{5,4},{6,7},{7,6},{8,9},{9,8},{10,11... | collective-permute-start | bytes 1572872 | tf_op jit(solution)/shard_map/ppermute | solution.py:484
  74.4 21.7 %collective-permute-start.12 = (f32[64,16,128]{2,1,0:T(8,128)S(1)}, f32[64,16,128]{2,1,0:T(8,128)S(1)}, u32[]{:S(2)}, u32[]{:S(2)}) collective-permute-start(f32[64,16,128]{2,1,0:T(8,128)S(1)} %fusion.3.refs_1_.before), channel_id=1, source_target_pairs={{3,4},{4,3},{7,8},{8,7},{11,12},{12,11},{1,2},{2,1},{5,6},{6,5},{9... | collective-permute-start | bytes 1572872 | tf_op jit(solution)/shard_map/ppermute | solution.py:484
  76.3 25.4 %collective-permute-start.11 = (f32[64,16,128]{2,1,0:T(8,128)S(1)}, f32[64,16,128]{2,1,0:T(8,128)S(1)}, u32[]{:S(2)}, u32[]{:S(2)}) collective-permute-start(f32[64,16,128]{2,1,0:T(8,128)S(1)} %fusion.1.refs_0_.before), channel_id=1, source_target_pairs={{3,4},{4,3},{7,8},{8,7},{11,12},{12,11},{1,2},{2,1},{5,6},{6,5},{9... | collective-permute-start | bytes 1572872 | tf_op jit(solution)/shard_map/ppermute | solution.py:484
  107.7 7.3 %collective-permute-start.17 = (f32[64,16,128]{2,1,0:T(8,128)S(1)}, f32[64,16,128]{2,1,0:T(8,128)S(1)}, u32[]{:S(2)}, u32[]{:S(2)}) collective-permute-start(f32[64,16,128]{2,1,0:T(8,128)S(1)} %get-tuple-element.53), channel_id=1, source_target_pairs={{0,1},{1,0},{2,3},{3,2},{4,5},{5,4},{6,7},{7,6},{8,9},{9,8},{10,11... | collective-permute-start | bytes 1572872 | tf_op jit(solution)/shard_map/ppermute | solution.py:484
  107.8 21.7 %collective-permute-start.18 = (f32[64,16,128]{2,1,0:T(8,128)S(1)}, f32[64,16,128]{2,1,0:T(8,128)S(1)}, u32[]{:S(2)}, u32[]{:S(2)}) collective-permute-start(f32[64,16,128]{2,1,0:T(8,128)S(1)} %get-tuple-element.54), channel_id=1, source_target_pairs={{3,4},{4,3},{7,8},{8,7},{11,12},{12,11},{1,2},{2,1},{5,6},{6,5},{9... | collective-permute-start | bytes 1572872 | tf_op jit(solution)/shard_map/ppermute | solution.py:484
  109.7 20.8 %collective-permute-start.15 = (f32[64,16,128]{2,1,0:T(8,128)S(1)}, f32[64,16,128]{2,1,0:T(8,128)S(1)}, u32[]{:S(2)}, u32[]{:S(2)}) collective-permute-start(f32[64,16,128]{2,1,0:T(8,128)S(1)} %get-tuple-element.50), channel_id=1, source_target_pairs={{0,1},{1,0},{2,3},{3,2},{4,5},{5,4},{6,7},{7,6},{8,9},{9,8},{10,11... | collective-permute-start | bytes 1572872 | tf_op jit(solution)/shard_map/ppermute | solution.py:484
  110.2 24.9 %collective-permute-start.16 = (f32[64,16,128]{2,1,0:T(8,128)S(1)}, f32[64,16,128]{2,1,0:T(8,128)S(1)}, u32[]{:S(2)}, u32[]{:S(2)}) collective-permute-start(f32[64,16,128]{2,1,0:T(8,128)S(1)} %get-tuple-element.51), channel_id=1, source_target_pairs={{3,4},{4,3},{7,8},{8,7},{11,12},{12,11},{1,2},{2,1},{5,6},{6,5},{9... | collective-permute-start | bytes 1572872 | tf_op jit(solution)/shard_map/ppermute | solution.py:484

commit v8 on v7

--- a/solution.py
+++ b/solution.py
@@ -189,8 +189,14 @@
     if count & (count - 1):
         return lax.psum(value, axis)
     steps = [1 << bit for bit in range(count.bit_length() - 1)]
-    for step in steps:
-        value = value + lax.ppermute(value, axis, [(i, i ^ step) for i in range(count)])
+    rounds = [[step] for step in steps[:2]]
+    for step in steps[2::2]:
+        rounds.append([step, 2 * step, 3 * step] if 2 * step < count else [step])
+    for offsets in rounds:
+        received = []
+        for step in offsets:
+            received.append(lax.ppermute(value, axis, [(i, i ^ step) for i in range(count)]))
+        value = sum(received, value)
     return value
 
 

time: 137 us -> 135 us (0.985); the launches traced: 136 us -> 133 us
  waiting for transfers between devices: 84.7 us -> 78.1 us
  starting transfers between devices: 32 us -> 35 us
    ppermute x15, waiting for transfers between devices: 59.4 us -> 55.9 us  [swap(): return lax.ppermute(value, 'slab', pairs)]
    ppermute x4 -> x5, waiting for transfers between devices: 25.3 us -> 22.2 us  [summed(): lax.ppermute(value, axis, [(i, i ^ step) for i in range(count)])]
    ppermute x4 -> x5, starting transfers between devices: 3.09 us -> 5.38 us  [summed(): lax.ppermute(value, axis, [(i, i ^ step) for i in range(count)])]
  transfers between devices with their start and end apart: 19 -> 20, of which waited for: 10 -> 9; matrix products, arithmetic and copies ran while one was open for 0% -> 0% of each run, Pallas kernels for 5% -> 5%
where the time goes in v8:
time: 135 us; the launch traced here: 133 us
  waiting for transfers between devices  78.1 us (58%)
  starting transfers between devices  35 us (26%)
  Pallas kernels  18.3 us (14%)
    ppermute x15, waiting for transfers between devices, swap(): return lax.ppermute(value, 'slab', pairs)  55.9 us
    ppermute x15, starting transfers between devices, swap(): return lax.ppermute(value, 'slab', pairs)  29.7 us
    ppermute x5, waiting for transfers between devices, summed(): lax.ppermute(value, axis, [(i, i ^ step) for i in range(count)])  22.2 us
    ppermute x5, starting transfers between devices, summed(): lax.ppermute(value, axis, [(i, i ^ step) for i in range(count)])  5.38 us
    pallas_call x4, Pallas kernels, backward_part(): pl.pallas_call(functools.partial(backward_kernel, block_len=block_len, of...  4.12 us
    pallas_call x2, Pallas kernels, forward_part(): pl.pallas_call(functools.partial(forward_kernel, block_len=block_len, tur...  4.05 us
    pallas_call x2, Pallas kernels, quotient_part(): pl.pallas_call(functools.partial(quotient_kernel, chunks=len(parts), bloc...  3.88 us
    pallas_call x1, Pallas kernels, prepare(): pl.pallas_call(functools.partial(prepare_kernel, count=lax.axis_size(axis...  3.13 us
  transfers between devices with their start and end apart: 20, of which 9 were waited for; matrix products, arithmetic and copies ran while one was open for 0% of the time, Pallas kernels for 5%

profile of v8, /device:TPU:11, one launch (start us, length us, event | category | flops | bytes accessed | tf_op | source)
XLA Modules:
  0.0 132.7 jit_solution(16807306894063174878)
XLA Ops:
  0.0 0.7 collective-permute-start.2
  0.7 3.1 %prepare.1 = (bf16[3,128,384]{2,1,0:T(8,128)(2,1)S(1)}, bf16[3,128,384]{2,1,0:T(8,128)(2,1)S(1)}, bf16[3,256,256]{2,1,0:T(8,128)(2,1)S(1)}, bf16[3,256,256]{2,1,...) custom-call(s32[1]{0:T(128)} %bitcast.1.position, ...), custom_call_target="tpu_custom_call" | custom-call | tf_op jit(solution)/shard_map/prepare/pallas_call | solution.py:157
  3.8 3.1 %collective-permute-start.1 = (f32[16,128,128]{2,1,0:T(8,128)S(1)}, f32[16,128,128]{2,1,0:T(8,128)S(1)}, u32[]{:S(2)}, u32[]{:S(2)}) collective-permute-start(f32[16,128,128]{2,1,0:T(8,128)S(1)} %copy-done), channel_id=1, source_target_pairs={{1,2},{2,1},{5,6},{6,5},{9,10},{10,9},{13,14},{14,13},{17,18},{18,... | collective-permute-start | bytes 3145736 | tf_op jit(solution)/shard_map/ppermute | solution.py:490
  7.0 0.7 collective-permute-start
  7.7 0.4 collective-permute-start.3
  8.1 0.9 collective-permute-done.3
  8.9 1.2 collective-permute-start.4
  10.2 19.9 %collective-permute-done.4 = f32[8,256]{1,0:T(8,128)S(1)} collective-permute-done((f32[8,256]{1,0:T(8,128)S(1)}, f32[8,256]{1,0:T(8,128)S(1)}, u32[]{:S(2)}, u32[]{:S(2)}) %collective-permute-start.4) | collective-permute-done | bytes 8224 | tf_op jit(solution)/shard_map/ppermute | solution.py:198
  30.1 0.2 collective-permute-start.5
  30.3 2.3 %collective-permute-start.6 = (f32[8,256]{1,0:T(8,128)S(1)}, f32[8,256]{1,0:T(8,128)S(1)}, u32[]{:S(2)}, u32[]{:S(2)}) collective-permute-start(f32[8,256]{1,0:T(8,128)S(1)} %add.28), channel_id=1, source_target_pairs={{0,8},{1,9},{2,10},{3,11},{4,12},{5,13},{6,14},{7,15},{8,0},{9,1},... | collective-permute-start | bytes 24584 | tf_op jit(solution)/shard_map/ppermute | solution.py:198
  32.6 0.0 collective-permute-done.5
  32.6 1.3 collective-permute-start.7
  33.9 0.0 collective-permute-done.6
  33.9 1.4 %collective-permute-done.7 = f32[8,256]{1,0:T(8,128)S(1)} collective-permute-done((f32[8,256]{1,0:T(8,128)S(1)}, f32[8,256]{1,0:T(8,128)S(1)}, u32[]{:S(2)}, u32[]{:S(2)}) %collective-permute-start.7) | collective-permute-done | bytes 8224 | tf_op jit(solution)/shard_map/ppermute | solution.py:198
  35.3 0.6 local_part.2.refs_2_
  36.0 0.0 collective-permute-done.refs_0_
  36.0 2.1 %forward_part.2.refs_0_ = f32[6192,128]{1,0:T(8,128)S(1)} custom-call(f32[16,128,128]{2,1,0:T(8,128)S(1)} %collective-permute-done.refs_0_, f32[16,128,128]{2,1,0:T(8,128)S(1)} %collective-permute-done.1.refs_1_, f32[128,48,128]{2,1,0:T(8,128)S(1)} %local_part.2.refs_2_, bf16[48,256]{1,0:T(8,128)(2,1)S(1)} %get-tuple-element.33.refs_3_, ...), custom_call_target="tpu_custom_call" | custom-call | tf_op jit(solution)/shard_map/forward_part/pallas_call | solution.py:321
  38.1 1.9 %quotient_part.2.field = f32[6272,128]{1,0:T(8,128)S(1)} custom-call(f32[6192,128]{1,0:T(8,128)S(1)} %forward_part.2.refs_0_, f32[48,128,128]{2,1,0:T(8,128)S(1)} %get-tuple-element.35.refs_1_, bf16[3,128,384]{2,1,0:T(8,128)(2,1)S(1)} %get-tuple-element.36.refs_2_, bf16[3,128,384]{2,1,0:T(8,128)(2,1)S(1)} %get-tuple-element.37.refs_3_), custom_call_target="tpu_custom_call" | custom-call | tf_op jit(solution)/shard_map/quotient_part/pallas_call | solution.py:375
  40.1 1.0 backward_part.5
  41.1 5.1 %collective-permute-start.10 = (f32[64,16,128]{2,1,0:T(8,128)S(1)}, f32[64,16,128]{2,1,0:T(8,128)S(1)}, u32[]{:S(2)}, u32[]{:S(2)}) collective-permute-start(f32[64,16,128]{2,1,0:T(8,128)S(1)} %get-tuple-element.45), channel_id=1, source_target_pairs={{3,4},{4,3},{7,8},{8,7},{11,12},{12,11},{1,2},{2,1},{5,6},{6,5},{9... | collective-permute-start | bytes 1572872 | tf_op jit(solution)/shard_map/ppermute | solution.py:490
  46.2 0.9 collective-permute-start.9
  47.1 1.0 backward_part.4
  48.2 4.7 %collective-permute-start.11 = (f32[64,16,128]{2,1,0:T(8,128)S(1)}, f32[64,16,128]{2,1,0:T(8,128)S(1)}, u32[]{:S(2)}, u32[]{:S(2)}) collective-permute-start(f32[64,16,128]{2,1,0:T(8,128)S(1)} %get-tuple-element.46), channel_id=1, source_target_pairs={{3,4},{4,3},{7,8},{8,7},{11,12},{12,11},{1,2},{2,1},{5,6},{6,5},{9... | collective-permute-start | bytes 1572872 | tf_op jit(solution)/shard_map/ppermute | solution.py:490
  52.8 0.1 collective-permute-start.8
  52.9 0.1 fusion.4
  53.0 11.3 %collective-permute-done.10 = f32[64,16,128]{2,1,0:T(8,128)S(1)} collective-permute-done((f32[64,16,128]{2,1,0:T(8,128)S(1)}, f32[64,16,128]{2,1,0:T(8,128)S(1)}, u32[]{:S(2)}, u32[]{:S(2)}) %collective-permute-start.10) | collective-permute-done | bytes 524320 | tf_op jit(solution)/shard_map/ppermute | solution.py:490
  64.3 0.4 fusion.1.refs_0_.before
  64.7 5.2 %collective-permute-done.11 = f32[64,16,128]{2,1,0:T(8,128)S(1)} collective-permute-done((f32[64,16,128]{2,1,0:T(8,128)S(1)}, f32[64,16,128]{2,1,0:T(8,128)S(1)}, u32[]{:S(2)}, u32[]{:S(2)}) %collective-permute-start.11) | collective-permute-done | bytes 524320 | tf_op jit(solution)/shard_map/ppermute | solution.py:490
  69.9 0.4 fusion.3.refs_1_.before
  70.4 0.1 collective-permute-start.15
  70.4 0.5 collective-permute-start.14
  70.9 3.6 %collective-permute-start.13 = (f32[64,16,128]{2,1,0:T(8,128)S(1)}, f32[64,16,128]{2,1,0:T(8,128)S(1)}, u32[]{:S(2)}, u32[]{:S(2)}) collective-permute-start(f32[64,16,128]{2,1,0:T(8,128)S(1)} %fusion.3.refs_1_.before), channel_id=1, source_target_pairs={{3,4},{4,3},{7,8},{8,7},{11,12},{12,11},{1,2},{2,1},{5,6},{6,5},{9... | collective-permute-start | bytes 1572872 | tf_op jit(solution)/shard_map/ppermute | solution.py:490
  74.6 2.1 %collective-permute-start.12 = (f32[64,16,128]{2,1,0:T(8,128)S(1)}, f32[64,16,128]{2,1,0:T(8,128)S(1)}, u32[]{:S(2)}, u32[]{:S(2)}) collective-permute-start(f32[64,16,128]{2,1,0:T(8,128)S(1)} %fusion.1.refs_0_.before), channel_id=1, source_target_pairs={{3,4},{4,3},{7,8},{8,7},{11,12},{12,11},{1,2},{2,1},{5,6},{6,5},{9... | collective-permute-start | bytes 1572872 | tf_op jit(solution)/shard_map/ppermute | solution.py:490
  76.7 0.6 local_part.3.refs_2_
  77.3 15.4 %collective-permute-done.13.refs_1_ = f32[64,16,128]{2,1,0:T(8,128)S(1)} collective-permute-done((f32[64,16,128]{2,1,0:T(8,128)S(1)}, f32[64,16,128]{2,1,0:T(8,128)S(1)}, u32[]{:S(2)}, u32[]{:S(2)}) %collective-permute-start.13) | collective-permute-done | bytes 524320 | tf_op jit(solution)/shard_map/ppermute | solution.py:490
  92.7 5.6 %collective-permute-done.12.refs_0_ = f32[64,16,128]{2,1,0:T(8,128)S(1)} collective-permute-done((f32[64,16,128]{2,1,0:T(8,128)S(1)}, f32[64,16,128]{2,1,0:T(8,128)S(1)}, u32[]{:S(2)}, u32[]{:S(2)}) %collective-permute-start.12) | collective-permute-done | bytes 524320 | tf_op jit(solution)/shard_map/ppermute | solution.py:490
  98.3 1.9 %forward_part.3.refs_0_ = f32[6192,128]{1,0:T(8,128)S(1)} custom-call(f32[64,16,128]{2,1,0:T(8,128)S(1)} %collective-permute-done.12.refs_0_, f32[64,16,128]{2,1,0:T(8,128)S(1)} %collective-permute-done.13.refs_1_, f32[128,48,128]{2,1,0:T(8,128)S(1)} %local_part.3.refs_2_, bf16[48,256]{1,0:T(8,128)(2,1)S(1)} %get-tuple-element.33.refs_3_, ...), custom_call_target="tpu_custom_call" | custom-call | tf_op jit(solution)/shard_map/forward_part/pallas_call | solution.py:321
  100.2 1.9 %quotient_part.3.field = f32[6272,128]{1,0:T(8,128)S(1)} custom-call(f32[6192,128]{1,0:T(8,128)S(1)} %forward_part.3.refs_0_, f32[48,128,128]{2,1,0:T(8,128)S(1)} %get-tuple-element.35.refs_1_, bf16[3,128,384]{2,1,0:T(8,128)(2,1)S(1)} %get-tuple-element.36.refs_2_, bf16[3,128,384]{2,1,0:T(8,128)(2,1)S(1)} %get-tuple-element.37.refs_3_), custom_call_target="tpu_custom_call" | custom-call | tf_op jit(solution)/shard_map/quotient_part/pallas_call | solution.py:375
  102.1 1.0 backward_part.7
  103.2 1.0 backward_part.6
  104.2 0.1 collective-permute-start.18
  104.3 3.6 %collective-permute-start.19 = (f32[64,16,128]{2,1,0:T(8,128)S(1)}, f32[64,16,128]{2,1,0:T(8,128)S(1)}, u32[]{:S(2)}, u32[]{:S(2)}) collective-permute-start(f32[64,16,128]{2,1,0:T(8,128)S(1)} %get-tuple-element.54), channel_id=1, source_target_pairs={{3,4},{4,3},{7,8},{8,7},{11,12},{12,11},{1,2},{2,1},{5,6},{6,5},{9... | collective-permute-start | bytes 1572872 | tf_op jit(solution)/shard_map/ppermute | solution.py:490
  107.9 2.5 %collective-permute-start.16 = (f32[64,16,128]{2,1,0:T(8,128)S(1)}, f32[64,16,128]{2,1,0:T(8,128)S(1)}, u32[]{:S(2)}, u32[]{:S(2)}) collective-permute-start(f32[64,16,128]{2,1,0:T(8,128)S(1)} %get-tuple-element.50), channel_id=1, source_target_pairs={{0,1},{1,0},{2,3},{3,2},{4,5},{5,4},{6,7},{7,6},{8,9},{9,8},{10,11... | collective-permute-start | bytes 1572872 | tf_op jit(solution)/shard_map/ppermute | solution.py:490
  110.4 1.9 %collective-permute-start.17 = (f32[64,16,128]{2,1,0:T(8,128)S(1)}, f32[64,16,128]{2,1,0:T(8,128)S(1)}, u32[]{:S(2)}, u32[]{:S(2)}) collective-permute-start(f32[64,16,128]{2,1,0:T(8,128)S(1)} %get-tuple-element.51), channel_id=1, source_target_pairs={{3,4},{4,3},{7,8},{8,7},{11,12},{12,11},{1,2},{2,1},{5,6},{6,5},{9... | collective-permute-start | bytes 1572872 | tf_op jit(solution)/shard_map/ppermute | solution.py:490
  112.3 13.7 %collective-permute-done.19.far = f32[64,16,128]{2,1,0:T(8,128)S(1)} collective-permute-done((f32[64,16,128]{2,1,0:T(8,128)S(1)}, f32[64,16,128]{2,1,0:T(8,128)S(1)}, u32[]{:S(2)}, u32[]{:S(2)}) %collective-permute-start.19) | collective-permute-done | bytes 524320 | tf_op jit(solution)/shard_map/ppermute | solution.py:490
  126.0 0.9 finish_part.2.refs_0_
  127.0 4.7 %collective-permute-done.17.far = f32[64,16,128]{2,1,0:T(8,128)S(1)} collective-permute-done((f32[64,16,128]{2,1,0:T(8,128)S(1)}, f32[64,16,128]{2,1,0:T(8,128)S(1)}, u32[]{:S(2)}, u32[]{:S(2)}) %collective-permute-start.17) | collective-permute-done | bytes 524320 | tf_op jit(solution)/shard_map/ppermute | solution.py:490
  131.6 0.9 finish_part.3
  (13 shorter events, 0.0 us)
Async XLA Ops:
  0.0 3.8 %copy-start = (f32[16,128,128]{2,1,0:T(8,128)S(1)}, f32[16,128,128]{2,1,0:T(8,128)}, u32[]{:S(2)}) copy-start(f32[16,128,128]{2,1,0:T(8,128)} %refs_0_.1) | copy-start | bytes 3145732
  0.0 35.3 %collective-permute-start.2 = (f32[16,128,128]{2,1,0:T(8,128)}, f32[16,128,128]{2,1,0:T(8,128)S(1)}, u32[]{:S(2)}, u32[]{:S(2)}) collective-permute-start(f32[16,128,128]{2,1,0:T(8,128)} %refs_0_.1), channel_id=1, source_target_pairs={{0,1},{1,0},{2,3},{3,2},{4,5},{5,4},{6,7},{7,6},{8,9},{9,8},{10,11... | collective-permute-start | bytes 3145736 | tf_op jit(solution)/shard_map/ppermute | solution.py:490
  3.8 32.1 %collective-permute-start.1 = (f32[16,128,128]{2,1,0:T(8,128)S(1)}, f32[16,128,128]{2,1,0:T(8,128)S(1)}, u32[]{:S(2)}, u32[]{:S(2)}) collective-permute-start(f32[16,128,128]{2,1,0:T(8,128)S(1)} %copy-done), channel_id=1, source_target_pairs={{1,2},{2,1},{5,6},{6,5},{9,10},{10,9},{13,14},{14,13},{17,18},{18,... | collective-permute-start | bytes 3145736 | tf_op jit(solution)/shard_map/ppermute | solution.py:490
  7.0 29.0 %collective-permute-start = (f32[16,128,128]{2,1,0:T(8,128)S(1)}, f32[16,128,128]{2,1,0:T(8,128)S(1)}, u32[]{:S(2)}, u32[]{:S(2)}) collective-permute-start(f32[16,128,128]{2,1,0:T(8,128)S(1)} %copy-done), channel_id=1, source_target_pairs={{3,4},{4,3},{7,8},{8,7},{11,12},{12,11},{19,20},{20,19},{23,24},{2... | collective-permute-start | bytes 3145736 | tf_op jit(solution)/shard_map/ppermute | solution.py:490
  7.7 1.2 collective-permute-start.3
  8.9 21.2 %collective-permute-start.4 = (f32[8,256]{1,0:T(8,128)S(1)}, f32[8,256]{1,0:T(8,128)S(1)}, u32[]{:S(2)}, u32[]{:S(2)}) collective-permute-start(f32[8,256]{1,0:T(8,128)S(1)} %add.27), channel_id=1, source_target_pairs={{0,2},{1,3},{2,0},{3,1},{4,6},{5,7},{6,4},{7,5},{8,10},{9,11},{10,... | collective-permute-start | bytes 24584 | tf_op jit(solution)/shard_map/ppermute | solution.py:198
  30.1 2.5 %collective-permute-start.5 = (f32[8,256]{1,0:T(8,128)S(1)}, f32[8,256]{1,0:T(8,128)S(1)}, u32[]{:S(2)}, u32[]{:S(2)}) collective-permute-start(f32[8,256]{1,0:T(8,128)S(1)} %add.28), channel_id=1, source_target_pairs={{0,4},{1,5},{2,6},{3,7},{4,0},{5,1},{6,2},{7,3},{8,12},{9,13},{10,... | collective-permute-start | bytes 24584 | tf_op jit(solution)/shard_map/ppermute | solution.py:198
  30.3 3.6 %collective-permute-start.6 = (f32[8,256]{1,0:T(8,128)S(1)}, f32[8,256]{1,0:T(8,128)S(1)}, u32[]{:S(2)}, u32[]{:S(2)}) collective-permute-start(f32[8,256]{1,0:T(8,128)S(1)} %add.28), channel_id=1, source_target_pairs={{0,8},{1,9},{2,10},{3,11},{4,12},{5,13},{6,14},{7,15},{8,0},{9,1},... | collective-permute-start | bytes 24584 | tf_op jit(solution)/shard_map/ppermute | solution.py:198
  32.6 2.7 %collective-permute-start.7 = (f32[8,256]{1,0:T(8,128)S(1)}, f32[8,256]{1,0:T(8,128)S(1)}, u32[]{:S(2)}, u32[]{:S(2)}) collective-permute-start(f32[8,256]{1,0:T(8,128)S(1)} %add.28), channel_id=1, source_target_pairs={{0,12},{1,13},{2,14},{3,15},{4,8},{5,9},{6,10},{7,11},{8,4},{9,5},... | collective-permute-start | bytes 24584 | tf_op jit(solution)/shard_map/ppermute | solution.py:198
  41.1 23.2 %collective-permute-start.10 = (f32[64,16,128]{2,1,0:T(8,128)S(1)}, f32[64,16,128]{2,1,0:T(8,128)S(1)}, u32[]{:S(2)}, u32[]{:S(2)}) collective-permute-start(f32[64,16,128]{2,1,0:T(8,128)S(1)} %get-tuple-element.45), channel_id=1, source_target_pairs={{3,4},{4,3},{7,8},{8,7},{11,12},{12,11},{1,2},{2,1},{5,6},{6,5},{9... | collective-permute-start | bytes 1572872 | tf_op jit(solution)/shard_map/ppermute | solution.py:490
  46.2 18.1 %collective-permute-start.9 = (f32[64,16,128]{2,1,0:T(8,128)S(1)}, f32[64,16,128]{2,1,0:T(8,128)S(1)}, u32[]{:S(2)}, u32[]{:S(2)}) collective-permute-start(f32[64,16,128]{2,1,0:T(8,128)S(1)} %get-tuple-element.44), channel_id=1, source_target_pairs={{0,1},{1,0},{2,3},{3,2},{4,5},{5,4},{6,7},{7,6},{8,9},{9,8},{10,11... | collective-permute-start | bytes 1572872 | tf_op jit(solution)/shard_map/ppermute | solution.py:490
  48.2 21.8 %collective-permute-start.11 = (f32[64,16,128]{2,1,0:T(8,128)S(1)}, f32[64,16,128]{2,1,0:T(8,128)S(1)}, u32[]{:S(2)}, u32[]{:S(2)}) collective-permute-start(f32[64,16,128]{2,1,0:T(8,128)S(1)} %get-tuple-element.46), channel_id=1, source_target_pairs={{3,4},{4,3},{7,8},{8,7},{11,12},{12,11},{1,2},{2,1},{5,6},{6,5},{9... | collective-permute-start | bytes 1572872 | tf_op jit(solution)/shard_map/ppermute | solution.py:490
  52.8 17.1 %collective-permute-start.8 = (f32[64,16,128]{2,1,0:T(8,128)S(1)}, f32[64,16,128]{2,1,0:T(8,128)S(1)}, u32[]{:S(2)}, u32[]{:S(2)}) collective-permute-start(f32[64,16,128]{2,1,0:T(8,128)S(1)} %get-tuple-element.42), channel_id=1, source_target_pairs={{0,1},{1,0},{2,3},{3,2},{4,5},{5,4},{6,7},{7,6},{8,9},{9,8},{10,11... | collective-permute-start | bytes 1572872 | tf_op jit(solution)/shard_map/ppermute | solution.py:490
  70.4 6.3 %collective-permute-start.15 = (f32[64,16,128]{2,1,0:T(8,128)S(1)}, f32[64,16,128]{2,1,0:T(8,128)S(1)}, u32[]{:S(2)}, u32[]{:S(2)}) collective-permute-start(f32[64,16,128]{2,1,0:T(8,128)S(1)} %fusion.3.refs_1_.before), channel_id=1, source_target_pairs={{0,1},{1,0},{2,3},{3,2},{4,5},{5,4},{6,7},{7,6},{8,9},{9,8},{10,11... | collective-permute-start | bytes 1572872 | tf_op jit(solution)/shard_map/ppermute | solution.py:490
  70.4 6.3 %collective-permute-start.14 = (f32[64,16,128]{2,1,0:T(8,128)S(1)}, f32[64,16,128]{2,1,0:T(8,128)S(1)}, u32[]{:S(2)}, u32[]{:S(2)}) collective-permute-start(f32[64,16,128]{2,1,0:T(8,128)S(1)} %fusion.1.refs_0_.before), channel_id=1, source_target_pairs={{0,1},{1,0},{2,3},{3,2},{4,5},{5,4},{6,7},{7,6},{8,9},{9,8},{10,11... | collective-permute-start | bytes 1572872 | tf_op jit(solution)/shard_map/ppermute | solution.py:490
  70.9 21.7 %collective-permute-start.13 = (f32[64,16,128]{2,1,0:T(8,128)S(1)}, f32[64,16,128]{2,1,0:T(8,128)S(1)}, u32[]{:S(2)}, u32[]{:S(2)}) collective-permute-start(f32[64,16,128]{2,1,0:T(8,128)S(1)} %fusion.3.refs_1_.before), channel_id=1, source_target_pairs={{3,4},{4,3},{7,8},{8,7},{11,12},{12,11},{1,2},{2,1},{5,6},{6,5},{9... | collective-permute-start | bytes 1572872 | tf_op jit(solution)/shard_map/ppermute | solution.py:490
  74.6 23.7 %collective-permute-start.12 = (f32[64,16,128]{2,1,0:T(8,128)S(1)}, f32[64,16,128]{2,1,0:T(8,128)S(1)}, u32[]{:S(2)}, u32[]{:S(2)}) collective-permute-start(f32[64,16,128]{2,1,0:T(8,128)S(1)} %fusion.1.refs_0_.before), channel_id=1, source_target_pairs={{3,4},{4,3},{7,8},{8,7},{11,12},{12,11},{1,2},{2,1},{5,6},{6,5},{9... | collective-permute-start | bytes 1572872 | tf_op jit(solution)/shard_map/ppermute | solution.py:490
  104.2 8.1 %collective-permute-start.18 = (f32[64,16,128]{2,1,0:T(8,128)S(1)}, f32[64,16,128]{2,1,0:T(8,128)S(1)}, u32[]{:S(2)}, u32[]{:S(2)}) collective-permute-start(f32[64,16,128]{2,1,0:T(8,128)S(1)} %get-tuple-element.53), channel_id=1, source_target_pairs={{0,1},{1,0},{2,3},{3,2},{4,5},{5,4},{6,7},{7,6},{8,9},{9,8},{10,11... | collective-permute-start | bytes 1572872 | tf_op jit(solution)/shard_map/ppermute | solution.py:490
  104.3 21.7 %collective-permute-start.19 = (f32[64,16,128]{2,1,0:T(8,128)S(1)}, f32[64,16,128]{2,1,0:T(8,128)S(1)}, u32[]{:S(2)}, u32[]{:S(2)}) collective-permute-start(f32[64,16,128]{2,1,0:T(8,128)S(1)} %get-tuple-element.54), channel_id=1, source_target_pairs={{3,4},{4,3},{7,8},{8,7},{11,12},{12,11},{1,2},{2,1},{5,6},{6,5},{9... | collective-permute-start | bytes 1572872 | tf_op jit(solution)/shard_map/ppermute | solution.py:490
  107.9 19.0 %collective-permute-start.16 = (f32[64,16,128]{2,1,0:T(8,128)S(1)}, f32[64,16,128]{2,1,0:T(8,128)S(1)}, u32[]{:S(2)}, u32[]{:S(2)}) collective-permute-start(f32[64,16,128]{2,1,0:T(8,128)S(1)} %get-tuple-element.50), channel_id=1, source_target_pairs={{0,1},{1,0},{2,3},{3,2},{4,5},{5,4},{6,7},{7,6},{8,9},{9,8},{10,11... | collective-permute-start | bytes 1572872 | tf_op jit(solution)/shard_map/ppermute | solution.py:490
  110.4 21.2 %collective-permute-start.17 = (f32[64,16,128]{2,1,0:T(8,128)S(1)}, f32[64,16,128]{2,1,0:T(8,128)S(1)}, u32[]{:S(2)}, u32[]{:S(2)}) collective-permute-start(f32[64,16,128]{2,1,0:T(8,128)S(1)} %get-tuple-element.51), channel_id=1, source_target_pairs={{3,4},{4,3},{7,8},{8,7},{11,12},{12,11},{1,2},{2,1},{5,6},{6,5},{9... | collective-permute-start | bytes 1572872 | tf_op jit(solution)/shard_map/ppermute | solution.py:490
